TPU v7x, 32 devices: a whole 2x2x4 slice. The times are simulated.
32 devices in a mesh: groups: 2 (over y), fsdp: 8 (over z, x), tensor: 2 (over core).
Axes of the slice: x: 2, y: 2, z: 4, core: 2. Of those that a mesh axis runs over, the one named last changes fastest.
Arguments:
- hidden_states: bfloat16 [8192, 4096], P(('groups', 'fsdp', 'tensor')), parts along dimension 0, may hold values from -6 to 6
- teacher_weight: bfloat16 [4096, 512], P('fsdp', 'tensor'), may hold values from -0.09375 to 0.09375
- student_weight: float32 [8192, 512], P(('groups', 'fsdp'), 'tensor'), parts along dimension 0, may hold values from -1 to 1
- first_moment: float32 [8192, 512], P(('groups', 'fsdp'), 'tensor'), parts along dimension 0, may hold values from -0.06 to 0.06
- second_moment: float32 [8192, 512], P(('groups', 'fsdp'), 'tensor'), parts along dimension 0, may hold values from 1e-05 to 0.001
Outputs:
- new_student: float32 [8192, 512], P(('groups', 'fsdp'), 'tensor'), parts along dimension 0
- new_first: float32 [8192, 512], P(('groups', 'fsdp'), 'tensor'), parts along dimension 0
- new_second: float32 [8192, 512], P(('groups', 'fsdp'), 'tensor'), parts along dimension 0
- distill_loss: float32 [2], P('groups'), parts along dimension 0
There are 2 independent parts, one for each index of `groups`. A program takes and returns all parts, laid end to end along the dimension named above; an argument that names none is the same for every part. Nothing has to cross between parts.
All inputs are finite; a program needn't handle non-finite values.
Results may differ from a plain program's by a relative error of at most 0.0031.
Values may be sent and summed in bfloat16 or wider, within the bound.
No kernel may reach another device: no remote copies, remote signals or barrier semaphores. Data moves between devices by JAX's collectives and lax.ppermute only.
A program may use at most 64 MiB of HBM per device.

v0:
```python
import math

import jax
import jax.numpy as jnp
from jax import lax
from jax.sharding import PartitionSpec as P

two_pi = 2.0 * math.pi
first_bias = 1.0 - 0.9**20
second_bias = 1.0 - 0.95**20


def soft_quantize(weights, quant_scale):
    scaled = weights / quant_scale
    return (quant_scale * (scaled - jnp.sin(two_pi * scaled) / two_pi)).astype(jnp.bfloat16)


def per_device(hidden_states, teacher_weight, student_weight, first_moment, second_moment):
    all_inputs = lax.all_gather(hidden_states, "tensor", axis=0, tiled=True)
    tokens_here = all_inputs.shape[0]
    total_tokens = tokens_here * lax.axis_size("fsdp")
    local_max = jnp.max(jnp.abs(student_weight), axis=0, keepdims=True)
    column_max = lax.pmax(local_max, "fsdp")
    quant_scale = (column_max + 1e-06) / 7.0

    def add_rows(panel):
        return jnp.dot(all_inputs, panel, preferred_element_type=jnp.float32)

    teacher_out = add_rows(lax.all_gather(teacher_weight, "fsdp", axis=0, tiled=True))
    student_out = add_rows(
        soft_quantize(lax.all_gather(student_weight, "fsdp", axis=0, tiled=True), quant_scale)
    )
    residual = student_out - teacher_out
    squared = jnp.sum(residual * residual).reshape(1)
    distill_loss = lax.psum(squared, ("fsdp", "tensor")) / total_tokens
    grad_out = (residual * (2.0 / total_tokens)).astype(jnp.bfloat16)
    gradient = lax.psum_scatter(
        lax.dot_general(
            all_inputs, grad_out, (((0,), (0,)), ((), ())), preferred_element_type=jnp.float32
        ),
        "fsdp",
        scatter_dimension=0,
        tiled=True,
    )
    new_first = 0.9 * first_moment + 0.1 * gradient
    new_second = 0.95 * second_moment + 0.05 * gradient * gradient
    update = new_first / first_bias / (jnp.sqrt(new_second / second_bias) + 1e-08)
    new_student = student_weight - 0.001 * (update + 0.1 * student_weight)
    return (new_student, new_first, new_second, distill_loss)


def solution(mesh):
    in_specs = (
        P(("groups", "fsdp", "tensor"), None),
        P("fsdp", "tensor"),
        P(("groups", "fsdp"), "tensor"),
        P(("groups", "fsdp"), "tensor"),
        P(("groups", "fsdp"), "tensor"),
    )
    out_specs = (
        P(("groups", "fsdp"), "tensor"),
        P(("groups", "fsdp"), "tensor"),
        P(("groups", "fsdp"), "tensor"),
        P("groups"),
    )
    return jax.shard_map(
        per_device, mesh=mesh, in_specs=in_specs, out_specs=out_specs, check_vma=False
    )
```

profile of v0, /device:TPU:0, one launch (start us, length us, event | category | flops | bytes accessed | tf_op | source)
XLA Modules:
  0.0 273.2 jit_solution(17129836485926717816)
XLA Ops:
  7.2 0.0 all-gather.8.cloned.1.call-start
  7.2 0.7 all-gather.8.cloned.1.call-update
  7.9 0.0 all-gather.6.cloned.1.call-start
  7.9 0.7 all-gather.6.cloned.1.call-update
  8.6 0.0 all-gather.4.cloned.1.call-start
  8.7 0.7 all-gather.4.cloned.1.call-update
  9.4 0.0 reduce-scatter.2.cloned.1.call-start
  9.4 1.1 abs_reduce_fusion
  10.5 23.3 %pmax.7 = f32[1,256]{1,0:T(1,128)S(1)} all-reduce(f32[1,256]{1,0:T(1,128)S(1)} %bitcast.13), channel_id=1, replica_groups=mesh['groups'=2,'fsdp'=8,'tensor'=2] {'fsdp'}, use_global_device_ids=true, to_apply=%region_1.0 | all-reduce | flops 256 | bytes 2048 | tf_op jit(solution)/shard_map/pmax | solution.py:23
  33.8 28.4 %all-gather.8.cloned.1.call-done = bf16[4096,256]{1,0:T(8,128)(2,1)} async-done(((bf16[512,256]{1,0:T(8,128)(2,1)}), bf16[4096,256]{1,0:T(8,128)(2,1)}) %all-gather.8.cloned.1.call-update) | async-done | bytes 2097168 | tf_op jit(solution)/shard_map/all_gather | solution.py:29
  62.2 13.7 %all-gather.6.cloned.1.call-done = bf16[512,4096]{1,0:T(8,128)(2,1)} async-done(((bf16[256,4096]{1,0:T(8,128)(2,1)}), bf16[512,4096]{1,0:T(8,128)(2,1)}) %all-gather.6.cloned.1.call-update) | async-done | bytes 4194320 | tf_op jit(solution)/shard_map/all_gather | solution.py:19
  75.9 4.2 %fusion.9 = f32[512,256]{0,1:T(8,128)S(1)} fusion(bf16[512,4096]{1,0:T(8,128)(2,1)} %all-gather.6.cloned.1.call-done, bf16[4096,256]{1,0:T(8,128)(2,1)} %all-gather.8.cloned.1.call-done), kind=kOutput, calls=%fused_computation.17 | convolution fusion | flops 1073741824 | bytes 6815744 | tf_op jit(solution)/shard_map/dot_general | solution.py:27
  80.1 72.6 %all-gather.4.cloned.1.call-done = f32[4096,256]{1,0:T(8,128)} async-done(((f32[512,256]{1,0:T(8,128)}), f32[4096,256]{1,0:T(8,128)}) %all-gather.4.cloned.1.call-update) | async-done | bytes 4194320 | tf_op jit(solution)/shard_map/all_gather | solution.py:31
  152.7 0.0 copy-start
  152.7 18.1 %multiply_reduce_fusion = (f32[]{:T(128)}, f32[512,256]{0,1:T(8,128)S(1)}) fusion(f32[512,256]{0,1:T(8,128)S(1)} %fusion.9, bf16[512,4096]{1,0:T(8,128)(2,1)} %all-gather.6.cloned.1.call-done, f32[4096,256]{1,0:T(8,128)} %all-gather.4.cloned.1.call-done, f32[256]{0:T(256)S(1)} %bitcast.14), kind=kOutput, calls=%fused_computation.7 | convolution fusion | flops 1080426496 | bytes 9438212 | tf_op jit(solution)/shard_map/dot_general | solution.py:27
  170.8 0.0 copy-done
  170.8 3.2 %convolution_bitcast_fusion = f32[4096,256]{0,1:T(8,128)} fusion(bf16[512,4096]{1,0:T(8,128)(2,1)S(1)} %copy-done, f32[512,256]{0,1:T(8,128)S(1)} %get-tuple-element.12), kind=kOutput, calls=%fused_computation | convolution fusion | flops 1074003968 | bytes 8912896 | tf_op jit(solution)/shard_map/dot_general | solution.py:38
  174.0 0.0 copy-start.1
  174.0 0.0 copy-start.2
  174.0 0.0 copy-start.3
  174.0 0.0 reduce-scatter.2.cloned.1.call-update
  174.0 1.0 copy-done.1
  175.1 0.2 copy.13
  175.3 0.0 copy-done.2
  175.3 0.2 copy.11
  175.5 0.0 copy-done.3
  175.5 0.2 copy.9
  175.7 32.7 %psum.7 = f32[1]{0:T(128)} all-reduce(f32[1]{0:T(128)} %bitcast.4), channel_id=1, replica_groups=mesh['groups'=2,'fsdp'=8,'tensor'=2] {'fsdp','tensor'}, use_global_device_ids=true, to_apply=%region_4.0 | all-reduce | flops 1 | bytes 8 | tf_op jit(solution)/shard_map/psum | solution.py:35
  209.0 52.1 %reduce-scatter.2.cloned.1.call-done = f32[512,256]{0,1:T(8,128)} async-done(((f32[4096,256]{0,1:T(8,128)}), f32[512,256]{0,1:T(8,128)}) %reduce-scatter.2.cloned.1.call-update) | async-done | bytes 524304 | tf_op jit(solution)/shard_map/reduce_scatter | solution.py:37
  261.1 1.5 multiply_subtract_fusion
  262.5 1.0 copy.14
  263.5 1.0 copy.15
  264.5 1.0 copy.16
  (1 shorter events, 0.0 us)
Async XLA Ops:
  7.2 55.0 %all-gather.8.cloned.1.call-start = ((), (), s32[]{:S(2)}) async-start(), calls=%async_computation.3 | async-start | bytes 2359296 | tf_op jit(solution)/shard_map/all_gather | solution.py:29
  7.9 68.0 %all-gather.6.cloned.1.call-start = ((), (), s32[]{:S(2)}) async-start(), calls=%async_computation.2 | async-start | bytes 6291456 | tf_op jit(solution)/shard_map/all_gather | solution.py:19
  8.6 144.0 %all-gather.4.cloned.1.call-start = ((), (), s32[]{:S(2)}) async-start(), calls=%async_computation.1 | async-start | bytes 4718592 | tf_op jit(solution)/shard_map/all_gather | solution.py:31
  9.4 251.7 %reduce-scatter.2.cloned.1.call-start = ((), (), s32[]{:S(2)}) async-start(), calls=%async_computation.4 | async-start | bytes 4718592 | tf_op jit(solution)/shard_map/reduce_scatter | solution.py:37
  152.7 18.1 %copy-start = (bf16[512,4096]{1,0:T(8,128)(2,1)S(1)}, bf16[512,4096]{1,0:T(8,128)(2,1)}, u32[]{:S(2)}) copy-start(bf16[512,4096]{1,0:T(8,128)(2,1)} %all-gather.6.cloned.1.call-done) | copy-start | bytes 12582916
  174.0 1.0 copy-start.1
  174.0 1.2 copy-start.2
  174.0 1.5 copy-start.3
Sparse Core Ops, SparseCore 0:
  10.1 52.0 all-gather.7
  63.7 12.1 all-gather.5
  78.1 74.5 all-gather.3
  174.2 86.8 reduce-scatter.1
where the time goes:
time: 273 us
  waiting for transfers between devices  169 us (62%)
  blocking collectives  56 us (21%)
  matrix products  25.5 us (9%)
  between operations  15.6 us (6%)
  local copies, waits for them, and re-layouts  4.6 us (2%)
    all_gather x1, waiting for transfers between devices, per_device(): lax.all_gather(student_weight, 'fsdp', axis=0, tiled=True)  72.6 us
    reduce_scatter x1, waiting for transfers between devices, per_device(): lax.psum_scatter(lax.dot_general(all_inputs, grad_out, (((0,), (0,)), (()...  52.1 us
    psum x1, blocking collectives, per_device(): distill_loss = lax.psum(squared, ('fsdp', 'tensor')) / total_tokens  32.7 us
    all_gather x1, waiting for transfers between devices, per_device(): lax.all_gather(teacher_weight, 'fsdp', axis=0, tiled=True)  28.4 us
    pmax x1, blocking collectives, per_device(): column_max = lax.pmax(local_max, 'fsdp')  23.3 us
    dot_general x2, matrix products, add_rows(): return jnp.dot(all_inputs, panel, preferred_element_type=jnp.float32)  22.3 us
    all_gather x1, waiting for transfers between devices, per_device(): all_inputs = lax.all_gather(hidden_states, 'tensor', axis=0, tiled=True)  13.7 us
  transfers between devices with their start and end apart: 4, of which 4 were waited for; matrix products, arithmetic and copies ran while one was open for 2% of the time, Pallas kernels for 0%

commit v1 on v0

v1 whole, which is shorter than its diff:
```python
import math

import jax
import jax.numpy as jnp
from jax import lax
from jax.experimental import pallas as pl
from jax.experimental.pallas import tpu as pltpu
from jax.sharding import PartitionSpec as P

two_pi = 2.0 * math.pi
first_bias = 1.0 - 0.9**20
second_bias = 1.0 - 0.95**20
f32 = jnp.float32
bf16 = jnp.bfloat16


def soft_quantize(weights, quant_scale):
    scaled = weights / quant_scale
    return (quant_scale * (scaled - jnp.sin(two_pi * scaled) / two_pi)).astype(bf16)


def adamw(gradient, student_weight, first_moment, second_moment):
    new_first = 0.9 * first_moment + 0.1 * gradient
    new_second = 0.95 * second_moment + 0.05 * gradient * gradient
    update = new_first / first_bias / (jnp.sqrt(new_second / second_bias) + 1e-08)
    new_student = student_weight - 0.001 * (update + 0.1 * student_weight)
    return new_student, new_first, new_second


def generic(hidden_states, teacher_weight, student_weight, first_moment, second_moment):
    all_inputs = lax.all_gather(hidden_states, "tensor", axis=0, tiled=True)
    total_tokens = all_inputs.shape[0] * lax.axis_size("fsdp")
    local_max = jnp.max(jnp.abs(student_weight), axis=0, keepdims=True)
    quant_scale = (lax.pmax(local_max, "fsdp") + 1e-06) / 7.0
    quantized = soft_quantize(student_weight, quant_scale)
    difference = (quantized.astype(f32) - teacher_weight.astype(f32)).astype(bf16)
    difference = lax.all_gather(difference, "fsdp", axis=0, tiled=True)
    residual = jnp.dot(all_inputs, difference, preferred_element_type=f32)
    squared = jnp.sum(residual * residual).reshape(1)
    distill_loss = lax.psum(squared, ("fsdp", "tensor")) / total_tokens
    grad_out = (residual * (2.0 / total_tokens)).astype(bf16)
    partial = lax.dot_general(
        all_inputs, grad_out, (((0,), (0,)), ((), ())), preferred_element_type=f32
    )
    gradient = lax.psum_scatter(partial, "fsdp", scatter_dimension=0, tiled=True)
    return (*adamw(gradient, student_weight, first_moment, second_moment), distill_loss)


def vmem(n):
    return [pl.BlockSpec(memory_space=pltpu.VMEM)] * n


params = pltpu.CompilerParams(vmem_limit_bytes=16 * 2**20)


def held(*arrays):
    return [pltpu.with_memory_space_constraint(a, pltpu.VMEM) for a in arrays]


def sort_features(hidden_states, blocks):
    tokens, features = hidden_states.shape
    width = features // (2 * blocks)

    def kernel(h_ref, keep_ref, send_ref):
        index = lax.axis_index("fsdp")
        rank, half = index // 2, index % 2
        for k in range(blocks):
            block = jnp.bitwise_xor(rank, k) * 2
            for ref, which in ((send_ref, 1 - half), (keep_ref, half)):
                start = pl.multiple_of((block + which) * width, width)
                ref[:, k * width : (k + 1) * width] = h_ref[:, pl.ds(start, width)]

    shape = pltpu.VMEM((tokens, features // 2), bf16)
    return pl.pallas_call(
        kernel, out_shape=(shape, shape), in_specs=vmem(1), out_specs=tuple(vmem(2)),
        name="sort_features", compiler_params=params,
    )(*held(hidden_states))


def partial_residual(pieces, differences):
    tokens = pieces[0].shape[0]
    width, columns = differences[0].shape
    n, m = len(pieces), len(differences)

    def kernel(*refs):
        h_refs, d_refs, (wide_ref, sent_ref) = refs[:n], refs[n : n + m], refs[n + m :]
        for i, h_ref in enumerate(h_refs):
            total = jnp.zeros((tokens, columns), f32)
            for k, d_ref in enumerate(d_refs):
                total += jnp.dot(
                    h_ref[:, k * width : (k + 1) * width], d_ref[...],
                    preferred_element_type=f32,
                )
            rows = slice(i * tokens, (i + 1) * tokens)
            wide_ref[rows, :] = total
            sent_ref[rows, :] = total.astype(bf16)

    shape = (n * tokens, columns)
    return pl.pallas_call(
        kernel,
        out_shape=(pltpu.VMEM(shape, f32), pltpu.VMEM(shape, bf16)),
        in_specs=vmem(n + m), out_specs=tuple(vmem(2)), name="partial_residual", compiler_params=params,
    )(*held(*pieces, *differences))


def partial_gradient(pieces, mine, theirs, blocks, total_tokens):
    tokens, features = pieces[0].shape
    width, columns, n = features // blocks, mine.shape[1], len(pieces)

    def kernel(*refs):
        h_refs, mine_ref, theirs_ref = refs[:n], refs[n], refs[n + 1]
        loss_ref, own_ref, *send_refs = refs[n + 2 :]
        half = n * tokens // 2
        top = mine_ref[:half, :] + theirs_ref[half:, :].astype(f32)
        bottom = mine_ref[half:, :] + theirs_ref[:half, :].astype(f32)
        loss_ref[...] = jnp.sum(top * top, axis=0, keepdims=True)
        grad_out = jnp.concatenate([top, bottom], axis=0) * (2.0 / total_tokens)
        grad_out = grad_out.astype(bf16)
        for k in range(blocks - 1, -1, -1):
            total = jnp.zeros((columns, width), f32)
            for i, h_ref in enumerate(h_refs):
                total += lax.dot_general(
                    grad_out[i * tokens : (i + 1) * tokens, :],
                    h_ref[:, k * width : (k + 1) * width],
                    (((0,), (0,)), ((), ())), preferred_element_type=f32,
                )
            if k:
                send_refs[k - 1][...] = total.astype(bf16)
            else:
                own_ref[...] = total

    shape = (columns, width)
    return pl.pallas_call(
        kernel,
        out_shape=(
            pltpu.VMEM((1, columns), f32), pltpu.VMEM(shape, f32),
            *[pltpu.VMEM(shape, bf16)] * (blocks - 1),
        ),
        in_specs=vmem(n + 2), out_specs=tuple(vmem(blocks + 1)), name="partial_gradient", compiler_params=params,
    )(*held(*pieces, mine, theirs))


def apply_update(own, received, student_weight, first_moment, second_moment):
    n = len(received)

    def kernel(own_ref, *refs):
        gradient = own_ref[...]
        for ref in refs[:n]:
            gradient += ref[...].astype(f32)
        w_ref, m_ref, v_ref, *out_refs = refs[n:]
        news = adamw(gradient.T, w_ref[...], m_ref[...], v_ref[...])
        for ref, new in zip(out_refs, news, strict=True):
            ref[...] = new

    shape = jax.ShapeDtypeStruct(student_weight.shape, f32)
    return pl.pallas_call(
        kernel, out_shape=(shape,) * 3, in_specs=vmem(n + 4), out_specs=tuple(vmem(3)),
        name="apply_update", compiler_params=params,
    )(*held(own, *received, student_weight, first_moment, second_moment))


def paired(hidden_states, teacher_weight, student_weight, first_moment, second_moment):
    fsdp = lax.axis_size("fsdp")
    blocks = fsdp // 2
    total_tokens = hidden_states.shape[0] * fsdp * lax.axis_size("tensor")

    def flip(array, bit):
        return lax.ppermute(array, "fsdp", [(i, i ^ bit) for i in range(fsdp)])

    def swap_cores(array):
        return lax.ppermute(array, "tensor", [(0, 1), (1, 0)])

    column_max = jnp.max(jnp.abs(student_weight), axis=0, keepdims=True)
    keep, send = sort_features(hidden_states, blocks)
    column_max = jnp.maximum(column_max, flip(column_max, 1))
    send, column_max = lax.optimization_barrier((send, column_max))
    peer = flip(send, 1)
    bit = 2
    while bit < fsdp:
        column_max = jnp.maximum(column_max, flip(column_max, bit))
        bit *= 2
    quant_scale = (column_max + 1e-06) / 7.0
    quantized = soft_quantize(student_weight, quant_scale)
    difference = (quantized.astype(f32) - teacher_weight.astype(f32)).astype(bf16)
    differences = [difference] + [flip(difference, 2 * k) for k in range(1, blocks)]
    peer, differences = lax.optimization_barrier((peer, differences))
    pieces = [keep, swap_cores(keep), peer, swap_cores(peer)]
    mine, sent = partial_residual(pieces, differences)
    theirs = flip(sent, 1)
    loss, own, *partials = partial_gradient(pieces, mine, theirs, blocks, total_tokens)
    received = [flip(p, 2 * k) for k, p in enumerate(partials, 1)]
    loss = jnp.sum(loss).reshape(1)
    bit = 1
    while bit < fsdp:
        loss = loss + flip(loss, bit)
        bit *= 2
    loss = (loss + swap_cores(loss)) / total_tokens
    news = apply_update(own, received, student_weight, first_moment, second_moment)
    return (*news, loss)


def solution(mesh):
    fsdp, tensor = mesh.shape["fsdp"], mesh.shape["tensor"]

    def per_device(hidden_states, *weights):
        rows = weights[0].shape[0]
        few = fsdp in (4, 8, 16) and tensor == 2 and rows % 128 == 0
        return (paired if few else generic)(hidden_states, *weights)

    rows = P(("groups", "fsdp"), "tensor")
    in_specs = (P(("groups", "fsdp", "tensor"), None), P("fsdp", "tensor"), rows, rows, rows)
    out_specs = (rows, rows, rows, P("groups"))
    return jax.shard_map(
        per_device, mesh=mesh, in_specs=in_specs, out_specs=out_specs, check_vma=False
    )
```

time: 273 us -> 91.3 us (0.33)
  waiting for transfers between devices: 169 us -> 43.2 us
  blocking collectives: 56 us -> 0 us
  starting transfers between devices: 0.15 us -> 33 us
  matrix products: 25.5 us -> 0 us
  between operations: 15.6 us -> 4.79 us
  Pallas kernels: 0 us -> 4.85 us
  local copies, waits for them, and re-layouts: 4.6 us -> 1.61 us
    all_gather x3 -> x0, waiting for transfers between devices: 115 us -> none  [the longest x1 72.6 us: per_device(): lax.all_gather(student_weight, 'fsdp', axis=0, tiled=True)]
    reduce_scatter x1 -> x0, waiting for transfers between devices: 52.1 us -> none  [per_device(): lax.psum_scatter(lax.dot_general(all_inputs, grad_out, (((0,), (0,)), (()...]
    ppermute x0 -> x17, waiting for transfers between devices: none -> 43.2 us  [the longest x14 40.3 us: flip(): return lax.ppermute(array, 'fsdp', [(i, i ^ bit) for i in range(fsdp)])]
    ppermute x0 -> x17, starting transfers between devices: none -> 33 us  [the longest x14 32 us: flip(): return lax.ppermute(array, 'fsdp', [(i, i ^ bit) for i in range(fsdp)])]
    psum x1 -> x0, blocking collectives: 32.7 us -> none  [per_device(): distill_loss = lax.psum(squared, ('fsdp', 'tensor')) / total_tokens]
    dot_general x3 -> x0, matrix products: 25.5 us -> none  [the longest x2 22.3 us: add_rows(): return jnp.dot(all_inputs, panel, preferred_element_type=jnp.float32)]
    pmax x1 -> x0, blocking collectives: 23.3 us -> none  [per_device(): column_max = lax.pmax(local_max, 'fsdp')]
    pallas_call x0 -> x4, Pallas kernels: none -> 4.85 us  [the longest x1 1.8 us: partial_gradient(): pl.pallas_call(kernel, out_shape=(pltpu.VMEM((1, columns), f32), pltpu.VM...]
  transfers between devices with their start and end apart: 4 -> 17, of which waited for: 4 -> 9; matrix products, arithmetic and copies ran while one was open for 2% -> 3% of each run, Pallas kernels for 0% -> 0%
where the time goes in v1:
time: 91.3 us; the launch traced here: 91.1 us
  waiting for transfers between devices  43.2 us (47%)
  starting transfers between devices  33 us (36%)
  Pallas kernels  4.85 us (5%)
  between operations  4.79 us (5%)
  other arithmetic  3.64 us (4%)
  local copies, waits for them, and re-layouts  1.61 us (2%)
    ppermute x14, waiting for transfers between devices, flip(): return lax.ppermute(array, 'fsdp', [(i, i ^ bit) for i in range(fsdp)])  40.3 us
    ppermute x14, starting transfers between devices, flip(): return lax.ppermute(array, 'fsdp', [(i, i ^ bit) for i in range(fsdp)])  32 us
    ppermute x3, waiting for transfers between devices, swap_cores(): return lax.ppermute(array, 'tensor', [(0, 1), (1, 0)])  2.94 us
    convert_element_type x1, other arithmetic, paired(): (quantized.astype(f32) - teacher_weight.astype(f32)).astype(bf16)  1.88 us
  transfers between devices with their start and end apart: 17, of which 9 were waited for; matrix products, arithmetic and copies ran while one was open for 3% of the time, Pallas kernels for 0%

profile of v1, /device:TPU:0, one launch (start us, length us, event | category | flops | bytes accessed | tf_op | source)
XLA Modules:
  0.0 91.1 jit_solution(3642569341326578308)
XLA Ops:
  0.6 0.0 copy-start
  0.6 1.1 %abs_reduce_fusion = f32[256]{0:T(256)S(1)} fusion(f32[512,256]{1,0:T(8,128)} %refs_3_.1), kind=kLoop, calls=%fused_computation.2 | loop fusion | flops 261888 | bytes 525312 | tf_op jit(solution)/shard_map/reduce_max | solution.py:173
  1.8 3.0 %collective-permute-start.1 = (f32[1,256]{1,0:T(1,128)S(1)}, f32[1,256]{1,0:T(1,128)S(1)}, u32[]{:S(2)}, u32[]{:S(2)}) collective-permute-start(f32[1,256]{1,0:T(1,128)S(1)} %bitcast.3), channel_id=1, source_target_pairs={{0,2},{2,0},{4,6},{6,4},{8,10},{10,8},{12,14},{14,12},{1,3},{3,1},... | collective-permute-start | bytes 3080 | tf_op jit(solution)/shard_map/ppermute | solution.py:168
  4.8 0.0 copy-start.1
  4.8 1.6 %copy-done.1 = bf16[256,4096]{1,0:T(8,128)(2,1)S(1)} copy-done((bf16[256,4096]{1,0:T(8,128)(2,1)S(1)}, bf16[256,4096]{1,0:T(8,128)(2,1)}, u32[]{:S(2)}) %copy-start.1) | copy-done | bytes 2097176
  6.4 0.0 copy-start.4
  6.4 0.2 sort_features.1
  6.6 0.0 collective-permute-done.1
  6.6 1.8 %collective-permute-start.2 = (bf16[256,2048]{1,0:T(8,128)(2,1)S(1)}, bf16[256,2048]{1,0:T(8,128)(2,1)S(1)}, u32[]{:S(2)}, u32[]{:S(2)}) collective-permute-start(bf16[256,2048]{1,0:T(8,128)(2,1)S(1)} %get-tuple-element.25), channel_id=1, source_target_pairs={{0,2},{2,0},{4,6},{6,4},{8,10},{10,8},{12,14},{14,12},{1,3},{3,1},... | collective-permute-start | bytes 3145736 | tf_op jit(solution)/shard_map/ppermute | solution.py:168
  8.4 1.6 %collective-permute-start.3 = (f32[1,256]{1,0:T(1,128)S(1)}, f32[1,256]{1,0:T(1,128)S(1)}, u32[]{:S(2)}, u32[]{:S(2)}) collective-permute-start(f32[1,256]{1,0:T(1,128)S(1)} %max.9), channel_id=1, source_target_pairs={{0,4},{2,6},{4,0},{6,2},{8,12},{10,14},{12,8},{14,10},{1,5},{3,7},... | collective-permute-start | bytes 3080 | tf_op jit(solution)/shard_map/ppermute | solution.py:168
  9.9 2.0 %collective-permute-done.3 = f32[1,256]{1,0:T(1,128)S(1)} collective-permute-done((f32[1,256]{1,0:T(1,128)S(1)}, f32[1,256]{1,0:T(1,128)S(1)}, u32[]{:S(2)}, u32[]{:S(2)}) %collective-permute-start.3) | collective-permute-done | bytes 1056 | tf_op jit(solution)/shard_map/ppermute | solution.py:168
  11.9 2.6 %collective-permute-start.4 = (f32[1,256]{1,0:T(1,128)S(1)}, f32[1,256]{1,0:T(1,128)S(1)}, u32[]{:S(2)}, u32[]{:S(2)}) collective-permute-start(f32[1,256]{1,0:T(1,128)S(1)} %max.10), channel_id=1, source_target_pairs={{0,8},{2,10},{4,12},{6,14},{8,0},{10,2},{12,4},{14,6},{1,9},{3,11}... | collective-permute-start | bytes 3080 | tf_op jit(solution)/shard_map/ppermute | solution.py:168
  14.5 1.9 %collective-permute-done.4 = f32[1,256]{1,0:T(1,128)S(1)} collective-permute-done((f32[1,256]{1,0:T(1,128)S(1)}, f32[1,256]{1,0:T(1,128)S(1)}, u32[]{:S(2)}, u32[]{:S(2)}) %collective-permute-start.4) | collective-permute-done | bytes 1056 | tf_op jit(solution)/shard_map/ppermute | solution.py:168
  16.4 0.0 copy-done
  16.4 0.0 copy-done.4
  16.4 1.9 %subtract_convert_fusion.refs_4_ = bf16[512,256]{1,0:T(8,128)(2,1)S(1)} fusion(bf16[512,256]{1,0:T(8,128)(2,1)S(1)} %copy-done.4, f32[512,256]{1,0:T(8,128)S(1)} %copy-done, f32[256]{0:T(256)S(1)} %bitcast.5), kind=kLoop, calls=%fused_computation | loop fusion | flops 1310720 | bytes 1049600 | tf_op jit(solution)/shard_map/convert_element_type | solution.py:184
  18.3 3.7 %collective-permute-start.7 = (bf16[512,256]{1,0:T(8,128)(2,1)S(1)}, bf16[512,256]{1,0:T(8,128)(2,1)S(1)}, u32[]{:S(2)}, u32[]{:S(2)}) collective-permute-start(bf16[512,256]{1,0:T(8,128)(2,1)S(1)} %subtract_convert_fusion.refs_4_), channel_id=1, source_target_pairs={{0,12},{2,14},{4,8},{6,10},{8,4},{10,6},{12,0},{14,2},{1,13},{3,15... | collective-permute-start | bytes 786440 | tf_op jit(solution)/shard_map/ppermute | solution.py:168
  22.0 0.0 collective-permute-start.6
  22.0 0.8 collective-permute-start.5
  22.8 0.0 collective-permute-start
  22.8 6.6 %collective-permute-done.7.refs_7_ = bf16[512,256]{1,0:T(8,128)(2,1)S(1)} collective-permute-done((bf16[512,256]{1,0:T(8,128)(2,1)S(1)}, bf16[512,256]{1,0:T(8,128)(2,1)S(1)}, u32[]{:S(2)}, u32[]{:S(2)}) %collective-permute-start.7) | collective-permute-done | bytes 262176 | tf_op jit(solution)/shard_map/ppermute | solution.py:168
  29.4 11.1 %collective-permute-done.6.refs_6_ = bf16[512,256]{1,0:T(8,128)(2,1)S(1)} collective-permute-done((bf16[512,256]{1,0:T(8,128)(2,1)S(1)}, bf16[512,256]{1,0:T(8,128)(2,1)S(1)}, u32[]{:S(2)}, u32[]{:S(2)}) %collective-permute-start.6) | collective-permute-done | bytes 262176 | tf_op jit(solution)/shard_map/ppermute | solution.py:168
  40.5 0.0 collective-permute-done.5.refs_5_
  40.6 0.0 collective-permute-done.2.refs_2_
  40.6 0.0 collective-permute-start.8
  40.6 0.0 collective-permute-done.refs_1_
  40.6 2.6 %collective-permute-done.8.refs_3_ = bf16[256,2048]{1,0:T(8,128)(2,1)S(1)} collective-permute-done((bf16[256,2048]{1,0:T(8,128)(2,1)S(1)}, bf16[256,2048]{1,0:T(8,128)(2,1)S(1)}, u32[]{:S(2)}, u32[]{:S(2)}) %collective-permute-start.8) | collective-permute-done | bytes 1048608 | tf_op jit(solution)/shard_map/ppermute | solution.py:171
  43.2 1.2 %partial_residual.1 = (f32[1024,256]{1,0:T(8,128)S(1)}, bf16[1024,256]{1,0:T(8,128)(2,1)S(1)}) custom-call(bf16[256,2048]{1,0:T(8,128)(2,1)S(1)} %get-tuple-element.23.refs_0_, bf16[256,2048]{1,0:T(8,128)(2,1)S(1)} %collective-permute-done.refs_1_, bf16[256,2048]{1,0:T(8,128)(2,1)S(1)} %collective-permute-done.2.refs_2_, ...), custom_call_target="tpu_custom_call" | custom-call | tf_op jit(solution)/shard_map/partial_residual/pallas_call | solution.py:99
  44.5 1.2 %collective-permute-start.9 = (bf16[1024,256]{1,0:T(8,128)(2,1)S(1)}, bf16[1024,256]{1,0:T(8,128)(2,1)S(1)}, u32[]{:S(2)}, u32[]{:S(2)}) collective-permute-start(bf16[1024,256]{1,0:T(8,128)(2,1)S(1)} %get-tuple-element.33), channel_id=1, source_target_pairs={{0,2},{2,0},{4,6},{6,4},{8,10},{10,8},{12,14},{14,12},{1,3},{3,1},... | collective-permute-start | bytes 1572872 | tf_op jit(solution)/shard_map/ppermute | solution.py:168
  45.7 12.8 %collective-permute-done.9.refs_5_ = bf16[1024,256]{1,0:T(8,128)(2,1)S(1)} collective-permute-done((bf16[1024,256]{1,0:T(8,128)(2,1)S(1)}, bf16[1024,256]{1,0:T(8,128)(2,1)S(1)}, u32[]{:S(2)}, u32[]{:S(2)}) %collective-permute-start.9) | collective-permute-done | bytes 524320 | tf_op jit(solution)/shard_map/ppermute | solution.py:168
  58.5 0.0 copy-start.2
  58.5 0.0 copy-start.3
  58.5 1.8 %partial_gradient.1 = (f32[1,256]{1,0:T(1,128)S(1)}, f32[256,512]{1,0:T(8,128)S(1)}, bf16[256,512]{1,0:T(8,128)(2,1)}, bf16[256,512]{1,0:T(8,128)(2,1)S(1)}, bf16[256,512]{1,0:T(8,128)(2,1)S(1)}) custom-call(bf16[256,2048]{1,0:T(8,128)(2,1)S(1)} %get-tuple-element.23.refs_0_, bf16[256,2048]{1,0:T(8,128)(2,1)S(1)} %collective-permute-done.refs_1_, ...), custom_call_target="tpu_custom_call" | custom-call | tf_op jit(solution)/shard_map/partial_gradient/pallas_call | solution.py:133
  60.3 0.0 collective-permute-start.10
  60.3 3.0 %collective-permute-start.11 = (bf16[256,512]{1,0:T(8,128)(2,1)S(1)}, bf16[256,512]{1,0:T(8,128)(2,1)S(1)}, u32[]{:S(2)}, u32[]{:S(2)}) collective-permute-start(bf16[256,512]{1,0:T(8,128)(2,1)S(1)} %get-tuple-element.36), channel_id=1, source_target_pairs={{0,8},{2,10},{4,12},{6,14},{8,0},{10,2},{12,4},{14,6},{1,9},{3,11}... | collective-permute-start | bytes 786440 | tf_op jit(solution)/shard_map/ppermute | solution.py:168
  63.4 1.3 %collective-permute-start.12 = (bf16[256,512]{1,0:T(8,128)(2,1)S(1)}, bf16[256,512]{1,0:T(8,128)(2,1)S(1)}, u32[]{:S(2)}, u32[]{:S(2)}) collective-permute-start(bf16[256,512]{1,0:T(8,128)(2,1)S(1)} %get-tuple-element.37), channel_id=1, source_target_pairs={{0,12},{2,14},{4,8},{6,10},{8,4},{10,6},{12,0},{14,2},{1,13},{3,15... | collective-permute-start | bytes 786440 | tf_op jit(solution)/shard_map/ppermute | solution.py:168
  64.7 0.6 reduce_sum.9
  65.3 1.2 %collective-permute-start.13 = (f32[1]{0:T(128)}, f32[1]{0:T(128)}, u32[]{:S(2)}, u32[]{:S(2)}) collective-permute-start(f32[1]{0:T(128)} %bitcast.2), channel_id=1, source_target_pairs={{0,2},{2,0},{4,6},{6,4},{8,10},{10,8},{12,14},{14,12},{1,3},{3,1},... | collective-permute-start | bytes 20 | tf_op jit(solution)/shard_map/ppermute | solution.py:168
  66.5 2.6 %collective-permute-done.13 = f32[1]{0:T(128)} collective-permute-done((f32[1]{0:T(128)}, f32[1]{0:T(128)}, u32[]{:S(2)}, u32[]{:S(2)}) %collective-permute-start.13) | collective-permute-done | bytes 36 | tf_op jit(solution)/shard_map/ppermute | solution.py:168
  70.3 6.9 %collective-permute-start.14 = (f32[1]{0:T(128)}, f32[1]{0:T(128)}, u32[]{:S(2)}, u32[]{:S(2)}) collective-permute-start(f32[1]{0:T(128)} %add.20), channel_id=1, source_target_pairs={{0,4},{2,6},{4,0},{6,2},{8,12},{10,14},{12,8},{14,10},{1,5},{3,7},... | collective-permute-start | bytes 20 | tf_op jit(solution)/shard_map/ppermute | solution.py:168
  77.2 0.0 collective-permute-done.14
  77.7 4.9 %collective-permute-start.15 = (f32[1]{0:T(128)}, f32[1]{0:T(128)}, u32[]{:S(2)}, u32[]{:S(2)}) collective-permute-start(f32[1]{0:T(128)} %add.21), channel_id=1, source_target_pairs={{0,8},{2,10},{4,12},{6,14},{8,0},{10,2},{12,4},{14,6},{1,9},{3,11}... | collective-permute-start | bytes 20 | tf_op jit(solution)/shard_map/ppermute | solution.py:168
  82.6 3.2 %collective-permute-done.15 = f32[1]{0:T(128)} collective-permute-done((f32[1]{0:T(128)}, f32[1]{0:T(128)}, u32[]{:S(2)}, u32[]{:S(2)}) %collective-permute-start.15) | collective-permute-done | bytes 36 | tf_op jit(solution)/shard_map/ppermute | solution.py:168
  86.4 1.0 %collective-permute-start.16 = (f32[1]{0:T(128)}, f32[1]{0:T(128)}, u32[]{:S(2)}, u32[]{:S(2)}) collective-permute-start(f32[1]{0:T(128)} %add.22), channel_id=1, source_target_pairs={{0,1},{1,0},{2,3},{3,2},{4,5},{5,4},{6,7},{7,6},{8,9},{9,8},{10,11... | collective-permute-start | bytes 20 | tf_op jit(solution)/shard_map/ppermute | solution.py:171
  87.4 0.3 collective-permute-done.16
  88.3 0.0 collective-permute-done.10.refs_0_
  88.3 0.0 collective-permute-done.11.refs_1_
  88.3 0.0 collective-permute-done.12.refs_2_
  88.3 0.0 copy-done.2
  88.3 0.0 copy-done.3
  88.4 1.6 %apply_update.1 = (f32[512,256]{1,0:T(8,128)}, f32[512,256]{1,0:T(8,128)}, f32[512,256]{1,0:T(8,128)}) custom-call(f32[256,512]{1,0:T(8,128)S(1)} %get-tuple-element.34.own_ref, bf16[256,512]{1,0:T(8,128)(2,1)S(1)} %collective-permute-done.10.refs_0_, bf16[256,512]{1,0:T(8,128)(2,1)S(1)} %collective-permute-done.11.refs_1_, ...), custom_call_target="tpu_custom_call" | custom-call | tf_op jit(solution)/shard_map/apply_update/pallas_call | solution.py:156
  (3 shorter events, 0.0 us)
Async XLA Ops:
  0.6 15.8 %copy-start = (f32[512,256]{1,0:T(8,128)S(1)}, f32[512,256]{1,0:T(8,128)}, u32[]{:S(2)}) copy-start(f32[512,256]{1,0:T(8,128)} %refs_3_.1) | copy-start | bytes 1572868
  1.8 4.8 %collective-permute-start.1 = (f32[1,256]{1,0:T(1,128)S(1)}, f32[1,256]{1,0:T(1,128)S(1)}, u32[]{:S(2)}, u32[]{:S(2)}) collective-permute-start(f32[1,256]{1,0:T(1,128)S(1)} %bitcast.3), channel_id=1, source_target_pairs={{0,2},{2,0},{4,6},{6,4},{8,10},{10,8},{12,14},{14,12},{1,3},{3,1},... | collective-permute-start | bytes 3080 | tf_op jit(solution)/shard_map/ppermute | solution.py:168
  4.8 1.6 %copy-start.1 = (bf16[256,4096]{1,0:T(8,128)(2,1)S(1)}, bf16[256,4096]{1,0:T(8,128)(2,1)}, u32[]{:S(2)}) copy-start(bf16[256,4096]{1,0:T(8,128)(2,1)} %h_ref.1) | copy-start | bytes 6291460
  6.4 10.0 %copy-start.4 = (bf16[512,256]{1,0:T(8,128)(2,1)S(1)}, bf16[512,256]{1,0:T(8,128)(2,1)}, u32[]{:S(2)}) copy-start(bf16[512,256]{1,0:T(8,128)(2,1)} %param.6) | copy-start | bytes 786436
  6.6 34.0 %collective-permute-start.2 = (bf16[256,2048]{1,0:T(8,128)(2,1)S(1)}, bf16[256,2048]{1,0:T(8,128)(2,1)S(1)}, u32[]{:S(2)}, u32[]{:S(2)}) collective-permute-start(bf16[256,2048]{1,0:T(8,128)(2,1)S(1)} %get-tuple-element.25), channel_id=1, source_target_pairs={{0,2},{2,0},{4,6},{6,4},{8,10},{10,8},{12,14},{14,12},{1,3},{3,1},... | collective-permute-start | bytes 3145736 | tf_op jit(solution)/shard_map/ppermute | solution.py:168
  8.4 3.6 %collective-permute-start.3 = (f32[1,256]{1,0:T(1,128)S(1)}, f32[1,256]{1,0:T(1,128)S(1)}, u32[]{:S(2)}, u32[]{:S(2)}) collective-permute-start(f32[1,256]{1,0:T(1,128)S(1)} %max.9), channel_id=1, source_target_pairs={{0,4},{2,6},{4,0},{6,2},{8,12},{10,14},{12,8},{14,10},{1,5},{3,7},... | collective-permute-start | bytes 3080 | tf_op jit(solution)/shard_map/ppermute | solution.py:168
  11.9 4.5 %collective-permute-start.4 = (f32[1,256]{1,0:T(1,128)S(1)}, f32[1,256]{1,0:T(1,128)S(1)}, u32[]{:S(2)}, u32[]{:S(2)}) collective-permute-start(f32[1,256]{1,0:T(1,128)S(1)} %max.10), channel_id=1, source_target_pairs={{0,8},{2,10},{4,12},{6,14},{8,0},{10,2},{12,4},{14,6},{1,9},{3,11}... | collective-permute-start | bytes 3080 | tf_op jit(solution)/shard_map/ppermute | solution.py:168
  18.3 11.1 %collective-permute-start.7 = (bf16[512,256]{1,0:T(8,128)(2,1)S(1)}, bf16[512,256]{1,0:T(8,128)(2,1)S(1)}, u32[]{:S(2)}, u32[]{:S(2)}) collective-permute-start(bf16[512,256]{1,0:T(8,128)(2,1)S(1)} %subtract_convert_fusion.refs_4_), channel_id=1, source_target_pairs={{0,12},{2,14},{4,8},{6,10},{8,4},{10,6},{12,0},{14,2},{1,13},{3,15... | collective-permute-start | bytes 786440 | tf_op jit(solution)/shard_map/ppermute | solution.py:168
  22.0 18.6 %collective-permute-start.6 = (bf16[512,256]{1,0:T(8,128)(2,1)S(1)}, bf16[512,256]{1,0:T(8,128)(2,1)S(1)}, u32[]{:S(2)}, u32[]{:S(2)}) collective-permute-start(bf16[512,256]{1,0:T(8,128)(2,1)S(1)} %subtract_convert_fusion.refs_4_), channel_id=1, source_target_pairs={{0,8},{2,10},{4,12},{6,14},{8,0},{10,2},{12,4},{14,6},{1,9},{3,11}... | collective-permute-start | bytes 786440 | tf_op jit(solution)/shard_map/ppermute | solution.py:168
  22.0 18.6 %collective-permute-start.5 = (bf16[512,256]{1,0:T(8,128)(2,1)S(1)}, bf16[512,256]{1,0:T(8,128)(2,1)S(1)}, u32[]{:S(2)}, u32[]{:S(2)}) collective-permute-start(bf16[512,256]{1,0:T(8,128)(2,1)S(1)} %subtract_convert_fusion.refs_4_), channel_id=1, source_target_pairs={{0,4},{2,6},{4,0},{6,2},{8,12},{10,14},{12,8},{14,10},{1,5},{3,7},... | collective-permute-start | bytes 786440 | tf_op jit(solution)/shard_map/ppermute | solution.py:168
  22.8 17.8 %collective-permute-start = (bf16[256,2048]{1,0:T(8,128)(2,1)S(1)}, bf16[256,2048]{1,0:T(8,128)(2,1)S(1)}, u32[]{:S(2)}, u32[]{:S(2)}) collective-permute-start(bf16[256,2048]{1,0:T(8,128)(2,1)S(1)} %get-tuple-element.23.refs_0_), channel_id=1, source_target_pairs={{0,1},{1,0},{2,3},{3,2},{4,5},{5,4},{6,7},{7,6},{8,9},{9,8},{10,11... | collective-permute-start | bytes 3145736 | tf_op jit(solution)/shard_map/ppermute | solution.py:171
  40.6 2.7 %collective-permute-start.8 = (bf16[256,2048]{1,0:T(8,128)(2,1)S(1)}, bf16[256,2048]{1,0:T(8,128)(2,1)S(1)}, u32[]{:S(2)}, u32[]{:S(2)}) collective-permute-start(bf16[256,2048]{1,0:T(8,128)(2,1)S(1)} %collective-permute-done.2.refs_2_), channel_id=1, source_target_pairs={{0,1},{1,0},{2,3},{3,2},{4,5},{5,4},{6,7},{7,6},{8,9},{9,8},{10,11... | collective-permute-start | bytes 3145736 | tf_op jit(solution)/shard_map/ppermute | solution.py:171
  44.5 14.0 %collective-permute-start.9 = (bf16[1024,256]{1,0:T(8,128)(2,1)S(1)}, bf16[1024,256]{1,0:T(8,128)(2,1)S(1)}, u32[]{:S(2)}, u32[]{:S(2)}) collective-permute-start(bf16[1024,256]{1,0:T(8,128)(2,1)S(1)} %get-tuple-element.33), channel_id=1, source_target_pairs={{0,2},{2,0},{4,6},{6,4},{8,10},{10,8},{12,14},{14,12},{1,3},{3,1},... | collective-permute-start | bytes 1572872 | tf_op jit(solution)/shard_map/ppermute | solution.py:168
  58.5 29.8 %copy-start.2 = (f32[512,256]{1,0:T(8,128)S(1)}, f32[512,256]{1,0:T(8,128)}, u32[]{:S(2)}) copy-start(f32[512,256]{1,0:T(8,128)} %refs_4_.1) | copy-start | bytes 1572868
  58.5 29.8 %copy-start.3 = (f32[512,256]{1,0:T(8,128)S(1)}, f32[512,256]{1,0:T(8,128)}, u32[]{:S(2)}) copy-start(f32[512,256]{1,0:T(8,128)} %refs_5_.1) | copy-start | bytes 1572868
  60.3 28.0 %collective-permute-start.10 = (bf16[256,512]{1,0:T(8,128)(2,1)}, bf16[256,512]{1,0:T(8,128)(2,1)S(1)}, u32[]{:S(2)}, u32[]{:S(2)}) collective-permute-start(bf16[256,512]{1,0:T(8,128)(2,1)} %get-tuple-element.35), channel_id=1, source_target_pairs={{0,4},{2,6},{4,0},{6,2},{8,12},{10,14},{12,8},{14,10},{1,5},{3,7},... | collective-permute-start | bytes 786440 | tf_op jit(solution)/shard_map/ppermute | solution.py:168
  60.3 28.0 %collective-permute-start.11 = (bf16[256,512]{1,0:T(8,128)(2,1)S(1)}, bf16[256,512]{1,0:T(8,128)(2,1)S(1)}, u32[]{:S(2)}, u32[]{:S(2)}) collective-permute-start(bf16[256,512]{1,0:T(8,128)(2,1)S(1)} %get-tuple-element.36), channel_id=1, source_target_pairs={{0,8},{2,10},{4,12},{6,14},{8,0},{10,2},{12,4},{14,6},{1,9},{3,11}... | collective-permute-start | bytes 786440 | tf_op jit(solution)/shard_map/ppermute | solution.py:168
  63.4 25.0 %collective-permute-start.12 = (bf16[256,512]{1,0:T(8,128)(2,1)S(1)}, bf16[256,512]{1,0:T(8,128)(2,1)S(1)}, u32[]{:S(2)}, u32[]{:S(2)}) collective-permute-start(bf16[256,512]{1,0:T(8,128)(2,1)S(1)} %get-tuple-element.37), channel_id=1, source_target_pairs={{0,12},{2,14},{4,8},{6,10},{8,4},{10,6},{12,0},{14,2},{1,13},{3,15... | collective-permute-start | bytes 786440 | tf_op jit(solution)/shard_map/ppermute | solution.py:168
  65.3 3.8 %collective-permute-start.13 = (f32[1]{0:T(128)}, f32[1]{0:T(128)}, u32[]{:S(2)}, u32[]{:S(2)}) collective-permute-start(f32[1]{0:T(128)} %bitcast.2), channel_id=1, source_target_pairs={{0,2},{2,0},{4,6},{6,4},{8,10},{10,8},{12,14},{14,12},{1,3},{3,1},... | collective-permute-start | bytes 20 | tf_op jit(solution)/shard_map/ppermute | solution.py:168
  70.3 6.9 %collective-permute-start.14 = (f32[1]{0:T(128)}, f32[1]{0:T(128)}, u32[]{:S(2)}, u32[]{:S(2)}) collective-permute-start(f32[1]{0:T(128)} %add.20), channel_id=1, source_target_pairs={{0,4},{2,6},{4,0},{6,2},{8,12},{10,14},{12,8},{14,10},{1,5},{3,7},... | collective-permute-start | bytes 20 | tf_op jit(solution)/shard_map/ppermute | solution.py:168
  77.7 8.1 %collective-permute-start.15 = (f32[1]{0:T(128)}, f32[1]{0:T(128)}, u32[]{:S(2)}, u32[]{:S(2)}) collective-permute-start(f32[1]{0:T(128)} %add.21), channel_id=1, source_target_pairs={{0,8},{2,10},{4,12},{6,14},{8,0},{10,2},{12,4},{14,6},{1,9},{3,11}... | collective-permute-start | bytes 20 | tf_op jit(solution)/shard_map/ppermute | solution.py:168
  86.4 1.3 %collective-permute-start.16 = (f32[1]{0:T(128)}, f32[1]{0:T(128)}, u32[]{:S(2)}, u32[]{:S(2)}) collective-permute-start(f32[1]{0:T(128)} %add.22), channel_id=1, source_target_pairs={{0,1},{1,0},{2,3},{3,2},{4,5},{5,4},{6,7},{7,6},{8,9},{9,8},{10,11... | collective-permute-start | bytes 20 | tf_op jit(solution)/shard_map/ppermute | solution.py:171

commit v2 on v1

v2 whole, which is shorter than its diff:
```python
import math

import jax
import jax.numpy as jnp
from jax import lax
from jax.experimental import pallas as pl
from jax.experimental.pallas import tpu as pltpu
from jax.sharding import PartitionSpec as P

two_pi = 2.0 * math.pi
first_bias = 1.0 - 0.9**20
second_bias = 1.0 - 0.95**20
f32 = jnp.float32
bf16 = jnp.bfloat16


def soft_quantize(weights, quant_scale):
    scaled = weights / quant_scale
    return (quant_scale * (scaled - jnp.sin(two_pi * scaled) / two_pi)).astype(bf16)


def adamw(gradient, student_weight, first_moment, second_moment):
    new_first = 0.9 * first_moment + 0.1 * gradient
    new_second = 0.95 * second_moment + 0.05 * gradient * gradient
    update = new_first / first_bias / (jnp.sqrt(new_second / second_bias) + 1e-08)
    new_student = student_weight - 0.001 * (update + 0.1 * student_weight)
    return new_student, new_first, new_second


def generic(hidden_states, teacher_weight, student_weight, first_moment, second_moment):
    all_inputs = lax.all_gather(hidden_states, "tensor", axis=0, tiled=True)
    total_tokens = all_inputs.shape[0] * lax.axis_size("fsdp")
    local_max = jnp.max(jnp.abs(student_weight), axis=0, keepdims=True)
    quant_scale = (lax.pmax(local_max, "fsdp") + 1e-06) / 7.0
    quantized = soft_quantize(student_weight, quant_scale)
    difference = (quantized.astype(f32) - teacher_weight.astype(f32)).astype(bf16)
    difference = lax.all_gather(difference, "fsdp", axis=0, tiled=True)
    residual = jnp.dot(all_inputs, difference, preferred_element_type=f32)
    squared = jnp.sum(residual * residual).reshape(1)
    distill_loss = lax.psum(squared, ("fsdp", "tensor")) / total_tokens
    grad_out = (residual * (2.0 / total_tokens)).astype(bf16)
    partial = lax.dot_general(
        all_inputs, grad_out, (((0,), (0,)), ((), ())), preferred_element_type=f32
    )
    gradient = lax.psum_scatter(partial, "fsdp", scatter_dimension=0, tiled=True)
    return (*adamw(gradient, student_weight, first_moment, second_moment), distill_loss)


params = pltpu.CompilerParams(vmem_limit_bytes=16 * 2**20)
sine_terms = (
    6.579736267281999,
    -12.987878760960296,
    12.208113946775761,
    -6.6937816308195295,
    2.4016117188086827,
    -0.6033682700805688,
    0.1006404612407522,
)


def vmem(n):
    return [pl.BlockSpec(memory_space=pltpu.VMEM)] * n


def held(*arrays):
    return [pltpu.with_memory_space_constraint(a, pltpu.VMEM) for a in arrays]


def rounded(array):
    return lax.reduce_precision(array, 8, 7)


def high_low(array):
    high = rounded(array)
    return high.astype(bf16), (array - high).astype(bf16)


def weight_difference(student_weight, teacher_weight, column_max):
    quant_scale = (column_max + 1e-06) / 7.0
    scaled = student_weight / quant_scale
    whole = jnp.round(scaled)
    rest = scaled - whole
    square = rest * rest
    series = jnp.full_like(square, sine_terms[-1])
    for term in sine_terms[-2::-1]:
        series = series * square + term
    quantized = rounded(quant_scale * (whole + rest * square * series))
    return quantized - teacher_weight.astype(f32)


def sort_features(hidden_states, blocks):
    tokens, features = hidden_states.shape
    width = features // (2 * blocks)

    def kernel(h_ref, keep_ref, send_ref):
        index = lax.axis_index("fsdp")
        rank, half = index // 2, index % 2
        for k in range(blocks):
            block = jnp.bitwise_xor(rank, k) * 2
            where = slice(k * width, (k + 1) * width)
            start = pl.multiple_of((block + half) * width, width)
            keep_ref[:, where] = h_ref[:, pl.ds(start, width)]
            start = pl.multiple_of((block + 1 - half) * width, width)
            send_ref[:, where] = h_ref[:, pl.ds(start, width)]

    shape = pltpu.VMEM((tokens, features // 2), bf16)
    return pl.pallas_call(
        kernel, out_shape=(shape, shape), in_specs=vmem(1), out_specs=tuple(vmem(2)),
        name="sort_features", compiler_params=params,
    )(*held(hidden_states))


def row_starts(pieces):
    starts = [0]
    for piece in pieces:
        starts.append(starts[-1] + piece.shape[0])
    return starts


def partial_residual(pieces, highs, lows):
    starts = row_starts(pieces)
    width, columns = highs[0].shape
    n, m = len(pieces), len(highs)

    def kernel(*refs):
        h_refs, d_refs, (wide_ref, sent_ref) = refs[:n], refs[n : n + 2 * m], refs[n + 2 * m :]
        weights = [
            jnp.concatenate([high[...], low[...]], axis=1)
            for high, low in zip(d_refs[:m], d_refs[m:], strict=True)
        ]
        for i, h_ref in enumerate(h_refs):
            total = jnp.zeros((h_ref.shape[0], 2 * columns), f32)
            for k, weight in enumerate(weights):
                total += jnp.dot(
                    h_ref[:, k * width : (k + 1) * width], weight, preferred_element_type=f32
                )
            total = (total[:, :columns] + total[:, columns:]) * 2.0**-15
            rows = slice(starts[i], starts[i + 1])
            wide_ref[rows, :] = total
            sent_ref[rows, :] = total.astype(bf16)

    shape = (starts[-1], columns)
    return pl.pallas_call(
        kernel,
        out_shape=(pltpu.VMEM(shape, f32), pltpu.VMEM(shape, bf16)),
        in_specs=vmem(n + 2 * m), out_specs=tuple(vmem(2)), name="partial_residual",
        compiler_params=params,
    )(*held(*pieces, *highs, *lows))


def split_float(array):
    rows = []
    for _ in range(3):
        rows.append(array.astype(bf16))
        array = array - rows[-1].astype(f32)
    return rows


note_rows = 16


def write_note(ref, start, row):
    width = ref.shape[1]
    parts = [p.astype(f32) for p in split_float(row)]
    parts.append(jnp.zeros((note_rows - 3, row.shape[1]), f32))
    note = jnp.concatenate(parts, axis=0).astype(bf16)
    pad = jnp.zeros((note_rows, width - row.shape[1]), bf16)
    ref[start : start + note_rows, :] = jnp.concatenate([note, pad], axis=1)


def read_note(ref, start, columns):
    note = ref[start : start + note_rows, :columns].astype(f32)
    return note[0:1, :] + note[1:2, :] + note[2:3, :]


def partial_gradient(pieces, mine, theirs, loss, total_tokens, ride):
    starts, features = row_starts(pieces), pieces[0].shape[1]
    width, columns, n = features // 4, mine.shape[1], len(pieces)

    def kernel(*refs):
        h_refs, mine_ref, theirs_ref, before_ref = refs[:n], *refs[n : n + 3]
        loss_ref, own_ref, far_ref, send_ref, *near_refs = refs[n + 3 :]
        half = starts[-1] // 2
        top, bottom = mine_ref[:half, :], mine_ref[half:, :]
        their_bottom = theirs_ref[:half, :].astype(f32)
        their_top = theirs_ref[half:, :].astype(f32)
        top, bottom = top + their_top, bottom + their_bottom
        grad_out = jnp.concatenate([top, bottom], axis=0) * (2.0 / total_tokens)
        grad_out = grad_out.astype(bf16)
        for k in (3, 1, 2, 0):
            total = jnp.zeros((columns, width), f32)
            for i, h_ref in enumerate(h_refs):
                total += lax.dot_general(
                    grad_out[starts[i] : starts[i + 1], :],
                    h_ref[:, k * width : (k + 1) * width],
                    (((0,), (0,)), ((), ())), preferred_element_type=f32,
                )
            if k == 3:
                send_ref[:columns, :] = total.astype(bf16)
            elif k == 1:
                near = total.astype(bf16)
                if ride:
                    send_ref[columns + note_rows :, :] = near
                else:
                    near_refs[0][...] = near
            elif k == 2:
                far_ref[...] = total
            else:
                own_ref[...] = total
        squares = [
            jnp.sum(jnp.square(a.astype(bf16).astype(f32) + b), axis=0, keepdims=True)
            for a, b in (
                (mine_ref[:half, :], their_top),
                (mine_ref[half:, :], their_bottom),
            )
        ]
        total = before_ref[...] + (squares[0] + squares[1])
        loss_ref[...] = total
        write_note(send_ref, columns, total)

    shape = (columns, width)
    return pl.pallas_call(
        kernel,
        out_shape=(
            pltpu.VMEM((1, columns), f32), pltpu.VMEM(shape, f32), pltpu.VMEM(shape, f32),
            pltpu.VMEM((columns * (1 + ride) + note_rows, width), bf16),
            *[pltpu.VMEM(shape, bf16)] * (1 - ride),
        ),
        in_specs=vmem(n + 3), out_specs=tuple(vmem(5 - ride)), name="partial_gradient",
        compiler_params=params,
    )(*held(*pieces, mine, theirs, loss))


def join_far(far, got, loss):
    columns, width = far.shape

    def kernel(far_ref, got_ref, loss_ref, send_ref, sum_ref):
        total = far_ref[...] + got_ref[:columns, :].astype(f32)
        send_ref[:columns, :] = total.astype(bf16)
        both = loss_ref[...] + read_note(got_ref, columns, columns)
        sum_ref[...] = both
        write_note(send_ref, columns, both)

    return pl.pallas_call(
        kernel,
        out_shape=(pltpu.VMEM((columns + note_rows, width), bf16), pltpu.VMEM((1, columns), f32)),
        in_specs=vmem(3), out_specs=tuple(vmem(2)), name="join_far", compiler_params=params,
    )(*held(far, got, loss))


def total_loss(loss, got):
    columns = loss.shape[1]

    def kernel(loss_ref, got_ref, out_ref):
        out_ref[...] = loss_ref[...] + read_note(got_ref, columns, columns)

    return pl.pallas_call(
        kernel, out_shape=pltpu.VMEM((1, columns), f32), in_specs=vmem(2), out_specs=vmem(1)[0],
        name="total_loss", compiler_params=params,
    )(*held(loss, got))


def apply_update(half, own, near, far, states, news=()):
    width, columns = own.shape[1], own.shape[0]
    n = len(news)

    def kernel(own_ref, near_ref, far_ref, w_ref, m_ref, v_ref, *refs):
        gradient = own_ref[...] + near_ref[-columns:, :].astype(f32)
        gradient += far_ref[:columns, :].astype(f32)
        where = (slice(None), slice(half * columns, (half + 1) * columns))
        results = adamw(gradient.T, w_ref[where], m_ref[where], v_ref[where])
        for ref, result in zip(refs[n:], results, strict=True):
            ref[...] = result

    shape = jax.ShapeDtypeStruct(states[0].shape, f32)
    block = pl.BlockSpec((width, columns), lambda i: (0, half))
    return pl.pallas_call(
        kernel, grid=(1,), out_shape=(shape,) * 3,
        in_specs=vmem(6) + [pl.BlockSpec(memory_space=pl.ANY)] * n, out_specs=(block,) * 3,
        input_output_aliases={6 + i: i for i in range(n)},
        name="apply_update", compiler_params=params,
    )(*held(own, near, far, *states), *news)


def paired(hidden_states, teacher_weight, student_weight, first_moment, second_moment):
    fsdp = lax.axis_size("fsdp")
    blocks = fsdp // 2
    total_tokens = hidden_states.shape[0] * fsdp * lax.axis_size("tensor")
    columns = student_weight.shape[1] // 2
    halves = [slice(0, columns), slice(columns, 2 * columns)]

    def flip(array, bit):
        return lax.ppermute(array, "fsdp", [(i, i ^ bit) for i in range(fsdp)])

    def swap_cores(array):
        return lax.ppermute(array, "tensor", [(0, 1), (1, 0)])

    def together(*values):
        return lax.optimization_barrier(values)

    column_max = jnp.max(jnp.abs(student_weight), axis=0, keepdims=True)
    keep, send = sort_features(hidden_states, blocks)
    column_max = jnp.maximum(column_max, flip(column_max, 1))
    keep, column_max = together(keep, column_max)
    peer = flip(send, 1)
    near_keep = swap_cores(keep)
    column_max = jnp.maximum(column_max, flip(column_max, 2))
    column_max = jnp.maximum(column_max, flip(column_max, 4))
    difference = weight_difference(student_weight, teacher_weight, column_max) * 2.0**15
    coded = difference.astype(jnp.float16)

    far = flip(coded, 4)
    near = flip(coded, 2)
    far, near, peer, near_keep = together(far, near, peer, near_keep)
    across = [flip(far[:, half], 2) for half in halves]
    pieces = [keep, near_keep, peer, swap_cores(peer)]

    def residual(c):
        parts = [p[:, halves[c]].astype(f32) for p in (difference, near, far)]
        pairs = [high_low(p) for p in (*parts, across[c].astype(f32))]
        return partial_residual(pieces, [p[0] for p in pairs], [p[1] for p in pairs])

    mine, sent = residual(0)
    theirs = flip(sent, 1)
    mine_next, sent_next = residual(1)
    theirs_next = flip(sent_next, 1)

    loss = jnp.zeros((1, columns), f32)
    loss, own, rest, to_across, to_near = partial_gradient(
        pieces, mine, theirs, loss, total_tokens, False
    )
    from_across = flip(to_across, 2)
    theirs_next, from_across = together(theirs_next, from_across)
    loss_next, own_next, rest_next, to_across = partial_gradient(
        pieces, mine_next, theirs_next, loss, total_tokens, True
    )
    from_across_next = flip(to_across, 2)
    from_near = flip(to_near, 2)
    to_far, _ = join_far(rest, from_across, loss)
    to_far, from_near = together(to_far, from_near)
    from_far = flip(to_far, 4)
    states = (student_weight, first_moment, second_moment)
    from_across_next, from_far = together(from_across_next, from_far)
    news = apply_update(0, own, from_near, from_far, states)
    to_far, loss = join_far(rest_next, from_across_next, loss_next)
    from_far_next = flip(to_far, 4)
    from_far_next, *news = together(from_far_next, *news)
    loss = total_loss(loss, from_far_next)
    loss = jnp.sum(loss + swap_cores(loss)).reshape(1) / total_tokens
    news = apply_update(1, own_next, from_across_next, from_far_next, states, news)
    return (*news, loss)


def solution(mesh):
    fsdp, tensor = mesh.shape["fsdp"], mesh.shape["tensor"]

    def per_device(hidden_states, *weights):
        rows = weights[0].shape[0]
        few = fsdp == 8 and tensor == 2 and rows % 128 == 0 and weights[0].shape[1] % 256 == 0
        return (paired if few else generic)(hidden_states, *weights)

    rows = P(("groups", "fsdp"), "tensor")
    in_specs = (P(("groups", "fsdp", "tensor"), None), P("fsdp", "tensor"), rows, rows, rows)
    out_specs = (rows, rows, rows, P("groups"))
    return jax.shard_map(
        per_device, mesh=mesh, in_specs=in_specs, out_specs=out_specs, check_vma=False
    )
```

time: 91.3 us -> 78.4 us (0.86)
  the two profiles are of different devices: /device:TPU:0 before, /device:TPU:29 now
where the time goes in v2:
time: 78.4 us; the launch traced here: 78.2 us
  waiting for transfers between devices  47.7 us (61%)
  starting transfers between devices  16.6 us (21%)
  Pallas kernels  7.13 us (9%)
  other arithmetic  2.56 us (3%)
  between operations  2.51 us (3%)
  local copies, waits for them, and re-layouts  1.66 us (2%)
    ppermute x15, waiting for transfers between devices, flip(): return lax.ppermute(array, 'fsdp', [(i, i ^ bit) for i in range(fsdp)])  47.7 us
    ppermute x3, starting transfers between devices, swap_cores(): return lax.ppermute(array, 'tensor', [(0, 1), (1, 0)])  9.65 us
    ppermute x15, starting transfers between devices, flip(): return lax.ppermute(array, 'fsdp', [(i, i ^ bit) for i in range(fsdp)])  6.94 us
    pallas_call x2, Pallas kernels, partial_residual(): pl.pallas_call(kernel, out_shape=(pltpu.VMEM(shape, f32), pltpu.VMEM(shap...  2.5 us
    pallas_call x2, Pallas kernels, apply_update(): pl.pallas_call(kernel, grid=(1,), out_shape=(shape,) * 3, in_specs=vmem(6...  2.3 us
    unnamed x10, local copies, waits for them, and re-layouts  1.61 us
    pallas_call x2, Pallas kernels, partial_gradient(): pl.pallas_call(kernel, out_shape=(pltpu.VMEM((1, columns), f32), pltpu.VM...  1.58 us
  transfers between devices with their start and end apart: 18, of which 11 were waited for; matrix products, arithmetic and copies ran while one was open for 1% of the time, Pallas kernels for 9%

profile of v2, /device:TPU:29, one launch (start us, length us, event | category | flops | bytes accessed | tf_op | source)
XLA Modules:
  0.0 78.2 jit_solution(18197520076806033307)
XLA Ops:
  0.6 0.0 copy-start
  0.6 1.1 %abs_reduce_fusion = f32[256]{0:T(256)S(1)} fusion(f32[512,256]{1,0:T(8,128)} %w_ref.3), kind=kLoop, calls=%fused_computation.19 | loop fusion | flops 261888 | bytes 525312 | tf_op jit(solution)/shard_map/reduce_max | solution.py:301
  1.8 1.3 %collective-permute-start = (f32[1,256]{1,0:T(1,128)S(1)}, f32[1,256]{1,0:T(1,128)S(1)}, u32[]{:S(2)}, u32[]{:S(2)}) collective-permute-start(f32[1,256]{1,0:T(1,128)S(1)} %bitcast.3), channel_id=1, source_target_pairs={{0,2},{2,0},{4,6},{6,4},{8,10},{10,8},{12,14},{14,12},{1,3},{3,1},... | collective-permute-start | bytes 3080 | tf_op jit(solution)/shard_map/ppermute | solution.py:293
  3.1 0.0 copy-start.1
  3.1 1.6 %copy-done.1 = bf16[256,4096]{1,0:T(8,128)(2,1)S(1)} copy-done((bf16[256,4096]{1,0:T(8,128)(2,1)S(1)}, bf16[256,4096]{1,0:T(8,128)(2,1)}, u32[]{:S(2)}) %copy-start.1) | copy-done | bytes 2097176
  4.6 0.0 copy-start.4
  4.6 0.2 sort_features.1
  4.8 0.3 collective-permute-start.5
  5.1 0.0 collective-permute-done
  5.1 1.2 %collective-permute-start.6 = (bf16[256,2048]{1,0:T(8,128)(2,1)S(1)}, bf16[256,2048]{1,0:T(8,128)(2,1)S(1)}, u32[]{:S(2)}, u32[]{:S(2)}) collective-permute-start(bf16[256,2048]{1,0:T(8,128)(2,1)S(1)} %get-tuple-element.45.refs_0_), channel_id=1, source_target_pairs={{0,1},{1,0},{2,3},{3,2},{4,5},{5,4},{6,7},{7,6},{8,9},{9,8},{10,11... | collective-permute-start | bytes 3145736 | tf_op jit(solution)/shard_map/ppermute | solution.py:296
  6.4 0.2 collective-permute-start.1
  6.5 2.5 %collective-permute-done.1 = f32[1,256]{1,0:T(1,128)S(1)} collective-permute-done((f32[1,256]{1,0:T(1,128)S(1)}, f32[1,256]{1,0:T(1,128)S(1)}, u32[]{:S(2)}, u32[]{:S(2)}) %collective-permute-start.1) | collective-permute-done | bytes 1056 | tf_op jit(solution)/shard_map/ppermute | solution.py:293
  9.1 0.1 collective-permute-start.2
  9.2 3.3 %collective-permute-done.2 = f32[1,256]{1,0:T(1,128)S(1)} collective-permute-done((f32[1,256]{1,0:T(1,128)S(1)}, f32[1,256]{1,0:T(1,128)S(1)}, u32[]{:S(2)}, u32[]{:S(2)}) %collective-permute-start.2) | collective-permute-done | bytes 1056 | tf_op jit(solution)/shard_map/ppermute | solution.py:293
  12.4 0.0 copy-done
  12.4 0.0 copy-done.4
  12.4 0.4 fusion.19
  12.9 0.1 collective-permute-start.3
  13.0 0.2 collective-permute-start.4
  13.2 14.4 %collective-permute-done.3 = f16[512,256]{1,0:T(8,128)(2,1)S(1)} collective-permute-done((f16[512,256]{1,0:T(8,128)(2,1)S(1)}, f16[512,256]{1,0:T(8,128)(2,1)S(1)}, u32[]{:S(2)}, u32[]{:S(2)}) %collective-permute-start.3) | collective-permute-done | bytes 262176 | tf_op jit(solution)/shard_map/ppermute | solution.py:293
  27.6 0.0 collective-permute-done.4
  27.6 1.0 %collective-permute-done.5.refs_2_ = bf16[256,2048]{1,0:T(8,128)(2,1)S(1)} collective-permute-done((bf16[256,2048]{1,0:T(8,128)(2,1)S(1)}, bf16[256,2048]{1,0:T(8,128)(2,1)S(1)}, u32[]{:S(2)}, u32[]{:S(2)}) %collective-permute-start.5) | collective-permute-done | bytes 1048608 | tf_op jit(solution)/shard_map/ppermute | solution.py:293
  28.6 0.0 collective-permute-done.6.refs_1_
  28.6 1.9 %collective-permute-start.7 = (bf16[256,2048]{1,0:T(8,128)(2,1)S(1)}, bf16[256,2048]{1,0:T(8,128)(2,1)S(1)}, u32[]{:S(2)}, u32[]{:S(2)}) collective-permute-start(bf16[256,2048]{1,0:T(8,128)(2,1)S(1)} %collective-permute-done.5.refs_2_), channel_id=1, source_target_pairs={{0,1},{1,0},{2,3},{3,2},{4,5},{5,4},{6,7},{7,6},{8,9},{9,8},{10,11... | collective-permute-start | bytes 3145736 | tf_op jit(solution)/shard_map/ppermute | solution.py:296
  30.5 0.1 fusion.15
  30.6 0.1 fusion.21
  30.6 0.2 collective-permute-start.10
  30.8 1.3 %collective-permute-start.8 = (f16[512,128]{1,0:T(8,128)(2,1)S(1)}, f16[512,128]{1,0:T(8,128)(2,1)S(1)}, u32[]{:S(2)}, u32[]{:S(2)}) collective-permute-start(f16[512,128]{1,0:T(8,128)(2,1)S(1)} %get-tuple-element.99), channel_id=1, source_target_pairs={{0,4},{2,6},{4,0},{6,2},{8,12},{10,14},{12,8},{14,10},{1,5},{3,7},... | collective-permute-start | bytes 393224 | tf_op jit(solution)/shard_map/ppermute | solution.py:293
  32.1 0.2 fusion.16
  32.3 3.5 %collective-permute-done.10 = f16[512,128]{1,0:T(8,128)(2,1)S(1)} collective-permute-done((f16[512,128]{1,0:T(8,128)(2,1)S(1)}, f16[512,128]{1,0:T(8,128)(2,1)S(1)}, u32[]{:S(2)}, u32[]{:S(2)}) %collective-permute-start.10) | collective-permute-done | bytes 131104 | tf_op jit(solution)/shard_map/ppermute | solution.py:293
  35.9 0.0 collective-permute-done.7.refs_3_
  35.9 1.2 %partial_residual.3 = (f32[1024,128]{1,0:T(8,128)S(1)}, bf16[1024,128]{1,0:T(8,128)(2,1)S(1)}) custom-call(bf16[256,2048]{1,0:T(8,128)(2,1)S(1)} %get-tuple-element.45.refs_0_, bf16[256,2048]{1,0:T(8,128)(2,1)S(1)} %collective-permute-done.6.refs_1_, bf16[256,2048]{1,0:T(8,128)(2,1)S(1)} %collective-permute-done.5.refs_2_, ...), custom_call_target="tpu_custom_call" | custom-call | tf_op jit(solution)/shard_map/partial_residual/pallas_call | solution.py:143
  37.1 0.3 collective-permute-start.11
  37.4 1.2 %collective-permute-done.8 = f16[512,128]{1,0:T(8,128)(2,1)S(1)} collective-permute-done((f16[512,128]{1,0:T(8,128)(2,1)S(1)}, f16[512,128]{1,0:T(8,128)(2,1)S(1)}, u32[]{:S(2)}, u32[]{:S(2)}) %collective-permute-start.8) | collective-permute-done | bytes 131104 | tf_op jit(solution)/shard_map/ppermute | solution.py:293
  38.7 1.2 %partial_residual.2 = (f32[1024,128]{1,0:T(8,128)S(1)}, bf16[1024,128]{1,0:T(8,128)(2,1)S(1)}) custom-call(bf16[256,2048]{1,0:T(8,128)(2,1)S(1)} %get-tuple-element.45.refs_0_, bf16[256,2048]{1,0:T(8,128)(2,1)S(1)} %collective-permute-done.6.refs_1_, bf16[256,2048]{1,0:T(8,128)(2,1)S(1)} %collective-permute-done.5.refs_2_, ...), custom_call_target="tpu_custom_call" | custom-call | tf_op jit(solution)/shard_map/partial_residual/pallas_call | solution.py:143
  39.9 0.3 collective-permute-start.9
  40.2 3.6 %collective-permute-done.11.refs_5_ = bf16[1024,128]{1,0:T(8,128)(2,1)S(1)} collective-permute-done((bf16[1024,128]{1,0:T(8,128)(2,1)S(1)}, bf16[1024,128]{1,0:T(8,128)(2,1)S(1)}, u32[]{:S(2)}, u32[]{:S(2)}) %collective-permute-start.11) | collective-permute-done | bytes 262176 | tf_op jit(solution)/shard_map/ppermute | solution.py:293
  43.8 0.8 %partial_gradient.2 = (f32[1,128]{1,0:T(1,128)S(1)}, f32[128,512]{1,0:T(8,128)S(1)}, f32[128,512]{1,0:T(8,128)S(1)}, bf16[144,512]{1,0:T(8,128)(2,1)S(1)}, bf16[128,512]{1,0:T(8,128)(2,1)S(1)}) custom-call(bf16[256,2048]{1,0:T(8,128)(2,1)S(1)} %get-tuple-element.45.refs_0_, bf16[256,2048]{1,0:T(8,128)(2,1)S(1)} %collective-permute-done.6.refs_1_, ...), custom_call_target="tpu_custom_call" | custom-call | tf_op jit(solution)/shard_map/partial_gradient/pallas_call | solution.py:222
  44.6 0.2 collective-permute-start.12
  44.8 1.3 %collective-permute-start.14 = (bf16[128,512]{1,0:T(8,128)(2,1)S(1)}, bf16[128,512]{1,0:T(8,128)(2,1)S(1)}, u32[]{:S(2)}, u32[]{:S(2)}) collective-permute-start(bf16[128,512]{1,0:T(8,128)(2,1)S(1)} %get-tuple-element.64), channel_id=1, source_target_pairs={{0,4},{2,6},{4,0},{6,2},{8,12},{10,14},{12,8},{14,10},{1,5},{3,7},... | collective-permute-start | bytes 393224 | tf_op jit(solution)/shard_map/ppermute | solution.py:293
  46.2 3.3 %collective-permute-done.9.refs_5_ = bf16[1024,128]{1,0:T(8,128)(2,1)S(1)} collective-permute-done((bf16[1024,128]{1,0:T(8,128)(2,1)S(1)}, bf16[1024,128]{1,0:T(8,128)(2,1)S(1)}, u32[]{:S(2)}, u32[]{:S(2)}) %collective-permute-start.9) | collective-permute-done | bytes 262176 | tf_op jit(solution)/shard_map/ppermute | solution.py:293
  49.4 0.0 collective-permute-done.12.got_ref
  49.4 0.0 copy-start.2
  49.4 0.0 copy-start.3
  49.4 0.8 %partial_gradient.3 = (f32[1,128]{1,0:T(1,128)S(1)}, f32[128,512]{1,0:T(8,128)S(1)}, f32[128,512]{1,0:T(8,128)S(1)}, bf16[272,512]{1,0:T(8,128)(2,1)S(1)}) custom-call(bf16[256,2048]{1,0:T(8,128)(2,1)S(1)} %get-tuple-element.45.refs_0_, bf16[256,2048]{1,0:T(8,128)(2,1)S(1)} %collective-permute-done.6.refs_1_, ...), custom_call_target="tpu_custom_call" | custom-call | tf_op jit(solution)/shard_map/partial_gradient/pallas_call | solution.py:222
  50.2 0.2 collective-permute-start.13
  50.5 0.5 join_far.2
  51.0 0.0 collective-permute-done.14.near_ref
  51.0 0.1 collective-permute-start.15
  51.1 7.4 %collective-permute-done.15.far_ref = bf16[144,512]{1,0:T(8,128)(2,1)S(1)} collective-permute-done((bf16[144,512]{1,0:T(8,128)(2,1)S(1)}, bf16[144,512]{1,0:T(8,128)(2,1)S(1)}, u32[]{:S(2)}, u32[]{:S(2)}) %collective-permute-start.15) | collective-permute-done | bytes 147488 | tf_op jit(solution)/shard_map/ppermute | solution.py:293
  58.5 2.0 %collective-permute-done.13.got_ref.near_ref = bf16[272,512]{1,0:T(8,128)(2,1)S(1)} collective-permute-done((bf16[272,512]{1,0:T(8,128)(2,1)S(1)}, bf16[272,512]{1,0:T(8,128)(2,1)S(1)}, u32[]{:S(2)}, u32[]{:S(2)}) %collective-permute-start.13) | collective-permute-done | bytes 278560 | tf_op jit(solution)/shard_map/ppermute | solution.py:293
  60.6 0.8 %collective-permute-start.16 = (bf16[144,512]{1,0:T(8,128)(2,1)S(1)}, bf16[144,512]{1,0:T(8,128)(2,1)S(1)}, u32[]{:S(2)}, u32[]{:S(2)}) collective-permute-start(bf16[144,512]{1,0:T(8,128)(2,1)S(1)} %get-tuple-element.69), channel_id=1, source_target_pairs={{0,8},{2,10},{4,12},{6,14},{8,0},{10,2},{12,4},{14,6},{1,9},{3,11}... | collective-permute-start | bytes 442376 | tf_op jit(solution)/shard_map/ppermute | solution.py:293
  61.4 0.0 copy-done.2
  61.4 0.0 copy-done.3
  61.4 1.2 %apply_update.2 = (f32[512,256]{1,0:T(8,128)}, f32[512,256]{1,0:T(8,128)}, f32[512,256]{1,0:T(8,128)}) custom-call(f32[128,512]{1,0:T(8,128)S(1)} %get-tuple-element.70.own_ref, bf16[128,512]{1,0:T(8,128)(2,1)S(1)} %collective-permute-done.14.near_ref, bf16[144,512]{1,0:T(8,128)(2,1)S(1)} %collective-permute-done.15.far_ref, f32[512,256]{1,0:T(8,128)S(1)} %copy-done, ...), custom_call_target="tpu_custom_call" | custom-call | tf_op jit(solution)/shard_map/apply_update/pallas_call | solution.py:277
  62.6 5.5 %collective-permute-done.16.far_ref.got_ref = bf16[144,512]{1,0:T(8,128)(2,1)S(1)} collective-permute-done((bf16[144,512]{1,0:T(8,128)(2,1)S(1)}, bf16[144,512]{1,0:T(8,128)(2,1)S(1)}, u32[]{:S(2)}, u32[]{:S(2)}) %collective-permute-start.16) | collective-permute-done | bytes 147488 | tf_op jit(solution)/shard_map/ppermute | solution.py:293
  68.1 6.6 %collective-permute-start.17 = (f32[1,128]{1,0:T(1,128)S(1)}, f32[1,128]{1,0:T(1,128)S(1)}, u32[]{:S(2)}, u32[]{:S(2)}) collective-permute-start(f32[1,128]{1,0:T(1,128)S(1)} %total_loss.1), channel_id=1, source_target_pairs={{0,1},{1,0},{2,3},{3,2},{4,5},{5,4},{6,7},{7,6},{8,9},{9,8},{10,11... | collective-permute-start | bytes 1544 | tf_op jit(solution)/shard_map/ppermute | solution.py:296
  74.7 1.1 %apply_update.3 = (f32[512,256]{1,0:T(8,128)}, f32[512,256]{1,0:T(8,128)}, f32[512,256]{1,0:T(8,128)}) custom-call(f32[128,512]{1,0:T(8,128)S(1)} %get-tuple-element.59.own_ref, bf16[272,512]{1,0:T(8,128)(2,1)S(1)} %collective-permute-done.13.got_ref.near_ref, ...), custom_call_target="tpu_custom_call", output_to_operand_aliasing={{0}: (6, {}), {1}: (7, {}), {2}: (8, {})} | custom-call | tf_op jit(solution)/shard_map/apply_update/pallas_call | solution.py:277
  75.8 0.0 collective-permute-done.17
  75.8 0.6 add_reduce_fusion
  (8 shorter events, 0.2 us)
Async XLA Ops:
  0.6 11.8 %copy-start = (f32[512,256]{1,0:T(8,128)S(1)}, f32[512,256]{1,0:T(8,128)}, u32[]{:S(2)}) copy-start(f32[512,256]{1,0:T(8,128)} %w_ref.3) | copy-start | bytes 1572868
  1.8 3.4 %collective-permute-start = (f32[1,256]{1,0:T(1,128)S(1)}, f32[1,256]{1,0:T(1,128)S(1)}, u32[]{:S(2)}, u32[]{:S(2)}) collective-permute-start(f32[1,256]{1,0:T(1,128)S(1)} %bitcast.3), channel_id=1, source_target_pairs={{0,2},{2,0},{4,6},{6,4},{8,10},{10,8},{12,14},{14,12},{1,3},{3,1},... | collective-permute-start | bytes 3080 | tf_op jit(solution)/shard_map/ppermute | solution.py:293
  3.1 1.6 %copy-start.1 = (bf16[256,4096]{1,0:T(8,128)(2,1)S(1)}, bf16[256,4096]{1,0:T(8,128)(2,1)}, u32[]{:S(2)}) copy-start(bf16[256,4096]{1,0:T(8,128)(2,1)} %h_ref.1) | copy-start | bytes 6291460
  4.6 7.8 %copy-start.4 = (bf16[512,256]{1,0:T(8,128)(2,1)S(1)}, bf16[512,256]{1,0:T(8,128)(2,1)}, u32[]{:S(2)}) copy-start(bf16[512,256]{1,0:T(8,128)(2,1)} %param.6) | copy-start | bytes 786436
  4.8 23.8 %collective-permute-start.5 = (bf16[256,2048]{1,0:T(8,128)(2,1)S(1)}, bf16[256,2048]{1,0:T(8,128)(2,1)S(1)}, u32[]{:S(2)}, u32[]{:S(2)}) collective-permute-start(bf16[256,2048]{1,0:T(8,128)(2,1)S(1)} %get-tuple-element.47), channel_id=1, source_target_pairs={{0,2},{2,0},{4,6},{6,4},{8,10},{10,8},{12,14},{14,12},{1,3},{3,1},... | collective-permute-start | bytes 3145736 | tf_op jit(solution)/shard_map/ppermute | solution.py:293
  5.1 23.5 %collective-permute-start.6 = (bf16[256,2048]{1,0:T(8,128)(2,1)S(1)}, bf16[256,2048]{1,0:T(8,128)(2,1)S(1)}, u32[]{:S(2)}, u32[]{:S(2)}) collective-permute-start(bf16[256,2048]{1,0:T(8,128)(2,1)S(1)} %get-tuple-element.45.refs_0_), channel_id=1, source_target_pairs={{0,1},{1,0},{2,3},{3,2},{4,5},{5,4},{6,7},{7,6},{8,9},{9,8},{10,11... | collective-permute-start | bytes 3145736 | tf_op jit(solution)/shard_map/ppermute | solution.py:296
  6.4 2.7 %collective-permute-start.1 = (f32[1,256]{1,0:T(1,128)S(1)}, f32[1,256]{1,0:T(1,128)S(1)}, u32[]{:S(2)}, u32[]{:S(2)}) collective-permute-start(f32[1,256]{1,0:T(1,128)S(1)} %max.9), channel_id=1, source_target_pairs={{0,4},{2,6},{4,0},{6,2},{8,12},{10,14},{12,8},{14,10},{1,5},{3,7},... | collective-permute-start | bytes 3080 | tf_op jit(solution)/shard_map/ppermute | solution.py:293
  9.1 3.3 %collective-permute-start.2 = (f32[1,256]{1,0:T(1,128)S(1)}, f32[1,256]{1,0:T(1,128)S(1)}, u32[]{:S(2)}, u32[]{:S(2)}) collective-permute-start(f32[1,256]{1,0:T(1,128)S(1)} %max.10), channel_id=1, source_target_pairs={{0,8},{2,10},{4,12},{6,14},{8,0},{10,2},{12,4},{14,6},{1,9},{3,11}... | collective-permute-start | bytes 3080 | tf_op jit(solution)/shard_map/ppermute | solution.py:293
  12.9 14.7 %collective-permute-start.3 = (f16[512,256]{1,0:T(8,128)(2,1)S(1)}, f16[512,256]{1,0:T(8,128)(2,1)S(1)}, u32[]{:S(2)}, u32[]{:S(2)}) collective-permute-start(f16[512,256]{1,0:T(8,128)(2,1)S(1)} %get-tuple-element.84), channel_id=1, source_target_pairs={{0,8},{2,10},{4,12},{6,14},{8,0},{10,2},{12,4},{14,6},{1,9},{3,11}... | collective-permute-start | bytes 786440 | tf_op jit(solution)/shard_map/ppermute | solution.py:293
  13.0 14.6 %collective-permute-start.4 = (f16[512,256]{1,0:T(8,128)(2,1)S(1)}, f16[512,256]{1,0:T(8,128)(2,1)S(1)}, u32[]{:S(2)}, u32[]{:S(2)}) collective-permute-start(f16[512,256]{1,0:T(8,128)(2,1)S(1)} %get-tuple-element.84), channel_id=1, source_target_pairs={{0,4},{2,6},{4,0},{6,2},{8,12},{10,14},{12,8},{14,10},{1,5},{3,7},... | collective-permute-start | bytes 786440 | tf_op jit(solution)/shard_map/ppermute | solution.py:293
  28.6 7.3 %collective-permute-start.7 = (bf16[256,2048]{1,0:T(8,128)(2,1)S(1)}, bf16[256,2048]{1,0:T(8,128)(2,1)S(1)}, u32[]{:S(2)}, u32[]{:S(2)}) collective-permute-start(bf16[256,2048]{1,0:T(8,128)(2,1)S(1)} %collective-permute-done.5.refs_2_), channel_id=1, source_target_pairs={{0,1},{1,0},{2,3},{3,2},{4,5},{5,4},{6,7},{7,6},{8,9},{9,8},{10,11... | collective-permute-start | bytes 3145736 | tf_op jit(solution)/shard_map/ppermute | solution.py:296
  30.6 5.2 %collective-permute-start.10 = (f16[512,128]{1,0:T(8,128)(2,1)S(1)}, f16[512,128]{1,0:T(8,128)(2,1)S(1)}, u32[]{:S(2)}, u32[]{:S(2)}) collective-permute-start(f16[512,128]{1,0:T(8,128)(2,1)S(1)} %get-tuple-element.98), channel_id=1, source_target_pairs={{0,4},{2,6},{4,0},{6,2},{8,12},{10,14},{12,8},{14,10},{1,5},{3,7},... | collective-permute-start | bytes 393224 | tf_op jit(solution)/shard_map/ppermute | solution.py:293
  30.8 7.8 %collective-permute-start.8 = (f16[512,128]{1,0:T(8,128)(2,1)S(1)}, f16[512,128]{1,0:T(8,128)(2,1)S(1)}, u32[]{:S(2)}, u32[]{:S(2)}) collective-permute-start(f16[512,128]{1,0:T(8,128)(2,1)S(1)} %get-tuple-element.99), channel_id=1, source_target_pairs={{0,4},{2,6},{4,0},{6,2},{8,12},{10,14},{12,8},{14,10},{1,5},{3,7},... | collective-permute-start | bytes 393224 | tf_op jit(solution)/shard_map/ppermute | solution.py:293
  37.1 6.7 %collective-permute-start.11 = (bf16[1024,128]{1,0:T(8,128)(2,1)S(1)}, bf16[1024,128]{1,0:T(8,128)(2,1)S(1)}, u32[]{:S(2)}, u32[]{:S(2)}) collective-permute-start(bf16[1024,128]{1,0:T(8,128)(2,1)S(1)} %get-tuple-element.55), channel_id=1, source_target_pairs={{0,2},{2,0},{4,6},{6,4},{8,10},{10,8},{12,14},{14,12},{1,3},{3,1},... | collective-permute-start | bytes 786440 | tf_op jit(solution)/shard_map/ppermute | solution.py:293
  39.9 9.5 %collective-permute-start.9 = (bf16[1024,128]{1,0:T(8,128)(2,1)S(1)}, bf16[1024,128]{1,0:T(8,128)(2,1)S(1)}, u32[]{:S(2)}, u32[]{:S(2)}) collective-permute-start(bf16[1024,128]{1,0:T(8,128)(2,1)S(1)} %get-tuple-element.53), channel_id=1, source_target_pairs={{0,2},{2,0},{4,6},{6,4},{8,10},{10,8},{12,14},{14,12},{1,3},{3,1},... | collective-permute-start | bytes 786440 | tf_op jit(solution)/shard_map/ppermute | solution.py:293
  44.6 4.8 %collective-permute-start.12 = (bf16[144,512]{1,0:T(8,128)(2,1)S(1)}, bf16[144,512]{1,0:T(8,128)(2,1)S(1)}, u32[]{:S(2)}, u32[]{:S(2)}) collective-permute-start(bf16[144,512]{1,0:T(8,128)(2,1)S(1)} %get-tuple-element.56), channel_id=1, source_target_pairs={{0,4},{2,6},{4,0},{6,2},{8,12},{10,14},{12,8},{14,10},{1,5},{3,7},... | collective-permute-start | bytes 442376 | tf_op jit(solution)/shard_map/ppermute | solution.py:293
  44.8 6.2 %collective-permute-start.14 = (bf16[128,512]{1,0:T(8,128)(2,1)S(1)}, bf16[128,512]{1,0:T(8,128)(2,1)S(1)}, u32[]{:S(2)}, u32[]{:S(2)}) collective-permute-start(bf16[128,512]{1,0:T(8,128)(2,1)S(1)} %get-tuple-element.64), channel_id=1, source_target_pairs={{0,4},{2,6},{4,0},{6,2},{8,12},{10,14},{12,8},{14,10},{1,5},{3,7},... | collective-permute-start | bytes 393224 | tf_op jit(solution)/shard_map/ppermute | solution.py:293
  49.4 12.0 %copy-start.2 = (f32[512,256]{1,0:T(8,128)S(1)}, f32[512,256]{1,0:T(8,128)}, u32[]{:S(2)}) copy-start(f32[512,256]{1,0:T(8,128)} %m_ref.3) | copy-start | bytes 1572868
  49.4 12.0 %copy-start.3 = (f32[512,256]{1,0:T(8,128)S(1)}, f32[512,256]{1,0:T(8,128)}, u32[]{:S(2)}) copy-start(f32[512,256]{1,0:T(8,128)} %v_ref.3) | copy-start | bytes 1572868
  50.2 10.3 %collective-permute-start.13 = (bf16[272,512]{1,0:T(8,128)(2,1)S(1)}, bf16[272,512]{1,0:T(8,128)(2,1)S(1)}, u32[]{:S(2)}, u32[]{:S(2)}) collective-permute-start(bf16[272,512]{1,0:T(8,128)(2,1)S(1)} %get-tuple-element.60), channel_id=1, source_target_pairs={{0,4},{2,6},{4,0},{6,2},{8,12},{10,14},{12,8},{14,10},{1,5},{3,7},... | collective-permute-start | bytes 835592 | tf_op jit(solution)/shard_map/ppermute | solution.py:293
  51.0 7.5 %collective-permute-start.15 = (bf16[144,512]{1,0:T(8,128)(2,1)S(1)}, bf16[144,512]{1,0:T(8,128)(2,1)S(1)}, u32[]{:S(2)}, u32[]{:S(2)}) collective-permute-start(bf16[144,512]{1,0:T(8,128)(2,1)S(1)} %get-tuple-element.65), channel_id=1, source_target_pairs={{0,8},{2,10},{4,12},{6,14},{8,0},{10,2},{12,4},{14,6},{1,9},{3,11}... | collective-permute-start | bytes 442376 | tf_op jit(solution)/shard_map/ppermute | solution.py:293
  60.6 7.5 %collective-permute-start.16 = (bf16[144,512]{1,0:T(8,128)(2,1)S(1)}, bf16[144,512]{1,0:T(8,128)(2,1)S(1)}, u32[]{:S(2)}, u32[]{:S(2)}) collective-permute-start(bf16[144,512]{1,0:T(8,128)(2,1)S(1)} %get-tuple-element.69), channel_id=1, source_target_pairs={{0,8},{2,10},{4,12},{6,14},{8,0},{10,2},{12,4},{14,6},{1,9},{3,11}... | collective-permute-start | bytes 442376 | tf_op jit(solution)/shard_map/ppermute | solution.py:293
  68.1 7.7 %collective-permute-start.17 = (f32[1,128]{1,0:T(1,128)S(1)}, f32[1,128]{1,0:T(1,128)S(1)}, u32[]{:S(2)}, u32[]{:S(2)}) collective-permute-start(f32[1,128]{1,0:T(1,128)S(1)} %total_loss.1), channel_id=1, source_target_pairs={{0,1},{1,0},{2,3},{3,2},{4,5},{5,4},{6,7},{7,6},{8,9},{9,8},{10,11... | collective-permute-start | bytes 1544 | tf_op jit(solution)/shard_map/ppermute | solution.py:296

commit v3 on v2

--- a/solution.py
+++ b/solution.py
@@ -304,15 +304,16 @@
     keep, column_max = together(keep, column_max)
     peer = flip(send, 1)
     near_keep = swap_cores(keep)
-    column_max = jnp.maximum(column_max, flip(column_max, 2))
-    column_max = jnp.maximum(column_max, flip(column_max, 4))
+    peaks = [column_max] + [flip(column_max, 2 * k) for k in range(1, blocks)]
+    column_max = jnp.maximum(jnp.maximum(peaks[0], peaks[1]), jnp.maximum(peaks[2], peaks[3]))
     difference = weight_difference(student_weight, teacher_weight, column_max) * 2.0**15
     coded = difference.astype(jnp.float16)
 
     far = flip(coded, 4)
     near = flip(coded, 2)
-    far, near, peer, near_keep = together(far, near, peer, near_keep)
+    far, near, near_keep = together(far, near, near_keep)
     across = [flip(far[:, half], 2) for half in halves]
+    peer, across[0] = together(peer, across[0])
     pieces = [keep, near_keep, peer, swap_cores(peer)]
 
     def residual(c):

time: 78.4 us -> 76.6 us (0.977)
  the two profiles are of different devices: /device:TPU:29 before, /device:TPU:0 now
where the time goes in v3:
time: 76.6 us; the launch traced here: 76.4 us
  waiting for transfers between devices  40.5 us (53%)
  starting transfers between devices  22 us (29%)
  Pallas kernels  7.13 us (9%)
  other arithmetic  2.56 us (3%)
  between operations  2.54 us (3%)
  local copies, waits for them, and re-layouts  1.66 us (2%)
    ppermute x16, waiting for transfers between devices, flip(): return lax.ppermute(array, 'fsdp', [(i, i ^ bit) for i in range(fsdp)])  38.8 us
    ppermute x16, starting transfers between devices, flip(): return lax.ppermute(array, 'fsdp', [(i, i ^ bit) for i in range(fsdp)])  21.9 us
    pallas_call x2, Pallas kernels, partial_residual(): pl.pallas_call(kernel, out_shape=(pltpu.VMEM(shape, f32), pltpu.VMEM(shap...  2.49 us
    pallas_call x2, Pallas kernels, apply_update(): pl.pallas_call(kernel, grid=(1,), out_shape=(shape,) * 3, in_specs=vmem(6...  2.31 us
    ppermute x3, waiting for transfers between devices, swap_cores(): return lax.ppermute(array, 'tensor', [(0, 1), (1, 0)])  1.66 us
    unnamed x10, local copies, waits for them, and re-layouts  1.61 us
    pallas_call x2, Pallas kernels, partial_gradient(): pl.pallas_call(kernel, out_shape=(pltpu.VMEM((1, columns), f32), pltpu.VM...  1.59 us
  transfers between devices with their start and end apart: 19, of which 13 were waited for; matrix products, arithmetic and copies ran while one was open for 1% of the time, Pallas kernels for 9%

profile of v3, /device:TPU:0, one launch (start us, length us, event | category | flops | bytes accessed | tf_op | source)
XLA Modules:
  0.0 76.4 jit_solution(5790463503036474851)
XLA Ops:
  0.6 0.0 copy-start
  0.6 1.1 %abs_reduce_fusion = f32[256]{0:T(256)S(1)} fusion(f32[512,256]{1,0:T(8,128)} %w_ref.3), kind=kLoop, calls=%fused_computation.19 | loop fusion | flops 261888 | bytes 525312 | tf_op jit(solution)/shard_map/reduce_max | solution.py:301
  1.8 3.0 %collective-permute-start = (f32[1,256]{1,0:T(1,128)S(1)}, f32[1,256]{1,0:T(1,128)S(1)}, u32[]{:S(2)}, u32[]{:S(2)}) collective-permute-start(f32[1,256]{1,0:T(1,128)S(1)} %bitcast.3), channel_id=1, source_target_pairs={{0,2},{2,0},{4,6},{6,4},{8,10},{10,8},{12,14},{14,12},{1,3},{3,1},... | collective-permute-start | bytes 3080 | tf_op jit(solution)/shard_map/ppermute | solution.py:293
  4.8 0.0 copy-start.1
  4.8 1.6 %copy-done.1 = bf16[256,4096]{1,0:T(8,128)(2,1)S(1)} copy-done((bf16[256,4096]{1,0:T(8,128)(2,1)S(1)}, bf16[256,4096]{1,0:T(8,128)(2,1)}, u32[]{:S(2)}) %copy-start.1) | copy-done | bytes 2097176
  6.4 0.0 copy-start.4
  6.4 0.1 sort_features.1
  6.5 0.0 collective-permute-done
  6.6 0.1 collective-permute-start.6
  6.6 1.8 %collective-permute-start.1 = (f32[1,256]{1,0:T(1,128)S(1)}, f32[1,256]{1,0:T(1,128)S(1)}, u32[]{:S(2)}, u32[]{:S(2)}) collective-permute-start(f32[1,256]{1,0:T(1,128)S(1)} %max.12), channel_id=1, source_target_pairs={{0,4},{2,6},{4,0},{6,2},{8,12},{10,14},{12,8},{14,10},{1,5},{3,7},... | collective-permute-start | bytes 3080 | tf_op jit(solution)/shard_map/ppermute | solution.py:293
  8.4 2.6 %collective-permute-start.2 = (f32[1,256]{1,0:T(1,128)S(1)}, f32[1,256]{1,0:T(1,128)S(1)}, u32[]{:S(2)}, u32[]{:S(2)}) collective-permute-start(f32[1,256]{1,0:T(1,128)S(1)} %max.12), channel_id=1, source_target_pairs={{0,8},{2,10},{4,12},{6,14},{8,0},{10,2},{12,4},{14,6},{1,9},{3,11}... | collective-permute-start | bytes 3080 | tf_op jit(solution)/shard_map/ppermute | solution.py:293
  11.0 0.1 collective-permute-start.3
  11.1 1.7 %collective-permute-start.7 = (bf16[256,2048]{1,0:T(8,128)(2,1)S(1)}, bf16[256,2048]{1,0:T(8,128)(2,1)S(1)}, u32[]{:S(2)}, u32[]{:S(2)}) collective-permute-start(bf16[256,2048]{1,0:T(8,128)(2,1)S(1)} %get-tuple-element.49), channel_id=1, source_target_pairs={{0,2},{2,0},{4,6},{6,4},{8,10},{10,8},{12,14},{14,12},{1,3},{3,1},... | collective-permute-start | bytes 3145736 | tf_op jit(solution)/shard_map/ppermute | solution.py:293
  12.7 0.0 collective-permute-done.1
  12.8 0.2 collective-permute-done.2
  12.9 3.5 %collective-permute-done.3 = f32[1,256]{1,0:T(1,128)S(1)} collective-permute-done((f32[1,256]{1,0:T(1,128)S(1)}, f32[1,256]{1,0:T(1,128)S(1)}, u32[]{:S(2)}, u32[]{:S(2)}) %collective-permute-start.3) | collective-permute-done | bytes 1056 | tf_op jit(solution)/shard_map/ppermute | solution.py:293
  16.4 0.0 copy-done
  16.4 0.0 copy-done.4
  16.4 0.4 fusion.19
  16.9 0.1 collective-permute-start.4
  16.9 0.6 collective-permute-start.5
  17.6 11.1 %collective-permute-done.4 = f16[512,256]{1,0:T(8,128)(2,1)S(1)} collective-permute-done((f16[512,256]{1,0:T(8,128)(2,1)S(1)}, f16[512,256]{1,0:T(8,128)(2,1)S(1)}, u32[]{:S(2)}, u32[]{:S(2)}) %collective-permute-start.4) | collective-permute-done | bytes 262176 | tf_op jit(solution)/shard_map/ppermute | solution.py:293
  28.7 1.0 %collective-permute-done.5 = f16[512,256]{1,0:T(8,128)(2,1)S(1)} collective-permute-done((f16[512,256]{1,0:T(8,128)(2,1)S(1)}, f16[512,256]{1,0:T(8,128)(2,1)S(1)}, u32[]{:S(2)}, u32[]{:S(2)}) %collective-permute-start.5) | collective-permute-done | bytes 262176 | tf_op jit(solution)/shard_map/ppermute | solution.py:293
  29.6 0.0 collective-permute-done.6.refs_1_
  29.6 0.1 fusion.21
  29.7 0.3 collective-permute-start.8
  30.0 6.0 %collective-permute-done.7.refs_2_ = bf16[256,2048]{1,0:T(8,128)(2,1)S(1)} collective-permute-done((bf16[256,2048]{1,0:T(8,128)(2,1)S(1)}, bf16[256,2048]{1,0:T(8,128)(2,1)S(1)}, u32[]{:S(2)}, u32[]{:S(2)}) %collective-permute-start.7) | collective-permute-done | bytes 1048608 | tf_op jit(solution)/shard_map/ppermute | solution.py:293
  36.0 0.0 collective-permute-done.8
  36.1 0.0 collective-permute-start.9
  36.1 0.1 fusion.15
  36.1 0.7 collective-permute-start.10
  36.8 0.2 fusion.16
  37.1 1.7 %collective-permute-done.9.refs_3_ = bf16[256,2048]{1,0:T(8,128)(2,1)S(1)} collective-permute-done((bf16[256,2048]{1,0:T(8,128)(2,1)S(1)}, bf16[256,2048]{1,0:T(8,128)(2,1)S(1)}, u32[]{:S(2)}, u32[]{:S(2)}) %collective-permute-start.9) | collective-permute-done | bytes 1048608 | tf_op jit(solution)/shard_map/ppermute | solution.py:296
  38.7 1.2 %partial_residual.3 = (f32[1024,128]{1,0:T(8,128)S(1)}, bf16[1024,128]{1,0:T(8,128)(2,1)S(1)}) custom-call(bf16[256,2048]{1,0:T(8,128)(2,1)S(1)} %get-tuple-element.46.refs_0_, bf16[256,2048]{1,0:T(8,128)(2,1)S(1)} %collective-permute-done.6.refs_1_, bf16[256,2048]{1,0:T(8,128)(2,1)S(1)} %collective-permute-done.7.refs_2_, ...), custom_call_target="tpu_custom_call" | custom-call | tf_op jit(solution)/shard_map/partial_residual/pallas_call | solution.py:143
  40.0 1.6 %collective-permute-start.12 = (bf16[1024,128]{1,0:T(8,128)(2,1)S(1)}, bf16[1024,128]{1,0:T(8,128)(2,1)S(1)}, u32[]{:S(2)}, u32[]{:S(2)}) collective-permute-start(bf16[1024,128]{1,0:T(8,128)(2,1)S(1)} %get-tuple-element.57), channel_id=1, source_target_pairs={{0,2},{2,0},{4,6},{6,4},{8,10},{10,8},{12,14},{14,12},{1,3},{3,1},... | collective-permute-start | bytes 786440 | tf_op jit(solution)/shard_map/ppermute | solution.py:293
  41.5 0.6 collective-permute-done.10
  42.2 1.2 %partial_residual.2 = (f32[1024,128]{1,0:T(8,128)S(1)}, bf16[1024,128]{1,0:T(8,128)(2,1)S(1)}) custom-call(bf16[256,2048]{1,0:T(8,128)(2,1)S(1)} %get-tuple-element.46.refs_0_, bf16[256,2048]{1,0:T(8,128)(2,1)S(1)} %collective-permute-done.6.refs_1_, bf16[256,2048]{1,0:T(8,128)(2,1)S(1)} %collective-permute-done.7.refs_2_, ...), custom_call_target="tpu_custom_call" | custom-call | tf_op jit(solution)/shard_map/partial_residual/pallas_call | solution.py:143
  43.4 1.6 %collective-permute-start.11 = (bf16[1024,128]{1,0:T(8,128)(2,1)S(1)}, bf16[1024,128]{1,0:T(8,128)(2,1)S(1)}, u32[]{:S(2)}, u32[]{:S(2)}) collective-permute-start(bf16[1024,128]{1,0:T(8,128)(2,1)S(1)} %get-tuple-element.54), channel_id=1, source_target_pairs={{0,2},{2,0},{4,6},{6,4},{8,10},{10,8},{12,14},{14,12},{1,3},{3,1},... | collective-permute-start | bytes 786440 | tf_op jit(solution)/shard_map/ppermute | solution.py:293
  45.0 4.2 %collective-permute-done.12.refs_5_ = bf16[1024,128]{1,0:T(8,128)(2,1)S(1)} collective-permute-done((bf16[1024,128]{1,0:T(8,128)(2,1)S(1)}, bf16[1024,128]{1,0:T(8,128)(2,1)S(1)}, u32[]{:S(2)}, u32[]{:S(2)}) %collective-permute-start.12) | collective-permute-done | bytes 262176 | tf_op jit(solution)/shard_map/ppermute | solution.py:293
  49.2 0.8 %partial_gradient.2 = (f32[1,128]{1,0:T(1,128)S(1)}, f32[128,512]{1,0:T(8,128)S(1)}, f32[128,512]{1,0:T(8,128)S(1)}, bf16[144,512]{1,0:T(8,128)(2,1)S(1)}, bf16[128,512]{1,0:T(8,128)(2,1)S(1)}) custom-call(bf16[256,2048]{1,0:T(8,128)(2,1)S(1)} %get-tuple-element.46.refs_0_, bf16[256,2048]{1,0:T(8,128)(2,1)S(1)} %collective-permute-done.6.refs_1_, ...), custom_call_target="tpu_custom_call" | custom-call | tf_op jit(solution)/shard_map/partial_gradient/pallas_call | solution.py:222
  50.0 0.7 collective-permute-start.13
  50.7 1.4 %collective-permute-start.15 = (bf16[128,512]{1,0:T(8,128)(2,1)S(1)}, bf16[128,512]{1,0:T(8,128)(2,1)S(1)}, u32[]{:S(2)}, u32[]{:S(2)}) collective-permute-start(bf16[128,512]{1,0:T(8,128)(2,1)S(1)} %get-tuple-element.66), channel_id=1, source_target_pairs={{0,4},{2,6},{4,0},{6,2},{8,12},{10,14},{12,8},{14,10},{1,5},{3,7},... | collective-permute-start | bytes 393224 | tf_op jit(solution)/shard_map/ppermute | solution.py:293
  52.1 1.9 %collective-permute-done.11.refs_5_ = bf16[1024,128]{1,0:T(8,128)(2,1)S(1)} collective-permute-done((bf16[1024,128]{1,0:T(8,128)(2,1)S(1)}, bf16[1024,128]{1,0:T(8,128)(2,1)S(1)}, u32[]{:S(2)}, u32[]{:S(2)}) %collective-permute-start.11) | collective-permute-done | bytes 262176 | tf_op jit(solution)/shard_map/ppermute | solution.py:293
  54.0 1.7 %collective-permute-done.13.got_ref = bf16[144,512]{1,0:T(8,128)(2,1)S(1)} collective-permute-done((bf16[144,512]{1,0:T(8,128)(2,1)S(1)}, bf16[144,512]{1,0:T(8,128)(2,1)S(1)}, u32[]{:S(2)}, u32[]{:S(2)}) %collective-permute-start.13) | collective-permute-done | bytes 147488 | tf_op jit(solution)/shard_map/ppermute | solution.py:293
  55.7 0.0 copy-start.2
  55.7 0.0 copy-start.3
  55.7 0.8 %partial_gradient.3 = (f32[1,128]{1,0:T(1,128)S(1)}, f32[128,512]{1,0:T(8,128)S(1)}, f32[128,512]{1,0:T(8,128)S(1)}, bf16[272,512]{1,0:T(8,128)(2,1)S(1)}) custom-call(bf16[256,2048]{1,0:T(8,128)(2,1)S(1)} %get-tuple-element.46.refs_0_, bf16[256,2048]{1,0:T(8,128)(2,1)S(1)} %collective-permute-done.6.refs_1_, ...), custom_call_target="tpu_custom_call" | custom-call | tf_op jit(solution)/shard_map/partial_gradient/pallas_call | solution.py:222
  56.5 0.7 collective-permute-start.14
  57.2 0.5 join_far.2
  57.7 0.0 collective-permute-done.15.near_ref
  57.7 3.5 %collective-permute-start.16 = (bf16[144,512]{1,0:T(8,128)(2,1)S(1)}, bf16[144,512]{1,0:T(8,128)(2,1)S(1)}, u32[]{:S(2)}, u32[]{:S(2)}) collective-permute-start(bf16[144,512]{1,0:T(8,128)(2,1)S(1)} %get-tuple-element.67), channel_id=1, source_target_pairs={{0,8},{2,10},{4,12},{6,14},{8,0},{10,2},{12,4},{14,6},{1,9},{3,11}... | collective-permute-start | bytes 442376 | tf_op jit(solution)/shard_map/ppermute | solution.py:293
  61.2 4.3 %collective-permute-done.16.far_ref = bf16[144,512]{1,0:T(8,128)(2,1)S(1)} collective-permute-done((bf16[144,512]{1,0:T(8,128)(2,1)S(1)}, bf16[144,512]{1,0:T(8,128)(2,1)S(1)}, u32[]{:S(2)}, u32[]{:S(2)}) %collective-permute-start.16) | collective-permute-done | bytes 147488 | tf_op jit(solution)/shard_map/ppermute | solution.py:293
  65.6 0.7 collective-permute-done.14.got_ref.near_ref
  66.3 1.7 %collective-permute-start.17 = (bf16[144,512]{1,0:T(8,128)(2,1)S(1)}, bf16[144,512]{1,0:T(8,128)(2,1)S(1)}, u32[]{:S(2)}, u32[]{:S(2)}) collective-permute-start(bf16[144,512]{1,0:T(8,128)(2,1)S(1)} %get-tuple-element.71), channel_id=1, source_target_pairs={{0,8},{2,10},{4,12},{6,14},{8,0},{10,2},{12,4},{14,6},{1,9},{3,11}... | collective-permute-start | bytes 442376 | tf_op jit(solution)/shard_map/ppermute | solution.py:293
  68.0 0.0 copy-done.2
  68.0 0.0 copy-done.3
  68.0 1.2 %apply_update.2 = (f32[512,256]{1,0:T(8,128)}, f32[512,256]{1,0:T(8,128)}, f32[512,256]{1,0:T(8,128)}) custom-call(f32[128,512]{1,0:T(8,128)S(1)} %get-tuple-element.72.own_ref, bf16[128,512]{1,0:T(8,128)(2,1)S(1)} %collective-permute-done.15.near_ref, bf16[144,512]{1,0:T(8,128)(2,1)S(1)} %collective-permute-done.16.far_ref, f32[512,256]{1,0:T(8,128)S(1)} %copy-done, ...), custom_call_target="tpu_custom_call" | custom-call | tf_op jit(solution)/shard_map/apply_update/pallas_call | solution.py:277
  69.2 3.6 %collective-permute-done.17.far_ref.got_ref = bf16[144,512]{1,0:T(8,128)(2,1)S(1)} collective-permute-done((bf16[144,512]{1,0:T(8,128)(2,1)S(1)}, bf16[144,512]{1,0:T(8,128)(2,1)S(1)}, u32[]{:S(2)}, u32[]{:S(2)}) %collective-permute-start.17) | collective-permute-done | bytes 147488 | tf_op jit(solution)/shard_map/ppermute | solution.py:293
  72.8 0.0 collective-permute-start.18
  72.8 1.2 %apply_update.3 = (f32[512,256]{1,0:T(8,128)}, f32[512,256]{1,0:T(8,128)}, f32[512,256]{1,0:T(8,128)}) custom-call(f32[128,512]{1,0:T(8,128)S(1)} %get-tuple-element.61.own_ref, bf16[272,512]{1,0:T(8,128)(2,1)S(1)} %collective-permute-done.14.got_ref.near_ref, ...), custom_call_target="tpu_custom_call", output_to_operand_aliasing={{0}: (6, {}), {1}: (7, {}), {2}: (8, {})} | custom-call | tf_op jit(solution)/shard_map/apply_update/pallas_call | solution.py:277
  74.0 0.0 collective-permute-done.18
  74.0 0.6 add_reduce_fusion
  (7 shorter events, 0.2 us)
Async XLA Ops:
  0.6 15.8 %copy-start = (f32[512,256]{1,0:T(8,128)S(1)}, f32[512,256]{1,0:T(8,128)}, u32[]{:S(2)}) copy-start(f32[512,256]{1,0:T(8,128)} %w_ref.3) | copy-start | bytes 1572868
  1.8 4.8 %collective-permute-start = (f32[1,256]{1,0:T(1,128)S(1)}, f32[1,256]{1,0:T(1,128)S(1)}, u32[]{:S(2)}, u32[]{:S(2)}) collective-permute-start(f32[1,256]{1,0:T(1,128)S(1)} %bitcast.3), channel_id=1, source_target_pairs={{0,2},{2,0},{4,6},{6,4},{8,10},{10,8},{12,14},{14,12},{1,3},{3,1},... | collective-permute-start | bytes 3080 | tf_op jit(solution)/shard_map/ppermute | solution.py:293
  4.8 1.6 %copy-start.1 = (bf16[256,4096]{1,0:T(8,128)(2,1)S(1)}, bf16[256,4096]{1,0:T(8,128)(2,1)}, u32[]{:S(2)}) copy-start(bf16[256,4096]{1,0:T(8,128)(2,1)} %h_ref.1) | copy-start | bytes 6291460
  6.4 10.0 %copy-start.4 = (bf16[512,256]{1,0:T(8,128)(2,1)S(1)}, bf16[512,256]{1,0:T(8,128)(2,1)}, u32[]{:S(2)}) copy-start(bf16[512,256]{1,0:T(8,128)(2,1)} %param.6) | copy-start | bytes 786436
  6.6 23.1 %collective-permute-start.6 = (bf16[256,2048]{1,0:T(8,128)(2,1)S(1)}, bf16[256,2048]{1,0:T(8,128)(2,1)S(1)}, u32[]{:S(2)}, u32[]{:S(2)}) collective-permute-start(bf16[256,2048]{1,0:T(8,128)(2,1)S(1)} %get-tuple-element.46.refs_0_), channel_id=1, source_target_pairs={{0,1},{1,0},{2,3},{3,2},{4,5},{5,4},{6,7},{7,6},{8,9},{9,8},{10,11... | collective-permute-start | bytes 3145736 | tf_op jit(solution)/shard_map/ppermute | solution.py:296
  6.6 6.1 %collective-permute-start.1 = (f32[1,256]{1,0:T(1,128)S(1)}, f32[1,256]{1,0:T(1,128)S(1)}, u32[]{:S(2)}, u32[]{:S(2)}) collective-permute-start(f32[1,256]{1,0:T(1,128)S(1)} %max.12), channel_id=1, source_target_pairs={{0,4},{2,6},{4,0},{6,2},{8,12},{10,14},{12,8},{14,10},{1,5},{3,7},... | collective-permute-start | bytes 3080 | tf_op jit(solution)/shard_map/ppermute | solution.py:293
  8.4 4.5 %collective-permute-start.2 = (f32[1,256]{1,0:T(1,128)S(1)}, f32[1,256]{1,0:T(1,128)S(1)}, u32[]{:S(2)}, u32[]{:S(2)}) collective-permute-start(f32[1,256]{1,0:T(1,128)S(1)} %max.12), channel_id=1, source_target_pairs={{0,8},{2,10},{4,12},{6,14},{8,0},{10,2},{12,4},{14,6},{1,9},{3,11}... | collective-permute-start | bytes 3080 | tf_op jit(solution)/shard_map/ppermute | solution.py:293
  11.0 5.4 %collective-permute-start.3 = (f32[1,256]{1,0:T(1,128)S(1)}, f32[1,256]{1,0:T(1,128)S(1)}, u32[]{:S(2)}, u32[]{:S(2)}) collective-permute-start(f32[1,256]{1,0:T(1,128)S(1)} %max.12), channel_id=1, source_target_pairs={{0,12},{2,14},{4,8},{6,10},{8,4},{10,6},{12,0},{14,2},{1,13},{3,15... | collective-permute-start | bytes 3080 | tf_op jit(solution)/shard_map/ppermute | solution.py:293
  11.1 25.0 %collective-permute-start.7 = (bf16[256,2048]{1,0:T(8,128)(2,1)S(1)}, bf16[256,2048]{1,0:T(8,128)(2,1)S(1)}, u32[]{:S(2)}, u32[]{:S(2)}) collective-permute-start(bf16[256,2048]{1,0:T(8,128)(2,1)S(1)} %get-tuple-element.49), channel_id=1, source_target_pairs={{0,2},{2,0},{4,6},{6,4},{8,10},{10,8},{12,14},{14,12},{1,3},{3,1},... | collective-permute-start | bytes 3145736 | tf_op jit(solution)/shard_map/ppermute | solution.py:293
  16.9 11.8 %collective-permute-start.4 = (f16[512,256]{1,0:T(8,128)(2,1)S(1)}, f16[512,256]{1,0:T(8,128)(2,1)S(1)}, u32[]{:S(2)}, u32[]{:S(2)}) collective-permute-start(f16[512,256]{1,0:T(8,128)(2,1)S(1)} %get-tuple-element.86), channel_id=1, source_target_pairs={{0,8},{2,10},{4,12},{6,14},{8,0},{10,2},{12,4},{14,6},{1,9},{3,11}... | collective-permute-start | bytes 786440 | tf_op jit(solution)/shard_map/ppermute | solution.py:293
  16.9 12.7 %collective-permute-start.5 = (f16[512,256]{1,0:T(8,128)(2,1)S(1)}, f16[512,256]{1,0:T(8,128)(2,1)S(1)}, u32[]{:S(2)}, u32[]{:S(2)}) collective-permute-start(f16[512,256]{1,0:T(8,128)(2,1)S(1)} %get-tuple-element.86), channel_id=1, source_target_pairs={{0,4},{2,6},{4,0},{6,2},{8,12},{10,14},{12,8},{14,10},{1,5},{3,7},... | collective-permute-start | bytes 786440 | tf_op jit(solution)/shard_map/ppermute | solution.py:293
  29.7 6.3 %collective-permute-start.8 = (f16[512,128]{1,0:T(8,128)(2,1)S(1)}, f16[512,128]{1,0:T(8,128)(2,1)S(1)}, u32[]{:S(2)}, u32[]{:S(2)}) collective-permute-start(f16[512,128]{1,0:T(8,128)(2,1)S(1)} %get-tuple-element.101), channel_id=1, source_target_pairs={{0,4},{2,6},{4,0},{6,2},{8,12},{10,14},{12,8},{14,10},{1,5},{3,7},... | collective-permute-start | bytes 393224 | tf_op jit(solution)/shard_map/ppermute | solution.py:293
  36.1 2.7 %collective-permute-start.9 = (bf16[256,2048]{1,0:T(8,128)(2,1)S(1)}, bf16[256,2048]{1,0:T(8,128)(2,1)S(1)}, u32[]{:S(2)}, u32[]{:S(2)}) collective-permute-start(bf16[256,2048]{1,0:T(8,128)(2,1)S(1)} %collective-permute-done.7.refs_2_), channel_id=1, source_target_pairs={{0,1},{1,0},{2,3},{3,2},{4,5},{5,4},{6,7},{7,6},{8,9},{9,8},{10,11... | collective-permute-start | bytes 3145736 | tf_op jit(solution)/shard_map/ppermute | solution.py:296
  36.1 6.0 %collective-permute-start.10 = (f16[512,128]{1,0:T(8,128)(2,1)S(1)}, f16[512,128]{1,0:T(8,128)(2,1)S(1)}, u32[]{:S(2)}, u32[]{:S(2)}) collective-permute-start(f16[512,128]{1,0:T(8,128)(2,1)S(1)} %get-tuple-element.100), channel_id=1, source_target_pairs={{0,4},{2,6},{4,0},{6,2},{8,12},{10,14},{12,8},{14,10},{1,5},{3,7},... | collective-permute-start | bytes 393224 | tf_op jit(solution)/shard_map/ppermute | solution.py:293
  40.0 9.2 %collective-permute-start.12 = (bf16[1024,128]{1,0:T(8,128)(2,1)S(1)}, bf16[1024,128]{1,0:T(8,128)(2,1)S(1)}, u32[]{:S(2)}, u32[]{:S(2)}) collective-permute-start(bf16[1024,128]{1,0:T(8,128)(2,1)S(1)} %get-tuple-element.57), channel_id=1, source_target_pairs={{0,2},{2,0},{4,6},{6,4},{8,10},{10,8},{12,14},{14,12},{1,3},{3,1},... | collective-permute-start | bytes 786440 | tf_op jit(solution)/shard_map/ppermute | solution.py:293
  43.4 10.6 %collective-permute-start.11 = (bf16[1024,128]{1,0:T(8,128)(2,1)S(1)}, bf16[1024,128]{1,0:T(8,128)(2,1)S(1)}, u32[]{:S(2)}, u32[]{:S(2)}) collective-permute-start(bf16[1024,128]{1,0:T(8,128)(2,1)S(1)} %get-tuple-element.54), channel_id=1, source_target_pairs={{0,2},{2,0},{4,6},{6,4},{8,10},{10,8},{12,14},{14,12},{1,3},{3,1},... | collective-permute-start | bytes 786440 | tf_op jit(solution)/shard_map/ppermute | solution.py:293
  50.0 5.7 %collective-permute-start.13 = (bf16[144,512]{1,0:T(8,128)(2,1)S(1)}, bf16[144,512]{1,0:T(8,128)(2,1)S(1)}, u32[]{:S(2)}, u32[]{:S(2)}) collective-permute-start(bf16[144,512]{1,0:T(8,128)(2,1)S(1)} %get-tuple-element.58), channel_id=1, source_target_pairs={{0,4},{2,6},{4,0},{6,2},{8,12},{10,14},{12,8},{14,10},{1,5},{3,7},... | collective-permute-start | bytes 442376 | tf_op jit(solution)/shard_map/ppermute | solution.py:293
  50.7 7.1 %collective-permute-start.15 = (bf16[128,512]{1,0:T(8,128)(2,1)S(1)}, bf16[128,512]{1,0:T(8,128)(2,1)S(1)}, u32[]{:S(2)}, u32[]{:S(2)}) collective-permute-start(bf16[128,512]{1,0:T(8,128)(2,1)S(1)} %get-tuple-element.66), channel_id=1, source_target_pairs={{0,4},{2,6},{4,0},{6,2},{8,12},{10,14},{12,8},{14,10},{1,5},{3,7},... | collective-permute-start | bytes 393224 | tf_op jit(solution)/shard_map/ppermute | solution.py:293
  55.7 12.3 %copy-start.2 = (f32[512,256]{1,0:T(8,128)S(1)}, f32[512,256]{1,0:T(8,128)}, u32[]{:S(2)}) copy-start(f32[512,256]{1,0:T(8,128)} %m_ref.3) | copy-start | bytes 1572868
  55.7 12.3 %copy-start.3 = (f32[512,256]{1,0:T(8,128)S(1)}, f32[512,256]{1,0:T(8,128)}, u32[]{:S(2)}) copy-start(f32[512,256]{1,0:T(8,128)} %v_ref.3) | copy-start | bytes 1572868
  56.5 9.7 %collective-permute-start.14 = (bf16[272,512]{1,0:T(8,128)(2,1)S(1)}, bf16[272,512]{1,0:T(8,128)(2,1)S(1)}, u32[]{:S(2)}, u32[]{:S(2)}) collective-permute-start(bf16[272,512]{1,0:T(8,128)(2,1)S(1)} %get-tuple-element.62), channel_id=1, source_target_pairs={{0,4},{2,6},{4,0},{6,2},{8,12},{10,14},{12,8},{14,10},{1,5},{3,7},... | collective-permute-start | bytes 835592 | tf_op jit(solution)/shard_map/ppermute | solution.py:293
  57.7 7.8 %collective-permute-start.16 = (bf16[144,512]{1,0:T(8,128)(2,1)S(1)}, bf16[144,512]{1,0:T(8,128)(2,1)S(1)}, u32[]{:S(2)}, u32[]{:S(2)}) collective-permute-start(bf16[144,512]{1,0:T(8,128)(2,1)S(1)} %get-tuple-element.67), channel_id=1, source_target_pairs={{0,8},{2,10},{4,12},{6,14},{8,0},{10,2},{12,4},{14,6},{1,9},{3,11}... | collective-permute-start | bytes 442376 | tf_op jit(solution)/shard_map/ppermute | solution.py:293
  66.3 6.5 %collective-permute-start.17 = (bf16[144,512]{1,0:T(8,128)(2,1)S(1)}, bf16[144,512]{1,0:T(8,128)(2,1)S(1)}, u32[]{:S(2)}, u32[]{:S(2)}) collective-permute-start(bf16[144,512]{1,0:T(8,128)(2,1)S(1)} %get-tuple-element.71), channel_id=1, source_target_pairs={{0,8},{2,10},{4,12},{6,14},{8,0},{10,2},{12,4},{14,6},{1,9},{3,11}... | collective-permute-start | bytes 442376 | tf_op jit(solution)/shard_map/ppermute | solution.py:293
  72.8 1.2 %collective-permute-start.18 = (f32[1,128]{1,0:T(1,128)S(1)}, f32[1,128]{1,0:T(1,128)S(1)}, u32[]{:S(2)}, u32[]{:S(2)}) collective-permute-start(f32[1,128]{1,0:T(1,128)S(1)} %total_loss.1), channel_id=1, source_target_pairs={{0,1},{1,0},{2,3},{3,2},{4,5},{5,4},{6,7},{7,6},{8,9},{9,8},{10,11... | collective-permute-start | bytes 1544 | tf_op jit(solution)/shard_map/ppermute | solution.py:296

commit v4 on v2

--- a/solution.py
+++ b/solution.py
@@ -88,11 +88,14 @@
     return quantized - teacher_weight.astype(f32)
 
 
+early = 3
+
+
 def sort_features(hidden_states, blocks):
     tokens, features = hidden_states.shape
     width = features // (2 * blocks)
 
-    def kernel(h_ref, keep_ref, send_ref):
+    def kernel(h_ref, keep_ref, most_ref, rest_ref):
         index = lax.axis_index("fsdp")
         rank, half = index // 2, index % 2
         for k in range(blocks):
@@ -101,26 +104,34 @@
             start = pl.multiple_of((block + half) * width, width)
             keep_ref[:, where] = h_ref[:, pl.ds(start, width)]
             start = pl.multiple_of((block + 1 - half) * width, width)
-            send_ref[:, where] = h_ref[:, pl.ds(start, width)]
-
-    shape = pltpu.VMEM((tokens, features // 2), bf16)
-    return pl.pallas_call(
-        kernel, out_shape=(shape, shape), in_specs=vmem(1), out_specs=tuple(vmem(2)),
+            if k < early:
+                most_ref[:, where] = h_ref[:, pl.ds(start, width)]
+            else:
+                where = slice((k - early) * width, (k - early + 1) * width)
+                rest_ref[:, where] = h_ref[:, pl.ds(start, width)]
+
+    shapes = [pltpu.VMEM((tokens, n * width), bf16) for n in (blocks, early, blocks - early)]
+    return pl.pallas_call(
+        kernel, out_shape=tuple(shapes), in_specs=vmem(1), out_specs=tuple(vmem(3)),
         name="sort_features", compiler_params=params,
     )(*held(hidden_states))
 
 
-def row_starts(pieces):
-    starts = [0]
+def locate(pieces, width):
+    places, i = [], 0
     for piece in pieces:
-        starts.append(starts[-1] + piece.shape[0])
-    return starts
+        places.append([])
+        for array in piece:
+            places[-1] += [(i, at) for at in range(0, array.shape[1], width)]
+            i += 1
+    return places, [array for piece in pieces for array in piece]
 
 
 def partial_residual(pieces, highs, lows):
-    starts = row_starts(pieces)
+    tokens = pieces[0][0].shape[0]
     width, columns = highs[0].shape
-    n, m = len(pieces), len(highs)
+    places, flat = locate(pieces, width)
+    n, m = len(flat), len(highs)
 
     def kernel(*refs):
         h_refs, d_refs, (wide_ref, sent_ref) = refs[:n], refs[n : n + 2 * m], refs[n + 2 * m :]
@@ -128,24 +139,24 @@
             jnp.concatenate([high[...], low[...]], axis=1)
             for high, low in zip(d_refs[:m], d_refs[m:], strict=True)
         ]
-        for i, h_ref in enumerate(h_refs):
-            total = jnp.zeros((h_ref.shape[0], 2 * columns), f32)
-            for k, weight in enumerate(weights):
+        for i, place in enumerate(places):
+            total = jnp.zeros((tokens, 2 * columns), f32)
+            for (j, at), weight in zip(place, weights, strict=True):
                 total += jnp.dot(
-                    h_ref[:, k * width : (k + 1) * width], weight, preferred_element_type=f32
+                    h_refs[j][:, at : at + width], weight, preferred_element_type=f32
                 )
             total = (total[:, :columns] + total[:, columns:]) * 2.0**-15
-            rows = slice(starts[i], starts[i + 1])
+            rows = slice(i * tokens, (i + 1) * tokens)
             wide_ref[rows, :] = total
             sent_ref[rows, :] = total.astype(bf16)
 
-    shape = (starts[-1], columns)
+    shape = (len(pieces) * tokens, columns)
     return pl.pallas_call(
         kernel,
         out_shape=(pltpu.VMEM(shape, f32), pltpu.VMEM(shape, bf16)),
         in_specs=vmem(n + 2 * m), out_specs=tuple(vmem(2)), name="partial_residual",
         compiler_params=params,
-    )(*held(*pieces, *highs, *lows))
+    )(*held(*flat, *highs, *lows))
 
 
 def split_float(array):
@@ -174,13 +185,15 @@
 
 
 def partial_gradient(pieces, mine, theirs, loss, total_tokens, ride):
-    starts, features = row_starts(pieces), pieces[0].shape[1]
-    width, columns, n = features // 4, mine.shape[1], len(pieces)
+    tokens, features = pieces[0][0].shape
+    width, columns = features // 4, mine.shape[1]
+    places, flat = locate(pieces, width)
+    n = len(flat)
 
     def kernel(*refs):
         h_refs, mine_ref, theirs_ref, before_ref = refs[:n], *refs[n : n + 3]
         loss_ref, own_ref, far_ref, send_ref, *near_refs = refs[n + 3 :]
-        half = starts[-1] // 2
+        half = len(places) * tokens // 2
         top, bottom = mine_ref[:half, :], mine_ref[half:, :]
         their_bottom = theirs_ref[:half, :].astype(f32)
         their_top = theirs_ref[half:, :].astype(f32)
@@ -189,10 +202,11 @@
         grad_out = grad_out.astype(bf16)
         for k in (3, 1, 2, 0):
             total = jnp.zeros((columns, width), f32)
-            for i, h_ref in enumerate(h_refs):
+            for i, place in enumerate(places):
+                j, at = place[k]
                 total += lax.dot_general(
-                    grad_out[starts[i] : starts[i + 1], :],
-                    h_ref[:, k * width : (k + 1) * width],
+                    grad_out[i * tokens : (i + 1) * tokens, :],
+                    h_refs[j][:, at : at + width],
                     (((0,), (0,)), ((), ())), preferred_element_type=f32,
                 )
             if k == 3:
@@ -228,7 +242,7 @@
         ),
         in_specs=vmem(n + 3), out_specs=tuple(vmem(5 - ride)), name="partial_gradient",
         compiler_params=params,
-    )(*held(*pieces, mine, theirs, loss))
+    )(*held(*flat, mine, theirs, loss))
 
 
 def join_far(far, got, loss):
@@ -299,10 +313,10 @@
         return lax.optimization_barrier(values)
 
     column_max = jnp.max(jnp.abs(student_weight), axis=0, keepdims=True)
-    keep, send = sort_features(hidden_states, blocks)
+    keep, *sends = sort_features(hidden_states, blocks)
     column_max = jnp.maximum(column_max, flip(column_max, 1))
     keep, column_max = together(keep, column_max)
-    peer = flip(send, 1)
+    peers = [flip(send, 1) for send in sends]
     near_keep = swap_cores(keep)
     column_max = jnp.maximum(column_max, flip(column_max, 2))
     column_max = jnp.maximum(column_max, flip(column_max, 4))
@@ -311,9 +325,10 @@
 
     far = flip(coded, 4)
     near = flip(coded, 2)
-    far, near, peer, near_keep = together(far, near, peer, near_keep)
+    far, near, peers[0], near_keep = together(far, near, peers[0], near_keep)
     across = [flip(far[:, half], 2) for half in halves]
-    pieces = [keep, near_keep, peer, swap_cores(peer)]
+    peers[1], across[0] = together(peers[1], across[0])
+    pieces = [(keep,), (near_keep,), peers, [swap_cores(peer) for peer in peers]]
 
     def residual(c):
         parts = [p[:, halves[c]].astype(f32) for p in (difference, near, far)]
@@ -331,23 +346,23 @@
     )
     from_across = flip(to_across, 2)
     theirs_next, from_across = together(theirs_next, from_across)
-    loss_next, own_next, rest_next, to_across = partial_gradient(
-        pieces, mine_next, theirs_next, loss, total_tokens, True
+    loss_next, own_next, rest_next, to_across, to_near_next = partial_gradient(
+        pieces, mine_next, theirs_next, loss, total_tokens, False
     )
+    from_near = flip(to_near, 2)
+    from_across, from_near, to_across = together(from_across, from_near, to_across)
     from_across_next = flip(to_across, 2)
-    from_near = flip(to_near, 2)
     to_far, _ = join_far(rest, from_across, loss)
-    to_far, from_near = together(to_far, from_near)
     from_far = flip(to_far, 4)
     states = (student_weight, first_moment, second_moment)
-    from_across_next, from_far = together(from_across_next, from_far)
     news = apply_update(0, own, from_near, from_far, states)
     to_far, loss = join_far(rest_next, from_across_next, loss_next)
     from_far_next = flip(to_far, 4)
+    from_near_next = flip(to_near_next, 2)
     from_far_next, *news = together(from_far_next, *news)
     loss = total_loss(loss, from_far_next)
     loss = jnp.sum(loss + swap_cores(loss)).reshape(1) / total_tokens
-    news = apply_update(1, own_next, from_across_next, from_far_next, states, news)
+    news = apply_update(1, own_next, from_near_next, from_far_next, states, news)
     return (*news, loss)
 
 

time: 78.4 us -> 75.6 us (0.964)
  the two profiles are of different devices: /device:TPU:29 before, /device:TPU:0 now
where the time goes in v4:
time: 75.6 us; the launch traced here: 75.4 us
  waiting for transfers between devices  33 us (44%)
  starting transfers between devices  28.5 us (38%)
  Pallas kernels  7.12 us (9%)
  other arithmetic  2.56 us (3%)
  between operations  2.55 us (3%)
  local copies, waits for them, and re-layouts  1.66 us (2%)
    ppermute x17, waiting for transfers between devices, flip(): return lax.ppermute(array, 'fsdp', [(i, i ^ bit) for i in range(fsdp)])  33 us
    ppermute x17, starting transfers between devices, flip(): return lax.ppermute(array, 'fsdp', [(i, i ^ bit) for i in range(fsdp)])  28.4 us
    pallas_call x2, Pallas kernels, partial_residual(): pl.pallas_call(kernel, out_shape=(pltpu.VMEM(shape, f32), pltpu.VMEM(shap...  2.5 us
    pallas_call x2, Pallas kernels, apply_update(): pl.pallas_call(kernel, grid=(1,), out_shape=(shape,) * 3, in_specs=vmem(6...  2.3 us
    unnamed x10, local copies, waits for them, and re-layouts  1.61 us
    pallas_call x2, Pallas kernels, partial_gradient(): pl.pallas_call(kernel, out_shape=(pltpu.VMEM((1, columns), f32), pltpu.VM...  1.58 us
  transfers between devices with their start and end apart: 21, of which 15 were waited for; matrix products, arithmetic and copies ran while one was open for 1% of the time, Pallas kernels for 9%

profile of v4, /device:TPU:0, one launch (start us, length us, event | category | flops | bytes accessed | tf_op | source)
XLA Modules:
  0.0 75.4 jit_solution(10112420509613881573)
XLA Ops:
  0.6 0.0 copy-start
  0.6 1.1 %abs_reduce_fusion = f32[256]{0:T(256)S(1)} fusion(f32[512,256]{1,0:T(8,128)} %w_ref.3), kind=kLoop, calls=%fused_computation.19 | loop fusion | flops 261888 | bytes 525312 | tf_op jit(solution)/shard_map/reduce_max | solution.py:315
  1.8 3.0 %collective-permute-start = (f32[1,256]{1,0:T(1,128)S(1)}, f32[1,256]{1,0:T(1,128)S(1)}, u32[]{:S(2)}, u32[]{:S(2)}) collective-permute-start(f32[1,256]{1,0:T(1,128)S(1)} %bitcast.3), channel_id=1, source_target_pairs={{0,2},{2,0},{4,6},{6,4},{8,10},{10,8},{12,14},{14,12},{1,3},{3,1},... | collective-permute-start | bytes 3080 | tf_op jit(solution)/shard_map/ppermute | solution.py:307
  4.8 0.0 copy-start.1
  4.8 1.6 %copy-done.1 = bf16[256,4096]{1,0:T(8,128)(2,1)S(1)} copy-done((bf16[256,4096]{1,0:T(8,128)(2,1)S(1)}, bf16[256,4096]{1,0:T(8,128)(2,1)}, u32[]{:S(2)}) %copy-start.1) | copy-done | bytes 2097176
  6.4 0.0 copy-start.4
  6.4 0.2 sort_features.1
  6.5 0.0 collective-permute-done
  6.6 0.1 collective-permute-start.6
  6.6 1.7 %collective-permute-start.5 = (bf16[256,1536]{1,0:T(8,128)(2,1)S(1)}, bf16[256,1536]{1,0:T(8,128)(2,1)S(1)}, u32[]{:S(2)}, u32[]{:S(2)}) collective-permute-start(bf16[256,1536]{1,0:T(8,128)(2,1)S(1)} %get-tuple-element.50), channel_id=1, source_target_pairs={{0,2},{2,0},{4,6},{6,4},{8,10},{10,8},{12,14},{14,12},{1,3},{3,1},... | collective-permute-start | bytes 2359304 | tf_op jit(solution)/shard_map/ppermute | solution.py:307
  8.4 1.6 %collective-permute-start.1 = (f32[1,256]{1,0:T(1,128)S(1)}, f32[1,256]{1,0:T(1,128)S(1)}, u32[]{:S(2)}, u32[]{:S(2)}) collective-permute-start(f32[1,256]{1,0:T(1,128)S(1)} %max.9), channel_id=1, source_target_pairs={{0,4},{2,6},{4,0},{6,2},{8,12},{10,14},{12,8},{14,10},{1,5},{3,7},... | collective-permute-start | bytes 3080 | tf_op jit(solution)/shard_map/ppermute | solution.py:307
  9.9 2.0 %collective-permute-done.1 = f32[1,256]{1,0:T(1,128)S(1)} collective-permute-done((f32[1,256]{1,0:T(1,128)S(1)}, f32[1,256]{1,0:T(1,128)S(1)}, u32[]{:S(2)}, u32[]{:S(2)}) %collective-permute-start.1) | collective-permute-done | bytes 1056 | tf_op jit(solution)/shard_map/ppermute | solution.py:307
  11.9 2.6 %collective-permute-start.2 = (f32[1,256]{1,0:T(1,128)S(1)}, f32[1,256]{1,0:T(1,128)S(1)}, u32[]{:S(2)}, u32[]{:S(2)}) collective-permute-start(f32[1,256]{1,0:T(1,128)S(1)} %max.10), channel_id=1, source_target_pairs={{0,8},{2,10},{4,12},{6,14},{8,0},{10,2},{12,4},{14,6},{1,9},{3,11}... | collective-permute-start | bytes 3080 | tf_op jit(solution)/shard_map/ppermute | solution.py:307
  14.5 1.9 %collective-permute-done.2 = f32[1,256]{1,0:T(1,128)S(1)} collective-permute-done((f32[1,256]{1,0:T(1,128)S(1)}, f32[1,256]{1,0:T(1,128)S(1)}, u32[]{:S(2)}, u32[]{:S(2)}) %collective-permute-start.2) | collective-permute-done | bytes 1056 | tf_op jit(solution)/shard_map/ppermute | solution.py:307
  16.4 0.0 copy-done
  16.4 0.0 copy-done.4
  16.4 0.4 fusion.19
  16.9 2.7 %collective-permute-start.3 = (f16[512,256]{1,0:T(8,128)(2,1)S(1)}, f16[512,256]{1,0:T(8,128)(2,1)S(1)}, u32[]{:S(2)}, u32[]{:S(2)}) collective-permute-start(f16[512,256]{1,0:T(8,128)(2,1)S(1)} %get-tuple-element.90), channel_id=1, source_target_pairs={{0,8},{2,10},{4,12},{6,14},{8,0},{10,2},{12,4},{14,6},{1,9},{3,11}... | collective-permute-start | bytes 786440 | tf_op jit(solution)/shard_map/ppermute | solution.py:307
  19.5 1.6 %collective-permute-start.4 = (f16[512,256]{1,0:T(8,128)(2,1)S(1)}, f16[512,256]{1,0:T(8,128)(2,1)S(1)}, u32[]{:S(2)}, u32[]{:S(2)}) collective-permute-start(f16[512,256]{1,0:T(8,128)(2,1)S(1)} %get-tuple-element.90), channel_id=1, source_target_pairs={{0,4},{2,6},{4,0},{6,2},{8,12},{10,14},{12,8},{14,10},{1,5},{3,7},... | collective-permute-start | bytes 786440 | tf_op jit(solution)/shard_map/ppermute | solution.py:307
  21.1 0.5 collective-permute-start.7
  21.6 8.4 %collective-permute-done.3 = f16[512,256]{1,0:T(8,128)(2,1)S(1)} collective-permute-done((f16[512,256]{1,0:T(8,128)(2,1)S(1)}, f16[512,256]{1,0:T(8,128)(2,1)S(1)}, u32[]{:S(2)}, u32[]{:S(2)}) %collective-permute-start.3) | collective-permute-done | bytes 262176 | tf_op jit(solution)/shard_map/ppermute | solution.py:307
  30.0 0.2 collective-permute-done.4
  30.2 0.0 collective-permute-done.5.refs_2_
  30.2 0.0 collective-permute-done.6.refs_1_
  30.2 0.0 collective-permute-start.9
  30.2 0.1 fusion.21
  30.3 1.5 %collective-permute-start.8 = (f16[512,128]{1,0:T(8,128)(2,1)S(1)}, f16[512,128]{1,0:T(8,128)(2,1)S(1)}, u32[]{:S(2)}, u32[]{:S(2)}) collective-permute-start(f16[512,128]{1,0:T(8,128)(2,1)S(1)} %get-tuple-element.105), channel_id=1, source_target_pairs={{0,4},{2,6},{4,0},{6,2},{8,12},{10,14},{12,8},{14,10},{1,5},{3,7},... | collective-permute-start | bytes 393224 | tf_op jit(solution)/shard_map/ppermute | solution.py:307
  31.8 0.1 fusion.15
  31.8 0.4 collective-permute-done.7.refs_3_
  32.2 4.0 %collective-permute-done.8 = f16[512,128]{1,0:T(8,128)(2,1)S(1)} collective-permute-done((f16[512,128]{1,0:T(8,128)(2,1)S(1)}, f16[512,128]{1,0:T(8,128)(2,1)S(1)}, u32[]{:S(2)}, u32[]{:S(2)}) %collective-permute-start.8) | collective-permute-done | bytes 131104 | tf_op jit(solution)/shard_map/ppermute | solution.py:307
  36.2 0.0 collective-permute-start.10
  36.2 0.2 fusion.16
  36.4 1.5 %collective-permute-start.11 = (f16[512,128]{1,0:T(8,128)(2,1)S(1)}, f16[512,128]{1,0:T(8,128)(2,1)S(1)}, u32[]{:S(2)}, u32[]{:S(2)}) collective-permute-start(f16[512,128]{1,0:T(8,128)(2,1)S(1)} %get-tuple-element.104), channel_id=1, source_target_pairs={{0,4},{2,6},{4,0},{6,2},{8,12},{10,14},{12,8},{14,10},{1,5},{3,7},... | collective-permute-start | bytes 393224 | tf_op jit(solution)/shard_map/ppermute | solution.py:307
  38.0 0.0 collective-permute-done.10.refs_5_
  38.0 0.0 collective-permute-done.9.refs_4_
  38.0 1.2 %partial_residual.3 = (f32[1024,128]{1,0:T(8,128)S(1)}, bf16[1024,128]{1,0:T(8,128)(2,1)S(1)}) custom-call(bf16[256,2048]{1,0:T(8,128)(2,1)S(1)} %get-tuple-element.48.refs_0_, bf16[256,2048]{1,0:T(8,128)(2,1)S(1)} %collective-permute-done.6.refs_1_, bf16[256,1536]{1,0:T(8,128)(2,1)S(1)} %collective-permute-done.5.refs_2_, ...), custom_call_target="tpu_custom_call" | custom-call | tf_op jit(solution)/shard_map/partial_residual/pallas_call | solution.py:154
  39.2 0.3 collective-permute-start.13
  39.5 2.8 %collective-permute-done.11 = f16[512,128]{1,0:T(8,128)(2,1)S(1)} collective-permute-done((f16[512,128]{1,0:T(8,128)(2,1)S(1)}, f16[512,128]{1,0:T(8,128)(2,1)S(1)}, u32[]{:S(2)}, u32[]{:S(2)}) %collective-permute-start.11) | collective-permute-done | bytes 131104 | tf_op jit(solution)/shard_map/ppermute | solution.py:307
  42.4 1.2 %partial_residual.2 = (f32[1024,128]{1,0:T(8,128)S(1)}, bf16[1024,128]{1,0:T(8,128)(2,1)S(1)}) custom-call(bf16[256,2048]{1,0:T(8,128)(2,1)S(1)} %get-tuple-element.48.refs_0_, bf16[256,2048]{1,0:T(8,128)(2,1)S(1)} %collective-permute-done.6.refs_1_, bf16[256,1536]{1,0:T(8,128)(2,1)S(1)} %collective-permute-done.5.refs_2_, ...), custom_call_target="tpu_custom_call" | custom-call | tf_op jit(solution)/shard_map/partial_residual/pallas_call | solution.py:154
  43.7 0.3 collective-permute-start.12
  43.9 4.5 %collective-permute-done.13.refs_7_ = bf16[1024,128]{1,0:T(8,128)(2,1)S(1)} collective-permute-done((bf16[1024,128]{1,0:T(8,128)(2,1)S(1)}, bf16[1024,128]{1,0:T(8,128)(2,1)S(1)}, u32[]{:S(2)}, u32[]{:S(2)}) %collective-permute-start.13) | collective-permute-done | bytes 262176 | tf_op jit(solution)/shard_map/ppermute | solution.py:307
  48.4 0.8 %partial_gradient.2 = (f32[1,128]{1,0:T(1,128)S(1)}, f32[128,512]{1,0:T(8,128)S(1)}, f32[128,512]{1,0:T(8,128)S(1)}, bf16[144,512]{1,0:T(8,128)(2,1)S(1)}, bf16[128,512]{1,0:T(8,128)(2,1)S(1)}) custom-call(bf16[256,2048]{1,0:T(8,128)(2,1)S(1)} %get-tuple-element.48.refs_0_, bf16[256,2048]{1,0:T(8,128)(2,1)S(1)} %collective-permute-done.6.refs_1_, ...), custom_call_target="tpu_custom_call" | custom-call | tf_op jit(solution)/shard_map/partial_gradient/pallas_call | solution.py:236
  49.2 1.3 %collective-permute-start.14 = (bf16[144,512]{1,0:T(8,128)(2,1)S(1)}, bf16[144,512]{1,0:T(8,128)(2,1)S(1)}, u32[]{:S(2)}, u32[]{:S(2)}) collective-permute-start(bf16[144,512]{1,0:T(8,128)(2,1)S(1)} %get-tuple-element.62), channel_id=1, source_target_pairs={{0,4},{2,6},{4,0},{6,2},{8,12},{10,14},{12,8},{14,10},{1,5},{3,7},... | collective-permute-start | bytes 442376 | tf_op jit(solution)/shard_map/ppermute | solution.py:307
  50.5 0.8 %collective-permute-start.16 = (bf16[128,512]{1,0:T(8,128)(2,1)S(1)}, bf16[128,512]{1,0:T(8,128)(2,1)S(1)}, u32[]{:S(2)}, u32[]{:S(2)}) collective-permute-start(bf16[128,512]{1,0:T(8,128)(2,1)S(1)} %get-tuple-element.69), channel_id=1, source_target_pairs={{0,4},{2,6},{4,0},{6,2},{8,12},{10,14},{12,8},{14,10},{1,5},{3,7},... | collective-permute-start | bytes 393224 | tf_op jit(solution)/shard_map/ppermute | solution.py:307
  51.3 2.0 %collective-permute-done.12.refs_7_ = bf16[1024,128]{1,0:T(8,128)(2,1)S(1)} collective-permute-done((bf16[1024,128]{1,0:T(8,128)(2,1)S(1)}, bf16[1024,128]{1,0:T(8,128)(2,1)S(1)}, u32[]{:S(2)}, u32[]{:S(2)}) %collective-permute-start.12) | collective-permute-done | bytes 262176 | tf_op jit(solution)/shard_map/ppermute | solution.py:307
  53.3 1.8 %collective-permute-done.14.got_ref = bf16[144,512]{1,0:T(8,128)(2,1)S(1)} collective-permute-done((bf16[144,512]{1,0:T(8,128)(2,1)S(1)}, bf16[144,512]{1,0:T(8,128)(2,1)S(1)}, u32[]{:S(2)}, u32[]{:S(2)}) %collective-permute-start.14) | collective-permute-done | bytes 147488 | tf_op jit(solution)/shard_map/ppermute | solution.py:307
  55.2 0.8 %partial_gradient.3 = (f32[1,128]{1,0:T(1,128)S(1)}, f32[128,512]{1,0:T(8,128)S(1)}, f32[128,512]{1,0:T(8,128)S(1)}, bf16[144,512]{1,0:T(8,128)(2,1)S(1)}, bf16[128,512]{1,0:T(8,128)(2,1)S(1)}) custom-call(bf16[256,2048]{1,0:T(8,128)(2,1)S(1)} %get-tuple-element.48.refs_0_, bf16[256,2048]{1,0:T(8,128)(2,1)S(1)} %collective-permute-done.6.refs_1_, ...), custom_call_target="tpu_custom_call" | custom-call | tf_op jit(solution)/shard_map/partial_gradient/pallas_call | solution.py:236
  56.0 0.6 collective-permute-done.16.near_ref
  56.6 1.0 %collective-permute-start.17 = (bf16[144,512]{1,0:T(8,128)(2,1)S(1)}, bf16[144,512]{1,0:T(8,128)(2,1)S(1)}, u32[]{:S(2)}, u32[]{:S(2)}) collective-permute-start(bf16[144,512]{1,0:T(8,128)(2,1)S(1)} %get-tuple-element.71), channel_id=1, source_target_pairs={{0,4},{2,6},{4,0},{6,2},{8,12},{10,14},{12,8},{14,10},{1,5},{3,7},... | collective-permute-start | bytes 442376 | tf_op jit(solution)/shard_map/ppermute | solution.py:307
  57.6 0.5 join_far.3
  58.1 2.4 %collective-permute-start.19 = (bf16[144,512]{1,0:T(8,128)(2,1)S(1)}, bf16[144,512]{1,0:T(8,128)(2,1)S(1)}, u32[]{:S(2)}, u32[]{:S(2)}) collective-permute-start(bf16[144,512]{1,0:T(8,128)(2,1)S(1)} %get-tuple-element.78), channel_id=1, source_target_pairs={{0,8},{2,10},{4,12},{6,14},{8,0},{10,2},{12,4},{14,6},{1,9},{3,11}... | collective-permute-start | bytes 442376 | tf_op jit(solution)/shard_map/ppermute | solution.py:307
  60.5 1.5 %collective-permute-done.17.got_ref = bf16[144,512]{1,0:T(8,128)(2,1)S(1)} collective-permute-done((bf16[144,512]{1,0:T(8,128)(2,1)S(1)}, bf16[144,512]{1,0:T(8,128)(2,1)S(1)}, u32[]{:S(2)}, u32[]{:S(2)}) %collective-permute-start.17) | collective-permute-done | bytes 147488 | tf_op jit(solution)/shard_map/ppermute | solution.py:307
  62.1 3.5 %collective-permute-start.18 = (bf16[144,512]{1,0:T(8,128)(2,1)S(1)}, bf16[144,512]{1,0:T(8,128)(2,1)S(1)}, u32[]{:S(2)}, u32[]{:S(2)}) collective-permute-start(bf16[144,512]{1,0:T(8,128)(2,1)S(1)} %get-tuple-element.73), channel_id=1, source_target_pairs={{0,8},{2,10},{4,12},{6,14},{8,0},{10,2},{12,4},{14,6},{1,9},{3,11}... | collective-permute-start | bytes 442376 | tf_op jit(solution)/shard_map/ppermute | solution.py:307
  65.7 2.2 %collective-permute-start.15 = (bf16[128,512]{1,0:T(8,128)(2,1)S(1)}, bf16[128,512]{1,0:T(8,128)(2,1)S(1)}, u32[]{:S(2)}, u32[]{:S(2)}) collective-permute-start(bf16[128,512]{1,0:T(8,128)(2,1)S(1)} %get-tuple-element.66), channel_id=1, source_target_pairs={{0,4},{2,6},{4,0},{6,2},{8,12},{10,14},{12,8},{14,10},{1,5},{3,7},... | collective-permute-start | bytes 393224 | tf_op jit(solution)/shard_map/ppermute | solution.py:307
  67.8 0.6 collective-permute-done.19.far_ref
  68.4 0.0 copy-done.2
  68.4 0.0 copy-done.3
  68.4 1.2 %apply_update.2 = (f32[512,256]{1,0:T(8,128)}, f32[512,256]{1,0:T(8,128)}, f32[512,256]{1,0:T(8,128)}) custom-call(f32[128,512]{1,0:T(8,128)S(1)} %get-tuple-element.74.own_ref, bf16[128,512]{1,0:T(8,128)(2,1)S(1)} %collective-permute-done.16.near_ref, bf16[144,512]{1,0:T(8,128)(2,1)S(1)} %collective-permute-done.19.far_ref, f32[512,256]{1,0:T(8,128)S(1)} %copy-done, ...), custom_call_target="tpu_custom_call" | custom-call | tf_op jit(solution)/shard_map/apply_update/pallas_call | solution.py:291
  69.6 2.1 %collective-permute-done.18.far_ref.got_ref = bf16[144,512]{1,0:T(8,128)(2,1)S(1)} collective-permute-done((bf16[144,512]{1,0:T(8,128)(2,1)S(1)}, bf16[144,512]{1,0:T(8,128)(2,1)S(1)}, u32[]{:S(2)}, u32[]{:S(2)}) %collective-permute-start.18) | collective-permute-done | bytes 147488 | tf_op jit(solution)/shard_map/ppermute | solution.py:307
  71.7 0.0 collective-permute-start.20
  71.7 0.2 collective-permute-done.15.near_ref
  71.8 1.1 %apply_update.3 = (f32[512,256]{1,0:T(8,128)}, f32[512,256]{1,0:T(8,128)}, f32[512,256]{1,0:T(8,128)}) custom-call(f32[128,512]{1,0:T(8,128)S(1)} %get-tuple-element.65.own_ref, bf16[128,512]{1,0:T(8,128)(2,1)S(1)} %collective-permute-done.15.near_ref, ...), custom_call_target="tpu_custom_call", output_to_operand_aliasing={{0}: (6, {}), {1}: (7, {}), {2}: (8, {})} | custom-call | tf_op jit(solution)/shard_map/apply_update/pallas_call | solution.py:291
  73.0 0.0 collective-permute-done.20
  73.0 0.6 add_reduce_fusion
  (10 shorter events, 0.2 us)
Async XLA Ops:
  0.6 15.8 %copy-start = (f32[512,256]{1,0:T(8,128)S(1)}, f32[512,256]{1,0:T(8,128)}, u32[]{:S(2)}) copy-start(f32[512,256]{1,0:T(8,128)} %w_ref.3) | copy-start | bytes 1572868
  1.8 4.8 %collective-permute-start = (f32[1,256]{1,0:T(1,128)S(1)}, f32[1,256]{1,0:T(1,128)S(1)}, u32[]{:S(2)}, u32[]{:S(2)}) collective-permute-start(f32[1,256]{1,0:T(1,128)S(1)} %bitcast.3), channel_id=1, source_target_pairs={{0,2},{2,0},{4,6},{6,4},{8,10},{10,8},{12,14},{14,12},{1,3},{3,1},... | collective-permute-start | bytes 3080 | tf_op jit(solution)/shard_map/ppermute | solution.py:307
  4.8 1.6 %copy-start.1 = (bf16[256,4096]{1,0:T(8,128)(2,1)S(1)}, bf16[256,4096]{1,0:T(8,128)(2,1)}, u32[]{:S(2)}) copy-start(bf16[256,4096]{1,0:T(8,128)(2,1)} %h_ref.1) | copy-start | bytes 6291460
  6.4 10.0 %copy-start.4 = (bf16[512,256]{1,0:T(8,128)(2,1)S(1)}, bf16[512,256]{1,0:T(8,128)(2,1)}, u32[]{:S(2)}) copy-start(bf16[512,256]{1,0:T(8,128)(2,1)} %param.6) | copy-start | bytes 786436
  6.6 23.6 %collective-permute-start.6 = (bf16[256,2048]{1,0:T(8,128)(2,1)S(1)}, bf16[256,2048]{1,0:T(8,128)(2,1)S(1)}, u32[]{:S(2)}, u32[]{:S(2)}) collective-permute-start(bf16[256,2048]{1,0:T(8,128)(2,1)S(1)} %get-tuple-element.48.refs_0_), channel_id=1, source_target_pairs={{0,1},{1,0},{2,3},{3,2},{4,5},{5,4},{6,7},{7,6},{8,9},{9,8},{10,11... | collective-permute-start | bytes 3145736 | tf_op jit(solution)/shard_map/ppermute | solution.py:310
  6.6 23.5 %collective-permute-start.5 = (bf16[256,1536]{1,0:T(8,128)(2,1)S(1)}, bf16[256,1536]{1,0:T(8,128)(2,1)S(1)}, u32[]{:S(2)}, u32[]{:S(2)}) collective-permute-start(bf16[256,1536]{1,0:T(8,128)(2,1)S(1)} %get-tuple-element.50), channel_id=1, source_target_pairs={{0,2},{2,0},{4,6},{6,4},{8,10},{10,8},{12,14},{14,12},{1,3},{3,1},... | collective-permute-start | bytes 2359304 | tf_op jit(solution)/shard_map/ppermute | solution.py:307
  8.4 3.6 %collective-permute-start.1 = (f32[1,256]{1,0:T(1,128)S(1)}, f32[1,256]{1,0:T(1,128)S(1)}, u32[]{:S(2)}, u32[]{:S(2)}) collective-permute-start(f32[1,256]{1,0:T(1,128)S(1)} %max.9), channel_id=1, source_target_pairs={{0,4},{2,6},{4,0},{6,2},{8,12},{10,14},{12,8},{14,10},{1,5},{3,7},... | collective-permute-start | bytes 3080 | tf_op jit(solution)/shard_map/ppermute | solution.py:307
  11.9 4.5 %collective-permute-start.2 = (f32[1,256]{1,0:T(1,128)S(1)}, f32[1,256]{1,0:T(1,128)S(1)}, u32[]{:S(2)}, u32[]{:S(2)}) collective-permute-start(f32[1,256]{1,0:T(1,128)S(1)} %max.10), channel_id=1, source_target_pairs={{0,8},{2,10},{4,12},{6,14},{8,0},{10,2},{12,4},{14,6},{1,9},{3,11}... | collective-permute-start | bytes 3080 | tf_op jit(solution)/shard_map/ppermute | solution.py:307
  16.9 13.1 %collective-permute-start.3 = (f16[512,256]{1,0:T(8,128)(2,1)S(1)}, f16[512,256]{1,0:T(8,128)(2,1)S(1)}, u32[]{:S(2)}, u32[]{:S(2)}) collective-permute-start(f16[512,256]{1,0:T(8,128)(2,1)S(1)} %get-tuple-element.90), channel_id=1, source_target_pairs={{0,8},{2,10},{4,12},{6,14},{8,0},{10,2},{12,4},{14,6},{1,9},{3,11}... | collective-permute-start | bytes 786440 | tf_op jit(solution)/shard_map/ppermute | solution.py:307
  19.5 10.7 %collective-permute-start.4 = (f16[512,256]{1,0:T(8,128)(2,1)S(1)}, f16[512,256]{1,0:T(8,128)(2,1)S(1)}, u32[]{:S(2)}, u32[]{:S(2)}) collective-permute-start(f16[512,256]{1,0:T(8,128)(2,1)S(1)} %get-tuple-element.90), channel_id=1, source_target_pairs={{0,4},{2,6},{4,0},{6,2},{8,12},{10,14},{12,8},{14,10},{1,5},{3,7},... | collective-permute-start | bytes 786440 | tf_op jit(solution)/shard_map/ppermute | solution.py:307
  21.1 11.1 %collective-permute-start.7 = (bf16[256,512]{1,0:T(8,128)(2,1)S(1)}, bf16[256,512]{1,0:T(8,128)(2,1)S(1)}, u32[]{:S(2)}, u32[]{:S(2)}) collective-permute-start(bf16[256,512]{1,0:T(8,128)(2,1)S(1)} %get-tuple-element.53), channel_id=1, source_target_pairs={{0,2},{2,0},{4,6},{6,4},{8,10},{10,8},{12,14},{14,12},{1,3},{3,1},... | collective-permute-start | bytes 786440 | tf_op jit(solution)/shard_map/ppermute | solution.py:307
  30.2 7.8 %collective-permute-start.9 = (bf16[256,1536]{1,0:T(8,128)(2,1)S(1)}, bf16[256,1536]{1,0:T(8,128)(2,1)S(1)}, u32[]{:S(2)}, u32[]{:S(2)}) collective-permute-start(bf16[256,1536]{1,0:T(8,128)(2,1)S(1)} %collective-permute-done.5.refs_2_), channel_id=1, source_target_pairs={{0,1},{1,0},{2,3},{3,2},{4,5},{5,4},{6,7},{7,6},{8,9},{9,8},{10,11... | collective-permute-start | bytes 2359304 | tf_op jit(solution)/shard_map/ppermute | solution.py:310
  30.3 6.0 %collective-permute-start.8 = (f16[512,128]{1,0:T(8,128)(2,1)S(1)}, f16[512,128]{1,0:T(8,128)(2,1)S(1)}, u32[]{:S(2)}, u32[]{:S(2)}) collective-permute-start(f16[512,128]{1,0:T(8,128)(2,1)S(1)} %get-tuple-element.105), channel_id=1, source_target_pairs={{0,4},{2,6},{4,0},{6,2},{8,12},{10,14},{12,8},{14,10},{1,5},{3,7},... | collective-permute-start | bytes 393224 | tf_op jit(solution)/shard_map/ppermute | solution.py:307
  36.2 1.7 %collective-permute-start.10 = (bf16[256,512]{1,0:T(8,128)(2,1)S(1)}, bf16[256,512]{1,0:T(8,128)(2,1)S(1)}, u32[]{:S(2)}, u32[]{:S(2)}) collective-permute-start(bf16[256,512]{1,0:T(8,128)(2,1)S(1)} %collective-permute-done.7.refs_3_), channel_id=1, source_target_pairs={{0,1},{1,0},{2,3},{3,2},{4,5},{5,4},{6,7},{7,6},{8,9},{9,8},{10,11... | collective-permute-start | bytes 786440 | tf_op jit(solution)/shard_map/ppermute | solution.py:310
  36.4 6.0 %collective-permute-start.11 = (f16[512,128]{1,0:T(8,128)(2,1)S(1)}, f16[512,128]{1,0:T(8,128)(2,1)S(1)}, u32[]{:S(2)}, u32[]{:S(2)}) collective-permute-start(f16[512,128]{1,0:T(8,128)(2,1)S(1)} %get-tuple-element.104), channel_id=1, source_target_pairs={{0,4},{2,6},{4,0},{6,2},{8,12},{10,14},{12,8},{14,10},{1,5},{3,7},... | collective-permute-start | bytes 393224 | tf_op jit(solution)/shard_map/ppermute | solution.py:307
  39.2 9.2 %collective-permute-start.13 = (bf16[1024,128]{1,0:T(8,128)(2,1)S(1)}, bf16[1024,128]{1,0:T(8,128)(2,1)S(1)}, u32[]{:S(2)}, u32[]{:S(2)}) collective-permute-start(bf16[1024,128]{1,0:T(8,128)(2,1)S(1)} %get-tuple-element.61), channel_id=1, source_target_pairs={{0,2},{2,0},{4,6},{6,4},{8,10},{10,8},{12,14},{14,12},{1,3},{3,1},... | collective-permute-start | bytes 786440 | tf_op jit(solution)/shard_map/ppermute | solution.py:307
  43.7 9.7 %collective-permute-start.12 = (bf16[1024,128]{1,0:T(8,128)(2,1)S(1)}, bf16[1024,128]{1,0:T(8,128)(2,1)S(1)}, u32[]{:S(2)}, u32[]{:S(2)}) collective-permute-start(bf16[1024,128]{1,0:T(8,128)(2,1)S(1)} %get-tuple-element.58), channel_id=1, source_target_pairs={{0,2},{2,0},{4,6},{6,4},{8,10},{10,8},{12,14},{14,12},{1,3},{3,1},... | collective-permute-start | bytes 786440 | tf_op jit(solution)/shard_map/ppermute | solution.py:307
  49.2 5.9 %collective-permute-start.14 = (bf16[144,512]{1,0:T(8,128)(2,1)S(1)}, bf16[144,512]{1,0:T(8,128)(2,1)S(1)}, u32[]{:S(2)}, u32[]{:S(2)}) collective-permute-start(bf16[144,512]{1,0:T(8,128)(2,1)S(1)} %get-tuple-element.62), channel_id=1, source_target_pairs={{0,4},{2,6},{4,0},{6,2},{8,12},{10,14},{12,8},{14,10},{1,5},{3,7},... | collective-permute-start | bytes 442376 | tf_op jit(solution)/shard_map/ppermute | solution.py:307
  50.5 6.0 %collective-permute-start.16 = (bf16[128,512]{1,0:T(8,128)(2,1)S(1)}, bf16[128,512]{1,0:T(8,128)(2,1)S(1)}, u32[]{:S(2)}, u32[]{:S(2)}) collective-permute-start(bf16[128,512]{1,0:T(8,128)(2,1)S(1)} %get-tuple-element.69), channel_id=1, source_target_pairs={{0,4},{2,6},{4,0},{6,2},{8,12},{10,14},{12,8},{14,10},{1,5},{3,7},... | collective-permute-start | bytes 393224 | tf_op jit(solution)/shard_map/ppermute | solution.py:307
  55.2 13.2 %copy-start.2 = (f32[512,256]{1,0:T(8,128)S(1)}, f32[512,256]{1,0:T(8,128)}, u32[]{:S(2)}) copy-start(f32[512,256]{1,0:T(8,128)} %m_ref.3) | copy-start | bytes 1572868
  55.2 13.3 %copy-start.3 = (f32[512,256]{1,0:T(8,128)S(1)}, f32[512,256]{1,0:T(8,128)}, u32[]{:S(2)}) copy-start(f32[512,256]{1,0:T(8,128)} %v_ref.3) | copy-start | bytes 1572868
  56.6 5.5 %collective-permute-start.17 = (bf16[144,512]{1,0:T(8,128)(2,1)S(1)}, bf16[144,512]{1,0:T(8,128)(2,1)S(1)}, u32[]{:S(2)}, u32[]{:S(2)}) collective-permute-start(bf16[144,512]{1,0:T(8,128)(2,1)S(1)} %get-tuple-element.71), channel_id=1, source_target_pairs={{0,4},{2,6},{4,0},{6,2},{8,12},{10,14},{12,8},{14,10},{1,5},{3,7},... | collective-permute-start | bytes 442376 | tf_op jit(solution)/shard_map/ppermute | solution.py:307
  58.1 10.3 %collective-permute-start.19 = (bf16[144,512]{1,0:T(8,128)(2,1)S(1)}, bf16[144,512]{1,0:T(8,128)(2,1)S(1)}, u32[]{:S(2)}, u32[]{:S(2)}) collective-permute-start(bf16[144,512]{1,0:T(8,128)(2,1)S(1)} %get-tuple-element.78), channel_id=1, source_target_pairs={{0,8},{2,10},{4,12},{6,14},{8,0},{10,2},{12,4},{14,6},{1,9},{3,11}... | collective-permute-start | bytes 442376 | tf_op jit(solution)/shard_map/ppermute | solution.py:307
  62.1 9.6 %collective-permute-start.18 = (bf16[144,512]{1,0:T(8,128)(2,1)S(1)}, bf16[144,512]{1,0:T(8,128)(2,1)S(1)}, u32[]{:S(2)}, u32[]{:S(2)}) collective-permute-start(bf16[144,512]{1,0:T(8,128)(2,1)S(1)} %get-tuple-element.73), channel_id=1, source_target_pairs={{0,8},{2,10},{4,12},{6,14},{8,0},{10,2},{12,4},{14,6},{1,9},{3,11}... | collective-permute-start | bytes 442376 | tf_op jit(solution)/shard_map/ppermute | solution.py:307
  65.7 6.2 %collective-permute-start.15 = (bf16[128,512]{1,0:T(8,128)(2,1)S(1)}, bf16[128,512]{1,0:T(8,128)(2,1)S(1)}, u32[]{:S(2)}, u32[]{:S(2)}) collective-permute-start(bf16[128,512]{1,0:T(8,128)(2,1)S(1)} %get-tuple-element.66), channel_id=1, source_target_pairs={{0,4},{2,6},{4,0},{6,2},{8,12},{10,14},{12,8},{14,10},{1,5},{3,7},... | collective-permute-start | bytes 393224 | tf_op jit(solution)/shard_map/ppermute | solution.py:307
  71.7 1.3 %collective-permute-start.20 = (f32[1,128]{1,0:T(1,128)S(1)}, f32[1,128]{1,0:T(1,128)S(1)}, u32[]{:S(2)}, u32[]{:S(2)}) collective-permute-start(f32[1,128]{1,0:T(1,128)S(1)} %total_loss.1), channel_id=1, source_target_pairs={{0,1},{1,0},{2,3},{3,2},{4,5},{5,4},{6,7},{7,6},{8,9},{9,8},{10,11... | collective-permute-start | bytes 1544 | tf_op jit(solution)/shard_map/ppermute | solution.py:310

commit v5 on v4

--- a/solution.py
+++ b/solution.py
@@ -167,7 +167,7 @@
     return rows
 
 
-note_rows = 16
+note_rows = 8
 
 
 def write_note(ref, start, row):
@@ -184,7 +184,7 @@
     return note[0:1, :] + note[1:2, :] + note[2:3, :]
 
 
-def partial_gradient(pieces, mine, theirs, loss, total_tokens, ride):
+def partial_gradient(pieces, mine, theirs, loss, total_tokens, noted):
     tokens, features = pieces[0][0].shape
     width, columns = features // 4, mine.shape[1]
     places, flat = locate(pieces, width)
@@ -192,7 +192,7 @@
 
     def kernel(*refs):
         h_refs, mine_ref, theirs_ref, before_ref = refs[:n], *refs[n : n + 3]
-        loss_ref, own_ref, far_ref, send_ref, *near_refs = refs[n + 3 :]
+        loss_ref, own_ref, far_ref, send_ref, near_ref = refs[n + 3 :]
         half = len(places) * tokens // 2
         top, bottom = mine_ref[:half, :], mine_ref[half:, :]
         their_bottom = theirs_ref[:half, :].astype(f32)
@@ -212,11 +212,7 @@
             if k == 3:
                 send_ref[:columns, :] = total.astype(bf16)
             elif k == 1:
-                near = total.astype(bf16)
-                if ride:
-                    send_ref[columns + note_rows :, :] = near
-                else:
-                    near_refs[0][...] = near
+                near_ref[...] = total.astype(bf16)
             elif k == 2:
                 far_ref[...] = total
             else:
@@ -230,17 +226,17 @@
         ]
         total = before_ref[...] + (squares[0] + squares[1])
         loss_ref[...] = total
-        write_note(send_ref, columns, total)
+        if noted:
+            write_note(send_ref, columns, total)
 
     shape = (columns, width)
     return pl.pallas_call(
         kernel,
         out_shape=(
             pltpu.VMEM((1, columns), f32), pltpu.VMEM(shape, f32), pltpu.VMEM(shape, f32),
-            pltpu.VMEM((columns * (1 + ride) + note_rows, width), bf16),
-            *[pltpu.VMEM(shape, bf16)] * (1 - ride),
+            pltpu.VMEM((columns + note_rows * noted, width), bf16), pltpu.VMEM(shape, bf16),
         ),
-        in_specs=vmem(n + 3), out_specs=tuple(vmem(5 - ride)), name="partial_gradient",
+        in_specs=vmem(n + 3), out_specs=tuple(vmem(5)), name="partial_gradient",
         compiler_params=params,
     )(*held(*flat, mine, theirs, loss))
 
@@ -251,7 +247,9 @@
     def kernel(far_ref, got_ref, loss_ref, send_ref, sum_ref):
         total = far_ref[...] + got_ref[:columns, :].astype(f32)
         send_ref[:columns, :] = total.astype(bf16)
-        both = loss_ref[...] + read_note(got_ref, columns, columns)
+        both = loss_ref[...]
+        if got_ref.shape[0] > columns:
+            both += read_note(got_ref, columns, columns)
         sum_ref[...] = both
         write_note(send_ref, columns, both)
 
@@ -347,7 +345,7 @@
     from_across = flip(to_across, 2)
     theirs_next, from_across = together(theirs_next, from_across)
     loss_next, own_next, rest_next, to_across, to_near_next = partial_gradient(
-        pieces, mine_next, theirs_next, loss, total_tokens, False
+        pieces, mine_next, theirs_next, loss, total_tokens, True
     )
     from_near = flip(to_near, 2)
     from_across, from_near, to_across = together(from_across, from_near, to_across)

time: 75.6 us -> 74.6 us (0.987)
  waiting for transfers between devices: 33 us -> 32.1 us
    ppermute x17, waiting for transfers between devices: 33 us -> 32.1 us  [flip(): return lax.ppermute(array, 'fsdp', [(i, i ^ bit) for i in range(fsdp)])]
  transfers between devices with their start and end apart: 21 -> 21, of which waited for: 15 -> 15; matrix products, arithmetic and copies ran while one was open for 1% -> 1% of each run, Pallas kernels for 9% -> 10%
where the time goes in v5:
time: 74.6 us; the launch traced here: 74.4 us
  waiting for transfers between devices  32.1 us (43%)
  starting transfers between devices  28.5 us (38%)
  Pallas kernels  7.07 us (9%)
  other arithmetic  2.56 us (3%)
  between operations  2.55 us (3%)
  local copies, waits for them, and re-layouts  1.66 us (2%)
    ppermute x17, waiting for transfers between devices, flip(): return lax.ppermute(array, 'fsdp', [(i, i ^ bit) for i in range(fsdp)])  32.1 us
    ppermute x17, starting transfers between devices, flip(): return lax.ppermute(array, 'fsdp', [(i, i ^ bit) for i in range(fsdp)])  28.4 us
    pallas_call x2, Pallas kernels, partial_residual(): pl.pallas_call(kernel, out_shape=(pltpu.VMEM(shape, f32), pltpu.VMEM(shap...  2.5 us
    pallas_call x2, Pallas kernels, apply_update(): pl.pallas_call(kernel, grid=(1,), out_shape=(shape,) * 3, in_specs=vmem(6...  2.3 us
    unnamed x10, local copies, waits for them, and re-layouts  1.61 us
    pallas_call x2, Pallas kernels, partial_gradient(): pl.pallas_call(kernel, out_shape=(pltpu.VMEM((1, columns), f32), pltpu.VM...  1.54 us
  transfers between devices with their start and end apart: 21, of which 15 were waited for; matrix products, arithmetic and copies ran while one was open for 1% of the time, Pallas kernels for 10%

profile of v5, /device:TPU:0, one launch (start us, length us, event | category | flops | bytes accessed | tf_op | source)
XLA Modules:
  0.0 74.4 jit_solution(5733202446172218035)
XLA Ops:
  0.6 0.0 copy-start
  0.6 1.1 %abs_reduce_fusion = f32[256]{0:T(256)S(1)} fusion(f32[512,256]{1,0:T(8,128)} %w_ref.3), kind=kLoop, calls=%fused_computation.19 | loop fusion | flops 261888 | bytes 525312 | tf_op jit(solution)/shard_map/reduce_max | solution.py:313
  1.8 3.0 %collective-permute-start = (f32[1,256]{1,0:T(1,128)S(1)}, f32[1,256]{1,0:T(1,128)S(1)}, u32[]{:S(2)}, u32[]{:S(2)}) collective-permute-start(f32[1,256]{1,0:T(1,128)S(1)} %bitcast.3), channel_id=1, source_target_pairs={{0,2},{2,0},{4,6},{6,4},{8,10},{10,8},{12,14},{14,12},{1,3},{3,1},... | collective-permute-start | bytes 3080 | tf_op jit(solution)/shard_map/ppermute | solution.py:305
  4.8 0.0 copy-start.1
  4.8 1.6 %copy-done.1 = bf16[256,4096]{1,0:T(8,128)(2,1)S(1)} copy-done((bf16[256,4096]{1,0:T(8,128)(2,1)S(1)}, bf16[256,4096]{1,0:T(8,128)(2,1)}, u32[]{:S(2)}) %copy-start.1) | copy-done | bytes 2097176
  6.4 0.0 copy-start.4
  6.4 0.2 sort_features.1
  6.5 0.0 collective-permute-done
  6.6 0.1 collective-permute-start.6
  6.6 1.7 %collective-permute-start.5 = (bf16[256,1536]{1,0:T(8,128)(2,1)S(1)}, bf16[256,1536]{1,0:T(8,128)(2,1)S(1)}, u32[]{:S(2)}, u32[]{:S(2)}) collective-permute-start(bf16[256,1536]{1,0:T(8,128)(2,1)S(1)} %get-tuple-element.50), channel_id=1, source_target_pairs={{0,2},{2,0},{4,6},{6,4},{8,10},{10,8},{12,14},{14,12},{1,3},{3,1},... | collective-permute-start | bytes 2359304 | tf_op jit(solution)/shard_map/ppermute | solution.py:305
  8.4 1.6 %collective-permute-start.1 = (f32[1,256]{1,0:T(1,128)S(1)}, f32[1,256]{1,0:T(1,128)S(1)}, u32[]{:S(2)}, u32[]{:S(2)}) collective-permute-start(f32[1,256]{1,0:T(1,128)S(1)} %max.9), channel_id=1, source_target_pairs={{0,4},{2,6},{4,0},{6,2},{8,12},{10,14},{12,8},{14,10},{1,5},{3,7},... | collective-permute-start | bytes 3080 | tf_op jit(solution)/shard_map/ppermute | solution.py:305
  9.9 2.0 %collective-permute-done.1 = f32[1,256]{1,0:T(1,128)S(1)} collective-permute-done((f32[1,256]{1,0:T(1,128)S(1)}, f32[1,256]{1,0:T(1,128)S(1)}, u32[]{:S(2)}, u32[]{:S(2)}) %collective-permute-start.1) | collective-permute-done | bytes 1056 | tf_op jit(solution)/shard_map/ppermute | solution.py:305
  11.9 2.6 %collective-permute-start.2 = (f32[1,256]{1,0:T(1,128)S(1)}, f32[1,256]{1,0:T(1,128)S(1)}, u32[]{:S(2)}, u32[]{:S(2)}) collective-permute-start(f32[1,256]{1,0:T(1,128)S(1)} %max.10), channel_id=1, source_target_pairs={{0,8},{2,10},{4,12},{6,14},{8,0},{10,2},{12,4},{14,6},{1,9},{3,11}... | collective-permute-start | bytes 3080 | tf_op jit(solution)/shard_map/ppermute | solution.py:305
  14.5 1.9 %collective-permute-done.2 = f32[1,256]{1,0:T(1,128)S(1)} collective-permute-done((f32[1,256]{1,0:T(1,128)S(1)}, f32[1,256]{1,0:T(1,128)S(1)}, u32[]{:S(2)}, u32[]{:S(2)}) %collective-permute-start.2) | collective-permute-done | bytes 1056 | tf_op jit(solution)/shard_map/ppermute | solution.py:305
  16.4 0.0 copy-done
  16.4 0.0 copy-done.4
  16.4 0.4 fusion.19
  16.9 2.7 %collective-permute-start.3 = (f16[512,256]{1,0:T(8,128)(2,1)S(1)}, f16[512,256]{1,0:T(8,128)(2,1)S(1)}, u32[]{:S(2)}, u32[]{:S(2)}) collective-permute-start(f16[512,256]{1,0:T(8,128)(2,1)S(1)} %get-tuple-element.90), channel_id=1, source_target_pairs={{0,8},{2,10},{4,12},{6,14},{8,0},{10,2},{12,4},{14,6},{1,9},{3,11}... | collective-permute-start | bytes 786440 | tf_op jit(solution)/shard_map/ppermute | solution.py:305
  19.5 1.6 %collective-permute-start.4 = (f16[512,256]{1,0:T(8,128)(2,1)S(1)}, f16[512,256]{1,0:T(8,128)(2,1)S(1)}, u32[]{:S(2)}, u32[]{:S(2)}) collective-permute-start(f16[512,256]{1,0:T(8,128)(2,1)S(1)} %get-tuple-element.90), channel_id=1, source_target_pairs={{0,4},{2,6},{4,0},{6,2},{8,12},{10,14},{12,8},{14,10},{1,5},{3,7},... | collective-permute-start | bytes 786440 | tf_op jit(solution)/shard_map/ppermute | solution.py:305
  21.1 0.5 collective-permute-start.7
  21.6 8.4 %collective-permute-done.3 = f16[512,256]{1,0:T(8,128)(2,1)S(1)} collective-permute-done((f16[512,256]{1,0:T(8,128)(2,1)S(1)}, f16[512,256]{1,0:T(8,128)(2,1)S(1)}, u32[]{:S(2)}, u32[]{:S(2)}) %collective-permute-start.3) | collective-permute-done | bytes 262176 | tf_op jit(solution)/shard_map/ppermute | solution.py:305
  30.0 0.2 collective-permute-done.4
  30.2 0.0 collective-permute-done.5.refs_2_
  30.2 0.0 collective-permute-done.6.refs_1_
  30.2 0.0 collective-permute-start.9
  30.2 0.1 fusion.21
  30.3 1.5 %collective-permute-start.8 = (f16[512,128]{1,0:T(8,128)(2,1)S(1)}, f16[512,128]{1,0:T(8,128)(2,1)S(1)}, u32[]{:S(2)}, u32[]{:S(2)}) collective-permute-start(f16[512,128]{1,0:T(8,128)(2,1)S(1)} %get-tuple-element.105), channel_id=1, source_target_pairs={{0,4},{2,6},{4,0},{6,2},{8,12},{10,14},{12,8},{14,10},{1,5},{3,7},... | collective-permute-start | bytes 393224 | tf_op jit(solution)/shard_map/ppermute | solution.py:305
  31.8 0.1 fusion.15
  31.8 0.4 collective-permute-done.7.refs_3_
  32.2 4.0 %collective-permute-done.8 = f16[512,128]{1,0:T(8,128)(2,1)S(1)} collective-permute-done((f16[512,128]{1,0:T(8,128)(2,1)S(1)}, f16[512,128]{1,0:T(8,128)(2,1)S(1)}, u32[]{:S(2)}, u32[]{:S(2)}) %collective-permute-start.8) | collective-permute-done | bytes 131104 | tf_op jit(solution)/shard_map/ppermute | solution.py:305
  36.2 0.0 collective-permute-start.10
  36.2 0.2 fusion.16
  36.4 1.5 %collective-permute-start.11 = (f16[512,128]{1,0:T(8,128)(2,1)S(1)}, f16[512,128]{1,0:T(8,128)(2,1)S(1)}, u32[]{:S(2)}, u32[]{:S(2)}) collective-permute-start(f16[512,128]{1,0:T(8,128)(2,1)S(1)} %get-tuple-element.104), channel_id=1, source_target_pairs={{0,4},{2,6},{4,0},{6,2},{8,12},{10,14},{12,8},{14,10},{1,5},{3,7},... | collective-permute-start | bytes 393224 | tf_op jit(solution)/shard_map/ppermute | solution.py:305
  38.0 0.0 collective-permute-done.10.refs_5_
  38.0 0.0 collective-permute-done.9.refs_4_
  38.0 1.2 %partial_residual.3 = (f32[1024,128]{1,0:T(8,128)S(1)}, bf16[1024,128]{1,0:T(8,128)(2,1)S(1)}) custom-call(bf16[256,2048]{1,0:T(8,128)(2,1)S(1)} %get-tuple-element.48.refs_0_, bf16[256,2048]{1,0:T(8,128)(2,1)S(1)} %collective-permute-done.6.refs_1_, bf16[256,1536]{1,0:T(8,128)(2,1)S(1)} %collective-permute-done.5.refs_2_, ...), custom_call_target="tpu_custom_call" | custom-call | tf_op jit(solution)/shard_map/partial_residual/pallas_call | solution.py:154
  39.2 0.3 collective-permute-start.13
  39.5 2.8 %collective-permute-done.11 = f16[512,128]{1,0:T(8,128)(2,1)S(1)} collective-permute-done((f16[512,128]{1,0:T(8,128)(2,1)S(1)}, f16[512,128]{1,0:T(8,128)(2,1)S(1)}, u32[]{:S(2)}, u32[]{:S(2)}) %collective-permute-start.11) | collective-permute-done | bytes 131104 | tf_op jit(solution)/shard_map/ppermute | solution.py:305
  42.4 1.2 %partial_residual.2 = (f32[1024,128]{1,0:T(8,128)S(1)}, bf16[1024,128]{1,0:T(8,128)(2,1)S(1)}) custom-call(bf16[256,2048]{1,0:T(8,128)(2,1)S(1)} %get-tuple-element.48.refs_0_, bf16[256,2048]{1,0:T(8,128)(2,1)S(1)} %collective-permute-done.6.refs_1_, bf16[256,1536]{1,0:T(8,128)(2,1)S(1)} %collective-permute-done.5.refs_2_, ...), custom_call_target="tpu_custom_call" | custom-call | tf_op jit(solution)/shard_map/partial_residual/pallas_call | solution.py:154
  43.7 0.3 collective-permute-start.12
  43.9 4.5 %collective-permute-done.13.refs_7_ = bf16[1024,128]{1,0:T(8,128)(2,1)S(1)} collective-permute-done((bf16[1024,128]{1,0:T(8,128)(2,1)S(1)}, bf16[1024,128]{1,0:T(8,128)(2,1)S(1)}, u32[]{:S(2)}, u32[]{:S(2)}) %collective-permute-start.13) | collective-permute-done | bytes 262176 | tf_op jit(solution)/shard_map/ppermute | solution.py:305
  48.4 0.8 %partial_gradient.2 = (f32[1,128]{1,0:T(1,128)S(1)}, f32[128,512]{1,0:T(8,128)S(1)}, f32[128,512]{1,0:T(8,128)S(1)}, bf16[128,512]{1,0:T(8,128)(2,1)S(1)}, bf16[128,512]{1,0:T(8,128)(2,1)S(1)}) custom-call(bf16[256,2048]{1,0:T(8,128)(2,1)S(1)} %get-tuple-element.48.refs_0_, bf16[256,2048]{1,0:T(8,128)(2,1)S(1)} %collective-permute-done.6.refs_1_, ...), custom_call_target="tpu_custom_call" | custom-call | tf_op jit(solution)/shard_map/partial_gradient/pallas_call | solution.py:233
  49.2 1.3 %collective-permute-start.14 = (bf16[128,512]{1,0:T(8,128)(2,1)S(1)}, bf16[128,512]{1,0:T(8,128)(2,1)S(1)}, u32[]{:S(2)}, u32[]{:S(2)}) collective-permute-start(bf16[128,512]{1,0:T(8,128)(2,1)S(1)} %get-tuple-element.62), channel_id=1, source_target_pairs={{0,4},{2,6},{4,0},{6,2},{8,12},{10,14},{12,8},{14,10},{1,5},{3,7},... | collective-permute-start | bytes 393224 | tf_op jit(solution)/shard_map/ppermute | solution.py:305
  50.5 0.8 %collective-permute-start.16 = (bf16[128,512]{1,0:T(8,128)(2,1)S(1)}, bf16[128,512]{1,0:T(8,128)(2,1)S(1)}, u32[]{:S(2)}, u32[]{:S(2)}) collective-permute-start(bf16[128,512]{1,0:T(8,128)(2,1)S(1)} %get-tuple-element.69), channel_id=1, source_target_pairs={{0,4},{2,6},{4,0},{6,2},{8,12},{10,14},{12,8},{14,10},{1,5},{3,7},... | collective-permute-start | bytes 393224 | tf_op jit(solution)/shard_map/ppermute | solution.py:305
  51.3 2.0 %collective-permute-done.12.refs_7_ = bf16[1024,128]{1,0:T(8,128)(2,1)S(1)} collective-permute-done((bf16[1024,128]{1,0:T(8,128)(2,1)S(1)}, bf16[1024,128]{1,0:T(8,128)(2,1)S(1)}, u32[]{:S(2)}, u32[]{:S(2)}) %collective-permute-start.12) | collective-permute-done | bytes 262176 | tf_op jit(solution)/shard_map/ppermute | solution.py:305
  53.3 1.5 %collective-permute-done.14.got_ref = bf16[128,512]{1,0:T(8,128)(2,1)S(1)} collective-permute-done((bf16[128,512]{1,0:T(8,128)(2,1)S(1)}, bf16[128,512]{1,0:T(8,128)(2,1)S(1)}, u32[]{:S(2)}, u32[]{:S(2)}) %collective-permute-start.14) | collective-permute-done | bytes 131104 | tf_op jit(solution)/shard_map/ppermute | solution.py:305
  54.8 0.8 %partial_gradient.3 = (f32[1,128]{1,0:T(1,128)S(1)}, f32[128,512]{1,0:T(8,128)S(1)}, f32[128,512]{1,0:T(8,128)S(1)}, bf16[136,512]{1,0:T(8,128)(2,1)S(1)}, bf16[128,512]{1,0:T(8,128)(2,1)S(1)}) custom-call(bf16[256,2048]{1,0:T(8,128)(2,1)S(1)} %get-tuple-element.48.refs_0_, bf16[256,2048]{1,0:T(8,128)(2,1)S(1)} %collective-permute-done.6.refs_1_, ...), custom_call_target="tpu_custom_call" | custom-call | tf_op jit(solution)/shard_map/partial_gradient/pallas_call | solution.py:233
  55.6 0.6 collective-permute-done.16.near_ref
  56.2 1.0 %collective-permute-start.17 = (bf16[136,512]{1,0:T(8,128)(2,1)S(1)}, bf16[136,512]{1,0:T(8,128)(2,1)S(1)}, u32[]{:S(2)}, u32[]{:S(2)}) collective-permute-start(bf16[136,512]{1,0:T(8,128)(2,1)S(1)} %get-tuple-element.71), channel_id=1, source_target_pairs={{0,4},{2,6},{4,0},{6,2},{8,12},{10,14},{12,8},{14,10},{1,5},{3,7},... | collective-permute-start | bytes 417800 | tf_op jit(solution)/shard_map/ppermute | solution.py:305
  57.2 0.5 join_far.3
  57.8 2.4 %collective-permute-start.19 = (bf16[136,512]{1,0:T(8,128)(2,1)S(1)}, bf16[136,512]{1,0:T(8,128)(2,1)S(1)}, u32[]{:S(2)}, u32[]{:S(2)}) collective-permute-start(bf16[136,512]{1,0:T(8,128)(2,1)S(1)} %get-tuple-element.78), channel_id=1, source_target_pairs={{0,8},{2,10},{4,12},{6,14},{8,0},{10,2},{12,4},{14,6},{1,9},{3,11}... | collective-permute-start | bytes 417800 | tf_op jit(solution)/shard_map/ppermute | solution.py:305
  60.2 1.4 %collective-permute-done.17.got_ref = bf16[136,512]{1,0:T(8,128)(2,1)S(1)} collective-permute-done((bf16[136,512]{1,0:T(8,128)(2,1)S(1)}, bf16[136,512]{1,0:T(8,128)(2,1)S(1)}, u32[]{:S(2)}, u32[]{:S(2)}) %collective-permute-start.17) | collective-permute-done | bytes 139296 | tf_op jit(solution)/shard_map/ppermute | solution.py:305
  61.6 3.6 %collective-permute-start.18 = (bf16[136,512]{1,0:T(8,128)(2,1)S(1)}, bf16[136,512]{1,0:T(8,128)(2,1)S(1)}, u32[]{:S(2)}, u32[]{:S(2)}) collective-permute-start(bf16[136,512]{1,0:T(8,128)(2,1)S(1)} %get-tuple-element.73), channel_id=1, source_target_pairs={{0,8},{2,10},{4,12},{6,14},{8,0},{10,2},{12,4},{14,6},{1,9},{3,11}... | collective-permute-start | bytes 417800 | tf_op jit(solution)/shard_map/ppermute | solution.py:305
  65.1 2.1 %collective-permute-start.15 = (bf16[128,512]{1,0:T(8,128)(2,1)S(1)}, bf16[128,512]{1,0:T(8,128)(2,1)S(1)}, u32[]{:S(2)}, u32[]{:S(2)}) collective-permute-start(bf16[128,512]{1,0:T(8,128)(2,1)S(1)} %get-tuple-element.66), channel_id=1, source_target_pairs={{0,4},{2,6},{4,0},{6,2},{8,12},{10,14},{12,8},{14,10},{1,5},{3,7},... | collective-permute-start | bytes 393224 | tf_op jit(solution)/shard_map/ppermute | solution.py:305
  67.3 0.2 collective-permute-done.19.far_ref
  67.5 0.0 copy-done.2
  67.5 0.0 copy-done.3
  67.5 1.1 %apply_update.2 = (f32[512,256]{1,0:T(8,128)}, f32[512,256]{1,0:T(8,128)}, f32[512,256]{1,0:T(8,128)}) custom-call(f32[128,512]{1,0:T(8,128)S(1)} %get-tuple-element.74.own_ref, bf16[128,512]{1,0:T(8,128)(2,1)S(1)} %collective-permute-done.16.near_ref, bf16[136,512]{1,0:T(8,128)(2,1)S(1)} %collective-permute-done.19.far_ref, f32[512,256]{1,0:T(8,128)S(1)} %copy-done, ...), custom_call_target="tpu_custom_call" | custom-call | tf_op jit(solution)/shard_map/apply_update/pallas_call | solution.py:289
  68.7 1.9 %collective-permute-done.18.far_ref.got_ref = bf16[136,512]{1,0:T(8,128)(2,1)S(1)} collective-permute-done((bf16[136,512]{1,0:T(8,128)(2,1)S(1)}, bf16[136,512]{1,0:T(8,128)(2,1)S(1)}, u32[]{:S(2)}, u32[]{:S(2)}) %collective-permute-start.18) | collective-permute-done | bytes 139296 | tf_op jit(solution)/shard_map/ppermute | solution.py:305
  70.6 0.0 collective-permute-start.20
  70.6 0.3 collective-permute-done.15.near_ref
  70.9 1.2 %apply_update.3 = (f32[512,256]{1,0:T(8,128)}, f32[512,256]{1,0:T(8,128)}, f32[512,256]{1,0:T(8,128)}) custom-call(f32[128,512]{1,0:T(8,128)S(1)} %get-tuple-element.65.own_ref, bf16[128,512]{1,0:T(8,128)(2,1)S(1)} %collective-permute-done.15.near_ref, ...), custom_call_target="tpu_custom_call", output_to_operand_aliasing={{0}: (6, {}), {1}: (7, {}), {2}: (8, {})} | custom-call | tf_op jit(solution)/shard_map/apply_update/pallas_call | solution.py:289
  72.0 0.0 collective-permute-done.20
  72.0 0.6 add_reduce_fusion
  (10 shorter events, 0.2 us)
Async XLA Ops:
  0.6 15.8 %copy-start = (f32[512,256]{1,0:T(8,128)S(1)}, f32[512,256]{1,0:T(8,128)}, u32[]{:S(2)}) copy-start(f32[512,256]{1,0:T(8,128)} %w_ref.3) | copy-start | bytes 1572868
  1.8 4.8 %collective-permute-start = (f32[1,256]{1,0:T(1,128)S(1)}, f32[1,256]{1,0:T(1,128)S(1)}, u32[]{:S(2)}, u32[]{:S(2)}) collective-permute-start(f32[1,256]{1,0:T(1,128)S(1)} %bitcast.3), channel_id=1, source_target_pairs={{0,2},{2,0},{4,6},{6,4},{8,10},{10,8},{12,14},{14,12},{1,3},{3,1},... | collective-permute-start | bytes 3080 | tf_op jit(solution)/shard_map/ppermute | solution.py:305
  4.8 1.6 %copy-start.1 = (bf16[256,4096]{1,0:T(8,128)(2,1)S(1)}, bf16[256,4096]{1,0:T(8,128)(2,1)}, u32[]{:S(2)}) copy-start(bf16[256,4096]{1,0:T(8,128)(2,1)} %h_ref.1) | copy-start | bytes 6291460
  6.4 10.0 %copy-start.4 = (bf16[512,256]{1,0:T(8,128)(2,1)S(1)}, bf16[512,256]{1,0:T(8,128)(2,1)}, u32[]{:S(2)}) copy-start(bf16[512,256]{1,0:T(8,128)(2,1)} %param.6) | copy-start | bytes 786436
  6.6 23.6 %collective-permute-start.6 = (bf16[256,2048]{1,0:T(8,128)(2,1)S(1)}, bf16[256,2048]{1,0:T(8,128)(2,1)S(1)}, u32[]{:S(2)}, u32[]{:S(2)}) collective-permute-start(bf16[256,2048]{1,0:T(8,128)(2,1)S(1)} %get-tuple-element.48.refs_0_), channel_id=1, source_target_pairs={{0,1},{1,0},{2,3},{3,2},{4,5},{5,4},{6,7},{7,6},{8,9},{9,8},{10,11... | collective-permute-start | bytes 3145736 | tf_op jit(solution)/shard_map/ppermute | solution.py:308
  6.6 23.5 %collective-permute-start.5 = (bf16[256,1536]{1,0:T(8,128)(2,1)S(1)}, bf16[256,1536]{1,0:T(8,128)(2,1)S(1)}, u32[]{:S(2)}, u32[]{:S(2)}) collective-permute-start(bf16[256,1536]{1,0:T(8,128)(2,1)S(1)} %get-tuple-element.50), channel_id=1, source_target_pairs={{0,2},{2,0},{4,6},{6,4},{8,10},{10,8},{12,14},{14,12},{1,3},{3,1},... | collective-permute-start | bytes 2359304 | tf_op jit(solution)/shard_map/ppermute | solution.py:305
  8.4 3.6 %collective-permute-start.1 = (f32[1,256]{1,0:T(1,128)S(1)}, f32[1,256]{1,0:T(1,128)S(1)}, u32[]{:S(2)}, u32[]{:S(2)}) collective-permute-start(f32[1,256]{1,0:T(1,128)S(1)} %max.9), channel_id=1, source_target_pairs={{0,4},{2,6},{4,0},{6,2},{8,12},{10,14},{12,8},{14,10},{1,5},{3,7},... | collective-permute-start | bytes 3080 | tf_op jit(solution)/shard_map/ppermute | solution.py:305
  11.9 4.5 %collective-permute-start.2 = (f32[1,256]{1,0:T(1,128)S(1)}, f32[1,256]{1,0:T(1,128)S(1)}, u32[]{:S(2)}, u32[]{:S(2)}) collective-permute-start(f32[1,256]{1,0:T(1,128)S(1)} %max.10), channel_id=1, source_target_pairs={{0,8},{2,10},{4,12},{6,14},{8,0},{10,2},{12,4},{14,6},{1,9},{3,11}... | collective-permute-start | bytes 3080 | tf_op jit(solution)/shard_map/ppermute | solution.py:305
  16.9 13.1 %collective-permute-start.3 = (f16[512,256]{1,0:T(8,128)(2,1)S(1)}, f16[512,256]{1,0:T(8,128)(2,1)S(1)}, u32[]{:S(2)}, u32[]{:S(2)}) collective-permute-start(f16[512,256]{1,0:T(8,128)(2,1)S(1)} %get-tuple-element.90), channel_id=1, source_target_pairs={{0,8},{2,10},{4,12},{6,14},{8,0},{10,2},{12,4},{14,6},{1,9},{3,11}... | collective-permute-start | bytes 786440 | tf_op jit(solution)/shard_map/ppermute | solution.py:305
  19.5 10.7 %collective-permute-start.4 = (f16[512,256]{1,0:T(8,128)(2,1)S(1)}, f16[512,256]{1,0:T(8,128)(2,1)S(1)}, u32[]{:S(2)}, u32[]{:S(2)}) collective-permute-start(f16[512,256]{1,0:T(8,128)(2,1)S(1)} %get-tuple-element.90), channel_id=1, source_target_pairs={{0,4},{2,6},{4,0},{6,2},{8,12},{10,14},{12,8},{14,10},{1,5},{3,7},... | collective-permute-start | bytes 786440 | tf_op jit(solution)/shard_map/ppermute | solution.py:305
  21.1 11.1 %collective-permute-start.7 = (bf16[256,512]{1,0:T(8,128)(2,1)S(1)}, bf16[256,512]{1,0:T(8,128)(2,1)S(1)}, u32[]{:S(2)}, u32[]{:S(2)}) collective-permute-start(bf16[256,512]{1,0:T(8,128)(2,1)S(1)} %get-tuple-element.53), channel_id=1, source_target_pairs={{0,2},{2,0},{4,6},{6,4},{8,10},{10,8},{12,14},{14,12},{1,3},{3,1},... | collective-permute-start | bytes 786440 | tf_op jit(solution)/shard_map/ppermute | solution.py:305
  30.2 7.8 %collective-permute-start.9 = (bf16[256,1536]{1,0:T(8,128)(2,1)S(1)}, bf16[256,1536]{1,0:T(8,128)(2,1)S(1)}, u32[]{:S(2)}, u32[]{:S(2)}) collective-permute-start(bf16[256,1536]{1,0:T(8,128)(2,1)S(1)} %collective-permute-done.5.refs_2_), channel_id=1, source_target_pairs={{0,1},{1,0},{2,3},{3,2},{4,5},{5,4},{6,7},{7,6},{8,9},{9,8},{10,11... | collective-permute-start | bytes 2359304 | tf_op jit(solution)/shard_map/ppermute | solution.py:308
  30.3 6.0 %collective-permute-start.8 = (f16[512,128]{1,0:T(8,128)(2,1)S(1)}, f16[512,128]{1,0:T(8,128)(2,1)S(1)}, u32[]{:S(2)}, u32[]{:S(2)}) collective-permute-start(f16[512,128]{1,0:T(8,128)(2,1)S(1)} %get-tuple-element.105), channel_id=1, source_target_pairs={{0,4},{2,6},{4,0},{6,2},{8,12},{10,14},{12,8},{14,10},{1,5},{3,7},... | collective-permute-start | bytes 393224 | tf_op jit(solution)/shard_map/ppermute | solution.py:305
  36.2 1.7 %collective-permute-start.10 = (bf16[256,512]{1,0:T(8,128)(2,1)S(1)}, bf16[256,512]{1,0:T(8,128)(2,1)S(1)}, u32[]{:S(2)}, u32[]{:S(2)}) collective-permute-start(bf16[256,512]{1,0:T(8,128)(2,1)S(1)} %collective-permute-done.7.refs_3_), channel_id=1, source_target_pairs={{0,1},{1,0},{2,3},{3,2},{4,5},{5,4},{6,7},{7,6},{8,9},{9,8},{10,11... | collective-permute-start | bytes 786440 | tf_op jit(solution)/shard_map/ppermute | solution.py:308
  36.4 6.0 %collective-permute-start.11 = (f16[512,128]{1,0:T(8,128)(2,1)S(1)}, f16[512,128]{1,0:T(8,128)(2,1)S(1)}, u32[]{:S(2)}, u32[]{:S(2)}) collective-permute-start(f16[512,128]{1,0:T(8,128)(2,1)S(1)} %get-tuple-element.104), channel_id=1, source_target_pairs={{0,4},{2,6},{4,0},{6,2},{8,12},{10,14},{12,8},{14,10},{1,5},{3,7},... | collective-permute-start | bytes 393224 | tf_op jit(solution)/shard_map/ppermute | solution.py:305
  39.2 9.2 %collective-permute-start.13 = (bf16[1024,128]{1,0:T(8,128)(2,1)S(1)}, bf16[1024,128]{1,0:T(8,128)(2,1)S(1)}, u32[]{:S(2)}, u32[]{:S(2)}) collective-permute-start(bf16[1024,128]{1,0:T(8,128)(2,1)S(1)} %get-tuple-element.61), channel_id=1, source_target_pairs={{0,2},{2,0},{4,6},{6,4},{8,10},{10,8},{12,14},{14,12},{1,3},{3,1},... | collective-permute-start | bytes 786440 | tf_op jit(solution)/shard_map/ppermute | solution.py:305
  43.7 9.7 %collective-permute-start.12 = (bf16[1024,128]{1,0:T(8,128)(2,1)S(1)}, bf16[1024,128]{1,0:T(8,128)(2,1)S(1)}, u32[]{:S(2)}, u32[]{:S(2)}) collective-permute-start(bf16[1024,128]{1,0:T(8,128)(2,1)S(1)} %get-tuple-element.58), channel_id=1, source_target_pairs={{0,2},{2,0},{4,6},{6,4},{8,10},{10,8},{12,14},{14,12},{1,3},{3,1},... | collective-permute-start | bytes 786440 | tf_op jit(solution)/shard_map/ppermute | solution.py:305
  49.2 5.6 %collective-permute-start.14 = (bf16[128,512]{1,0:T(8,128)(2,1)S(1)}, bf16[128,512]{1,0:T(8,128)(2,1)S(1)}, u32[]{:S(2)}, u32[]{:S(2)}) collective-permute-start(bf16[128,512]{1,0:T(8,128)(2,1)S(1)} %get-tuple-element.62), channel_id=1, source_target_pairs={{0,4},{2,6},{4,0},{6,2},{8,12},{10,14},{12,8},{14,10},{1,5},{3,7},... | collective-permute-start | bytes 393224 | tf_op jit(solution)/shard_map/ppermute | solution.py:305
  50.5 5.7 %collective-permute-start.16 = (bf16[128,512]{1,0:T(8,128)(2,1)S(1)}, bf16[128,512]{1,0:T(8,128)(2,1)S(1)}, u32[]{:S(2)}, u32[]{:S(2)}) collective-permute-start(bf16[128,512]{1,0:T(8,128)(2,1)S(1)} %get-tuple-element.69), channel_id=1, source_target_pairs={{0,4},{2,6},{4,0},{6,2},{8,12},{10,14},{12,8},{14,10},{1,5},{3,7},... | collective-permute-start | bytes 393224 | tf_op jit(solution)/shard_map/ppermute | solution.py:305
  54.8 12.7 %copy-start.2 = (f32[512,256]{1,0:T(8,128)S(1)}, f32[512,256]{1,0:T(8,128)}, u32[]{:S(2)}) copy-start(f32[512,256]{1,0:T(8,128)} %m_ref.3) | copy-start | bytes 1572868
  54.8 12.7 %copy-start.3 = (f32[512,256]{1,0:T(8,128)S(1)}, f32[512,256]{1,0:T(8,128)}, u32[]{:S(2)}) copy-start(f32[512,256]{1,0:T(8,128)} %v_ref.3) | copy-start | bytes 1572868
  56.2 5.3 %collective-permute-start.17 = (bf16[136,512]{1,0:T(8,128)(2,1)S(1)}, bf16[136,512]{1,0:T(8,128)(2,1)S(1)}, u32[]{:S(2)}, u32[]{:S(2)}) collective-permute-start(bf16[136,512]{1,0:T(8,128)(2,1)S(1)} %get-tuple-element.71), channel_id=1, source_target_pairs={{0,4},{2,6},{4,0},{6,2},{8,12},{10,14},{12,8},{14,10},{1,5},{3,7},... | collective-permute-start | bytes 417800 | tf_op jit(solution)/shard_map/ppermute | solution.py:305
  57.8 9.7 %collective-permute-start.19 = (bf16[136,512]{1,0:T(8,128)(2,1)S(1)}, bf16[136,512]{1,0:T(8,128)(2,1)S(1)}, u32[]{:S(2)}, u32[]{:S(2)}) collective-permute-start(bf16[136,512]{1,0:T(8,128)(2,1)S(1)} %get-tuple-element.78), channel_id=1, source_target_pairs={{0,8},{2,10},{4,12},{6,14},{8,0},{10,2},{12,4},{14,6},{1,9},{3,11}... | collective-permute-start | bytes 417800 | tf_op jit(solution)/shard_map/ppermute | solution.py:305
  61.6 9.0 %collective-permute-start.18 = (bf16[136,512]{1,0:T(8,128)(2,1)S(1)}, bf16[136,512]{1,0:T(8,128)(2,1)S(1)}, u32[]{:S(2)}, u32[]{:S(2)}) collective-permute-start(bf16[136,512]{1,0:T(8,128)(2,1)S(1)} %get-tuple-element.73), channel_id=1, source_target_pairs={{0,8},{2,10},{4,12},{6,14},{8,0},{10,2},{12,4},{14,6},{1,9},{3,11}... | collective-permute-start | bytes 417800 | tf_op jit(solution)/shard_map/ppermute | solution.py:305
  65.1 5.7 %collective-permute-start.15 = (bf16[128,512]{1,0:T(8,128)(2,1)S(1)}, bf16[128,512]{1,0:T(8,128)(2,1)S(1)}, u32[]{:S(2)}, u32[]{:S(2)}) collective-permute-start(bf16[128,512]{1,0:T(8,128)(2,1)S(1)} %get-tuple-element.66), channel_id=1, source_target_pairs={{0,4},{2,6},{4,0},{6,2},{8,12},{10,14},{12,8},{14,10},{1,5},{3,7},... | collective-permute-start | bytes 393224 | tf_op jit(solution)/shard_map/ppermute | solution.py:305
  70.6 1.4 %collective-permute-start.20 = (f32[1,128]{1,0:T(1,128)S(1)}, f32[1,128]{1,0:T(1,128)S(1)}, u32[]{:S(2)}, u32[]{:S(2)}) collective-permute-start(f32[1,128]{1,0:T(1,128)S(1)} %total_loss.1), channel_id=1, source_target_pairs={{0,1},{1,0},{2,3},{3,2},{4,5},{5,4},{6,7},{7,6},{8,9},{9,8},{10,11... | collective-permute-start | bytes 1544 | tf_op jit(solution)/shard_map/ppermute | solution.py:308

commit v6 on v5

--- a/solution.py
+++ b/solution.py
@@ -260,11 +260,11 @@
     )(*held(far, got, loss))
 
 
-def total_loss(loss, got):
+def total_loss(loss, got, total_tokens):
     columns = loss.shape[1]
 
     def kernel(loss_ref, got_ref, out_ref):
-        out_ref[...] = loss_ref[...] + read_note(got_ref, columns, columns)
+        out_ref[...] = (loss_ref[...] + read_note(got_ref, columns, columns)) / total_tokens
 
     return pl.pallas_call(
         kernel, out_shape=pltpu.VMEM((1, columns), f32), in_specs=vmem(2), out_specs=vmem(1)[0],
@@ -358,8 +358,8 @@
     from_far_next = flip(to_far, 4)
     from_near_next = flip(to_near_next, 2)
     from_far_next, *news = together(from_far_next, *news)
-    loss = total_loss(loss, from_far_next)
-    loss = jnp.sum(loss + swap_cores(loss)).reshape(1) / total_tokens
+    loss = total_loss(loss, from_far_next, total_tokens)
+    loss = jnp.sum(loss + swap_cores(loss)).reshape(1)
     news = apply_update(1, own_next, from_near_next, from_far_next, states, news)
     return (*news, loss)
 

time: 74.6 us -> 72.8 us (0.976)
  between operations: 2.55 us -> 0.78 us
where the time goes in v6:
time: 72.8 us; the launch traced here: 72.6 us
  waiting for transfers between devices  32.1 us (44%)
  starting transfers between devices  28.5 us (39%)
  Pallas kernels  7.07 us (10%)
  other arithmetic  2.56 us (4%)
  local copies, waits for them, and re-layouts  1.66 us (2%)
  between operations  0.78 us (1%)
    ppermute x17, waiting for transfers between devices, flip(): return lax.ppermute(array, 'fsdp', [(i, i ^ bit) for i in range(fsdp)])  32.1 us
    ppermute x17, starting transfers between devices, flip(): return lax.ppermute(array, 'fsdp', [(i, i ^ bit) for i in range(fsdp)])  28.4 us
    pallas_call x2, Pallas kernels, partial_residual(): pl.pallas_call(kernel, out_shape=(pltpu.VMEM(shape, f32), pltpu.VMEM(shap...  2.5 us
    pallas_call x2, Pallas kernels, apply_update(): pl.pallas_call(kernel, grid=(1,), out_shape=(shape,) * 3, in_specs=vmem(6...  2.3 us
    unnamed x10, local copies, waits for them, and re-layouts  1.61 us
    pallas_call x2, Pallas kernels, partial_gradient(): pl.pallas_call(kernel, out_shape=(pltpu.VMEM((1, columns), f32), pltpu.VM...  1.54 us
  transfers between devices with their start and end apart: 21, of which 15 were waited for; matrix products, arithmetic and copies ran while one was open for 1% of the time, Pallas kernels for 10%

profile of v6, /device:TPU:0, one launch (start us, length us, event | category | flops | bytes accessed | tf_op | source)
XLA Modules:
  0.0 72.6 jit_solution(6333274050457827589)
XLA Ops:
  0.6 0.0 copy-start
  0.6 1.1 %abs_reduce_fusion = f32[256]{0:T(256)S(1)} fusion(f32[512,256]{1,0:T(8,128)} %w_ref.3), kind=kLoop, calls=%fused_computation.19 | loop fusion | flops 261888 | bytes 525312 | tf_op jit(solution)/shard_map/reduce_max | solution.py:313
  1.8 3.0 %collective-permute-start = (f32[1,256]{1,0:T(1,128)S(1)}, f32[1,256]{1,0:T(1,128)S(1)}, u32[]{:S(2)}, u32[]{:S(2)}) collective-permute-start(f32[1,256]{1,0:T(1,128)S(1)} %bitcast.3), channel_id=1, source_target_pairs={{0,2},{2,0},{4,6},{6,4},{8,10},{10,8},{12,14},{14,12},{1,3},{3,1},... | collective-permute-start | bytes 3080 | tf_op jit(solution)/shard_map/ppermute | solution.py:305
  4.8 0.0 copy-start.1
  4.8 1.6 %copy-done.1 = bf16[256,4096]{1,0:T(8,128)(2,1)S(1)} copy-done((bf16[256,4096]{1,0:T(8,128)(2,1)S(1)}, bf16[256,4096]{1,0:T(8,128)(2,1)}, u32[]{:S(2)}) %copy-start.1) | copy-done | bytes 2097176
  6.4 0.0 copy-start.4
  6.4 0.2 sort_features.1
  6.5 0.0 collective-permute-done
  6.6 0.1 collective-permute-start.6
  6.6 1.7 %collective-permute-start.5 = (bf16[256,1536]{1,0:T(8,128)(2,1)S(1)}, bf16[256,1536]{1,0:T(8,128)(2,1)S(1)}, u32[]{:S(2)}, u32[]{:S(2)}) collective-permute-start(bf16[256,1536]{1,0:T(8,128)(2,1)S(1)} %get-tuple-element.50), channel_id=1, source_target_pairs={{0,2},{2,0},{4,6},{6,4},{8,10},{10,8},{12,14},{14,12},{1,3},{3,1},... | collective-permute-start | bytes 2359304 | tf_op jit(solution)/shard_map/ppermute | solution.py:305
  8.4 1.6 %collective-permute-start.1 = (f32[1,256]{1,0:T(1,128)S(1)}, f32[1,256]{1,0:T(1,128)S(1)}, u32[]{:S(2)}, u32[]{:S(2)}) collective-permute-start(f32[1,256]{1,0:T(1,128)S(1)} %max.9), channel_id=1, source_target_pairs={{0,4},{2,6},{4,0},{6,2},{8,12},{10,14},{12,8},{14,10},{1,5},{3,7},... | collective-permute-start | bytes 3080 | tf_op jit(solution)/shard_map/ppermute | solution.py:305
  9.9 2.0 %collective-permute-done.1 = f32[1,256]{1,0:T(1,128)S(1)} collective-permute-done((f32[1,256]{1,0:T(1,128)S(1)}, f32[1,256]{1,0:T(1,128)S(1)}, u32[]{:S(2)}, u32[]{:S(2)}) %collective-permute-start.1) | collective-permute-done | bytes 1056 | tf_op jit(solution)/shard_map/ppermute | solution.py:305
  11.9 2.6 %collective-permute-start.2 = (f32[1,256]{1,0:T(1,128)S(1)}, f32[1,256]{1,0:T(1,128)S(1)}, u32[]{:S(2)}, u32[]{:S(2)}) collective-permute-start(f32[1,256]{1,0:T(1,128)S(1)} %max.10), channel_id=1, source_target_pairs={{0,8},{2,10},{4,12},{6,14},{8,0},{10,2},{12,4},{14,6},{1,9},{3,11}... | collective-permute-start | bytes 3080 | tf_op jit(solution)/shard_map/ppermute | solution.py:305
  14.5 1.9 %collective-permute-done.2 = f32[1,256]{1,0:T(1,128)S(1)} collective-permute-done((f32[1,256]{1,0:T(1,128)S(1)}, f32[1,256]{1,0:T(1,128)S(1)}, u32[]{:S(2)}, u32[]{:S(2)}) %collective-permute-start.2) | collective-permute-done | bytes 1056 | tf_op jit(solution)/shard_map/ppermute | solution.py:305
  16.4 0.0 copy-done
  16.4 0.0 copy-done.4
  16.4 0.4 fusion.19
  16.9 2.7 %collective-permute-start.3 = (f16[512,256]{1,0:T(8,128)(2,1)S(1)}, f16[512,256]{1,0:T(8,128)(2,1)S(1)}, u32[]{:S(2)}, u32[]{:S(2)}) collective-permute-start(f16[512,256]{1,0:T(8,128)(2,1)S(1)} %get-tuple-element.90), channel_id=1, source_target_pairs={{0,8},{2,10},{4,12},{6,14},{8,0},{10,2},{12,4},{14,6},{1,9},{3,11}... | collective-permute-start | bytes 786440 | tf_op jit(solution)/shard_map/ppermute | solution.py:305
  19.5 1.6 %collective-permute-start.4 = (f16[512,256]{1,0:T(8,128)(2,1)S(1)}, f16[512,256]{1,0:T(8,128)(2,1)S(1)}, u32[]{:S(2)}, u32[]{:S(2)}) collective-permute-start(f16[512,256]{1,0:T(8,128)(2,1)S(1)} %get-tuple-element.90), channel_id=1, source_target_pairs={{0,4},{2,6},{4,0},{6,2},{8,12},{10,14},{12,8},{14,10},{1,5},{3,7},... | collective-permute-start | bytes 786440 | tf_op jit(solution)/shard_map/ppermute | solution.py:305
  21.1 0.5 collective-permute-start.7
  21.6 8.4 %collective-permute-done.3 = f16[512,256]{1,0:T(8,128)(2,1)S(1)} collective-permute-done((f16[512,256]{1,0:T(8,128)(2,1)S(1)}, f16[512,256]{1,0:T(8,128)(2,1)S(1)}, u32[]{:S(2)}, u32[]{:S(2)}) %collective-permute-start.3) | collective-permute-done | bytes 262176 | tf_op jit(solution)/shard_map/ppermute | solution.py:305
  30.0 0.2 collective-permute-done.4
  30.2 0.0 collective-permute-done.5.refs_2_
  30.2 0.0 collective-permute-done.6.refs_1_
  30.2 0.0 collective-permute-start.9
  30.2 0.1 fusion.21
  30.3 1.5 %collective-permute-start.8 = (f16[512,128]{1,0:T(8,128)(2,1)S(1)}, f16[512,128]{1,0:T(8,128)(2,1)S(1)}, u32[]{:S(2)}, u32[]{:S(2)}) collective-permute-start(f16[512,128]{1,0:T(8,128)(2,1)S(1)} %get-tuple-element.105), channel_id=1, source_target_pairs={{0,4},{2,6},{4,0},{6,2},{8,12},{10,14},{12,8},{14,10},{1,5},{3,7},... | collective-permute-start | bytes 393224 | tf_op jit(solution)/shard_map/ppermute | solution.py:305
  31.8 0.1 fusion.15
  31.8 0.4 collective-permute-done.7.refs_3_
  32.2 4.0 %collective-permute-done.8 = f16[512,128]{1,0:T(8,128)(2,1)S(1)} collective-permute-done((f16[512,128]{1,0:T(8,128)(2,1)S(1)}, f16[512,128]{1,0:T(8,128)(2,1)S(1)}, u32[]{:S(2)}, u32[]{:S(2)}) %collective-permute-start.8) | collective-permute-done | bytes 131104 | tf_op jit(solution)/shard_map/ppermute | solution.py:305
  36.2 0.0 collective-permute-start.10
  36.2 0.2 fusion.16
  36.4 1.5 %collective-permute-start.11 = (f16[512,128]{1,0:T(8,128)(2,1)S(1)}, f16[512,128]{1,0:T(8,128)(2,1)S(1)}, u32[]{:S(2)}, u32[]{:S(2)}) collective-permute-start(f16[512,128]{1,0:T(8,128)(2,1)S(1)} %get-tuple-element.104), channel_id=1, source_target_pairs={{0,4},{2,6},{4,0},{6,2},{8,12},{10,14},{12,8},{14,10},{1,5},{3,7},... | collective-permute-start | bytes 393224 | tf_op jit(solution)/shard_map/ppermute | solution.py:305
  38.0 0.0 collective-permute-done.10.refs_5_
  38.0 0.0 collective-permute-done.9.refs_4_
  38.0 1.2 %partial_residual.3 = (f32[1024,128]{1,0:T(8,128)S(1)}, bf16[1024,128]{1,0:T(8,128)(2,1)S(1)}) custom-call(bf16[256,2048]{1,0:T(8,128)(2,1)S(1)} %get-tuple-element.48.refs_0_, bf16[256,2048]{1,0:T(8,128)(2,1)S(1)} %collective-permute-done.6.refs_1_, bf16[256,1536]{1,0:T(8,128)(2,1)S(1)} %collective-permute-done.5.refs_2_, ...), custom_call_target="tpu_custom_call" | custom-call | tf_op jit(solution)/shard_map/partial_residual/pallas_call | solution.py:154
  39.2 0.3 collective-permute-start.13
  39.5 2.8 %collective-permute-done.11 = f16[512,128]{1,0:T(8,128)(2,1)S(1)} collective-permute-done((f16[512,128]{1,0:T(8,128)(2,1)S(1)}, f16[512,128]{1,0:T(8,128)(2,1)S(1)}, u32[]{:S(2)}, u32[]{:S(2)}) %collective-permute-start.11) | collective-permute-done | bytes 131104 | tf_op jit(solution)/shard_map/ppermute | solution.py:305
  42.4 1.2 %partial_residual.2 = (f32[1024,128]{1,0:T(8,128)S(1)}, bf16[1024,128]{1,0:T(8,128)(2,1)S(1)}) custom-call(bf16[256,2048]{1,0:T(8,128)(2,1)S(1)} %get-tuple-element.48.refs_0_, bf16[256,2048]{1,0:T(8,128)(2,1)S(1)} %collective-permute-done.6.refs_1_, bf16[256,1536]{1,0:T(8,128)(2,1)S(1)} %collective-permute-done.5.refs_2_, ...), custom_call_target="tpu_custom_call" | custom-call | tf_op jit(solution)/shard_map/partial_residual/pallas_call | solution.py:154
  43.7 0.3 collective-permute-start.12
  43.9 4.5 %collective-permute-done.13.refs_7_ = bf16[1024,128]{1,0:T(8,128)(2,1)S(1)} collective-permute-done((bf16[1024,128]{1,0:T(8,128)(2,1)S(1)}, bf16[1024,128]{1,0:T(8,128)(2,1)S(1)}, u32[]{:S(2)}, u32[]{:S(2)}) %collective-permute-start.13) | collective-permute-done | bytes 262176 | tf_op jit(solution)/shard_map/ppermute | solution.py:305
  48.4 0.8 %partial_gradient.2 = (f32[1,128]{1,0:T(1,128)S(1)}, f32[128,512]{1,0:T(8,128)S(1)}, f32[128,512]{1,0:T(8,128)S(1)}, bf16[128,512]{1,0:T(8,128)(2,1)S(1)}, bf16[128,512]{1,0:T(8,128)(2,1)S(1)}) custom-call(bf16[256,2048]{1,0:T(8,128)(2,1)S(1)} %get-tuple-element.48.refs_0_, bf16[256,2048]{1,0:T(8,128)(2,1)S(1)} %collective-permute-done.6.refs_1_, ...), custom_call_target="tpu_custom_call" | custom-call | tf_op jit(solution)/shard_map/partial_gradient/pallas_call | solution.py:233
  49.2 1.3 %collective-permute-start.14 = (bf16[128,512]{1,0:T(8,128)(2,1)S(1)}, bf16[128,512]{1,0:T(8,128)(2,1)S(1)}, u32[]{:S(2)}, u32[]{:S(2)}) collective-permute-start(bf16[128,512]{1,0:T(8,128)(2,1)S(1)} %get-tuple-element.62), channel_id=1, source_target_pairs={{0,4},{2,6},{4,0},{6,2},{8,12},{10,14},{12,8},{14,10},{1,5},{3,7},... | collective-permute-start | bytes 393224 | tf_op jit(solution)/shard_map/ppermute | solution.py:305
  50.5 0.8 %collective-permute-start.16 = (bf16[128,512]{1,0:T(8,128)(2,1)S(1)}, bf16[128,512]{1,0:T(8,128)(2,1)S(1)}, u32[]{:S(2)}, u32[]{:S(2)}) collective-permute-start(bf16[128,512]{1,0:T(8,128)(2,1)S(1)} %get-tuple-element.69), channel_id=1, source_target_pairs={{0,4},{2,6},{4,0},{6,2},{8,12},{10,14},{12,8},{14,10},{1,5},{3,7},... | collective-permute-start | bytes 393224 | tf_op jit(solution)/shard_map/ppermute | solution.py:305
  51.3 2.0 %collective-permute-done.12.refs_7_ = bf16[1024,128]{1,0:T(8,128)(2,1)S(1)} collective-permute-done((bf16[1024,128]{1,0:T(8,128)(2,1)S(1)}, bf16[1024,128]{1,0:T(8,128)(2,1)S(1)}, u32[]{:S(2)}, u32[]{:S(2)}) %collective-permute-start.12) | collective-permute-done | bytes 262176 | tf_op jit(solution)/shard_map/ppermute | solution.py:305
  53.3 1.5 %collective-permute-done.14.got_ref = bf16[128,512]{1,0:T(8,128)(2,1)S(1)} collective-permute-done((bf16[128,512]{1,0:T(8,128)(2,1)S(1)}, bf16[128,512]{1,0:T(8,128)(2,1)S(1)}, u32[]{:S(2)}, u32[]{:S(2)}) %collective-permute-start.14) | collective-permute-done | bytes 131104 | tf_op jit(solution)/shard_map/ppermute | solution.py:305
  54.8 0.8 %partial_gradient.3 = (f32[1,128]{1,0:T(1,128)S(1)}, f32[128,512]{1,0:T(8,128)S(1)}, f32[128,512]{1,0:T(8,128)S(1)}, bf16[136,512]{1,0:T(8,128)(2,1)S(1)}, bf16[128,512]{1,0:T(8,128)(2,1)S(1)}) custom-call(bf16[256,2048]{1,0:T(8,128)(2,1)S(1)} %get-tuple-element.48.refs_0_, bf16[256,2048]{1,0:T(8,128)(2,1)S(1)} %collective-permute-done.6.refs_1_, ...), custom_call_target="tpu_custom_call" | custom-call | tf_op jit(solution)/shard_map/partial_gradient/pallas_call | solution.py:233
  55.6 0.6 collective-permute-done.16.near_ref
  56.2 1.0 %collective-permute-start.17 = (bf16[136,512]{1,0:T(8,128)(2,1)S(1)}, bf16[136,512]{1,0:T(8,128)(2,1)S(1)}, u32[]{:S(2)}, u32[]{:S(2)}) collective-permute-start(bf16[136,512]{1,0:T(8,128)(2,1)S(1)} %get-tuple-element.71), channel_id=1, source_target_pairs={{0,4},{2,6},{4,0},{6,2},{8,12},{10,14},{12,8},{14,10},{1,5},{3,7},... | collective-permute-start | bytes 417800 | tf_op jit(solution)/shard_map/ppermute | solution.py:305
  57.2 0.5 join_far.3
  57.8 2.4 %collective-permute-start.19 = (bf16[136,512]{1,0:T(8,128)(2,1)S(1)}, bf16[136,512]{1,0:T(8,128)(2,1)S(1)}, u32[]{:S(2)}, u32[]{:S(2)}) collective-permute-start(bf16[136,512]{1,0:T(8,128)(2,1)S(1)} %get-tuple-element.78), channel_id=1, source_target_pairs={{0,8},{2,10},{4,12},{6,14},{8,0},{10,2},{12,4},{14,6},{1,9},{3,11}... | collective-permute-start | bytes 417800 | tf_op jit(solution)/shard_map/ppermute | solution.py:305
  60.2 1.4 %collective-permute-done.17.got_ref = bf16[136,512]{1,0:T(8,128)(2,1)S(1)} collective-permute-done((bf16[136,512]{1,0:T(8,128)(2,1)S(1)}, bf16[136,512]{1,0:T(8,128)(2,1)S(1)}, u32[]{:S(2)}, u32[]{:S(2)}) %collective-permute-start.17) | collective-permute-done | bytes 139296 | tf_op jit(solution)/shard_map/ppermute | solution.py:305
  61.6 3.6 %collective-permute-start.18 = (bf16[136,512]{1,0:T(8,128)(2,1)S(1)}, bf16[136,512]{1,0:T(8,128)(2,1)S(1)}, u32[]{:S(2)}, u32[]{:S(2)}) collective-permute-start(bf16[136,512]{1,0:T(8,128)(2,1)S(1)} %get-tuple-element.73), channel_id=1, source_target_pairs={{0,8},{2,10},{4,12},{6,14},{8,0},{10,2},{12,4},{14,6},{1,9},{3,11}... | collective-permute-start | bytes 417800 | tf_op jit(solution)/shard_map/ppermute | solution.py:305
  65.1 2.1 %collective-permute-start.15 = (bf16[128,512]{1,0:T(8,128)(2,1)S(1)}, bf16[128,512]{1,0:T(8,128)(2,1)S(1)}, u32[]{:S(2)}, u32[]{:S(2)}) collective-permute-start(bf16[128,512]{1,0:T(8,128)(2,1)S(1)} %get-tuple-element.66), channel_id=1, source_target_pairs={{0,4},{2,6},{4,0},{6,2},{8,12},{10,14},{12,8},{14,10},{1,5},{3,7},... | collective-permute-start | bytes 393224 | tf_op jit(solution)/shard_map/ppermute | solution.py:305
  67.3 0.2 collective-permute-done.19.far_ref
  67.5 0.0 copy-done.2
  67.5 0.0 copy-done.3
  67.5 1.1 %apply_update.2 = (f32[512,256]{1,0:T(8,128)}, f32[512,256]{1,0:T(8,128)}, f32[512,256]{1,0:T(8,128)}) custom-call(f32[128,512]{1,0:T(8,128)S(1)} %get-tuple-element.74.own_ref, bf16[128,512]{1,0:T(8,128)(2,1)S(1)} %collective-permute-done.16.near_ref, bf16[136,512]{1,0:T(8,128)(2,1)S(1)} %collective-permute-done.19.far_ref, f32[512,256]{1,0:T(8,128)S(1)} %copy-done, ...), custom_call_target="tpu_custom_call" | custom-call | tf_op jit(solution)/shard_map/apply_update/pallas_call | solution.py:289
  68.7 1.9 %collective-permute-done.18.far_ref.got_ref = bf16[136,512]{1,0:T(8,128)(2,1)S(1)} collective-permute-done((bf16[136,512]{1,0:T(8,128)(2,1)S(1)}, bf16[136,512]{1,0:T(8,128)(2,1)S(1)}, u32[]{:S(2)}, u32[]{:S(2)}) %collective-permute-start.18) | collective-permute-done | bytes 139296 | tf_op jit(solution)/shard_map/ppermute | solution.py:305
  70.6 0.0 collective-permute-start.20
  70.6 0.3 collective-permute-done.15.near_ref
  70.9 1.2 %apply_update.3 = (f32[512,256]{1,0:T(8,128)}, f32[512,256]{1,0:T(8,128)}, f32[512,256]{1,0:T(8,128)}) custom-call(f32[128,512]{1,0:T(8,128)S(1)} %get-tuple-element.65.own_ref, bf16[128,512]{1,0:T(8,128)(2,1)S(1)} %collective-permute-done.15.near_ref, ...), custom_call_target="tpu_custom_call", output_to_operand_aliasing={{0}: (6, {}), {1}: (7, {}), {2}: (8, {})} | custom-call | tf_op jit(solution)/shard_map/apply_update/pallas_call | solution.py:289
  72.0 0.0 collective-permute-done.20
  72.0 0.6 add_reduce_fusion
  (10 shorter events, 0.2 us)
Async XLA Ops:
  0.6 15.8 %copy-start = (f32[512,256]{1,0:T(8,128)S(1)}, f32[512,256]{1,0:T(8,128)}, u32[]{:S(2)}) copy-start(f32[512,256]{1,0:T(8,128)} %w_ref.3) | copy-start | bytes 1572868
  1.8 4.8 %collective-permute-start = (f32[1,256]{1,0:T(1,128)S(1)}, f32[1,256]{1,0:T(1,128)S(1)}, u32[]{:S(2)}, u32[]{:S(2)}) collective-permute-start(f32[1,256]{1,0:T(1,128)S(1)} %bitcast.3), channel_id=1, source_target_pairs={{0,2},{2,0},{4,6},{6,4},{8,10},{10,8},{12,14},{14,12},{1,3},{3,1},... | collective-permute-start | bytes 3080 | tf_op jit(solution)/shard_map/ppermute | solution.py:305
  4.8 1.6 %copy-start.1 = (bf16[256,4096]{1,0:T(8,128)(2,1)S(1)}, bf16[256,4096]{1,0:T(8,128)(2,1)}, u32[]{:S(2)}) copy-start(bf16[256,4096]{1,0:T(8,128)(2,1)} %h_ref.1) | copy-start | bytes 6291460
  6.4 10.0 %copy-start.4 = (bf16[512,256]{1,0:T(8,128)(2,1)S(1)}, bf16[512,256]{1,0:T(8,128)(2,1)}, u32[]{:S(2)}) copy-start(bf16[512,256]{1,0:T(8,128)(2,1)} %param.6) | copy-start | bytes 786436
  6.6 23.6 %collective-permute-start.6 = (bf16[256,2048]{1,0:T(8,128)(2,1)S(1)}, bf16[256,2048]{1,0:T(8,128)(2,1)S(1)}, u32[]{:S(2)}, u32[]{:S(2)}) collective-permute-start(bf16[256,2048]{1,0:T(8,128)(2,1)S(1)} %get-tuple-element.48.refs_0_), channel_id=1, source_target_pairs={{0,1},{1,0},{2,3},{3,2},{4,5},{5,4},{6,7},{7,6},{8,9},{9,8},{10,11... | collective-permute-start | bytes 3145736 | tf_op jit(solution)/shard_map/ppermute | solution.py:308
  6.6 23.5 %collective-permute-start.5 = (bf16[256,1536]{1,0:T(8,128)(2,1)S(1)}, bf16[256,1536]{1,0:T(8,128)(2,1)S(1)}, u32[]{:S(2)}, u32[]{:S(2)}) collective-permute-start(bf16[256,1536]{1,0:T(8,128)(2,1)S(1)} %get-tuple-element.50), channel_id=1, source_target_pairs={{0,2},{2,0},{4,6},{6,4},{8,10},{10,8},{12,14},{14,12},{1,3},{3,1},... | collective-permute-start | bytes 2359304 | tf_op jit(solution)/shard_map/ppermute | solution.py:305
  8.4 3.6 %collective-permute-start.1 = (f32[1,256]{1,0:T(1,128)S(1)}, f32[1,256]{1,0:T(1,128)S(1)}, u32[]{:S(2)}, u32[]{:S(2)}) collective-permute-start(f32[1,256]{1,0:T(1,128)S(1)} %max.9), channel_id=1, source_target_pairs={{0,4},{2,6},{4,0},{6,2},{8,12},{10,14},{12,8},{14,10},{1,5},{3,7},... | collective-permute-start | bytes 3080 | tf_op jit(solution)/shard_map/ppermute | solution.py:305
  11.9 4.5 %collective-permute-start.2 = (f32[1,256]{1,0:T(1,128)S(1)}, f32[1,256]{1,0:T(1,128)S(1)}, u32[]{:S(2)}, u32[]{:S(2)}) collective-permute-start(f32[1,256]{1,0:T(1,128)S(1)} %max.10), channel_id=1, source_target_pairs={{0,8},{2,10},{4,12},{6,14},{8,0},{10,2},{12,4},{14,6},{1,9},{3,11}... | collective-permute-start | bytes 3080 | tf_op jit(solution)/shard_map/ppermute | solution.py:305
  16.9 13.1 %collective-permute-start.3 = (f16[512,256]{1,0:T(8,128)(2,1)S(1)}, f16[512,256]{1,0:T(8,128)(2,1)S(1)}, u32[]{:S(2)}, u32[]{:S(2)}) collective-permute-start(f16[512,256]{1,0:T(8,128)(2,1)S(1)} %get-tuple-element.90), channel_id=1, source_target_pairs={{0,8},{2,10},{4,12},{6,14},{8,0},{10,2},{12,4},{14,6},{1,9},{3,11}... | collective-permute-start | bytes 786440 | tf_op jit(solution)/shard_map/ppermute | solution.py:305
  19.5 10.7 %collective-permute-start.4 = (f16[512,256]{1,0:T(8,128)(2,1)S(1)}, f16[512,256]{1,0:T(8,128)(2,1)S(1)}, u32[]{:S(2)}, u32[]{:S(2)}) collective-permute-start(f16[512,256]{1,0:T(8,128)(2,1)S(1)} %get-tuple-element.90), channel_id=1, source_target_pairs={{0,4},{2,6},{4,0},{6,2},{8,12},{10,14},{12,8},{14,10},{1,5},{3,7},... | collective-permute-start | bytes 786440 | tf_op jit(solution)/shard_map/ppermute | solution.py:305
  21.1 11.1 %collective-permute-start.7 = (bf16[256,512]{1,0:T(8,128)(2,1)S(1)}, bf16[256,512]{1,0:T(8,128)(2,1)S(1)}, u32[]{:S(2)}, u32[]{:S(2)}) collective-permute-start(bf16[256,512]{1,0:T(8,128)(2,1)S(1)} %get-tuple-element.53), channel_id=1, source_target_pairs={{0,2},{2,0},{4,6},{6,4},{8,10},{10,8},{12,14},{14,12},{1,3},{3,1},... | collective-permute-start | bytes 786440 | tf_op jit(solution)/shard_map/ppermute | solution.py:305
  30.2 7.8 %collective-permute-start.9 = (bf16[256,1536]{1,0:T(8,128)(2,1)S(1)}, bf16[256,1536]{1,0:T(8,128)(2,1)S(1)}, u32[]{:S(2)}, u32[]{:S(2)}) collective-permute-start(bf16[256,1536]{1,0:T(8,128)(2,1)S(1)} %collective-permute-done.5.refs_2_), channel_id=1, source_target_pairs={{0,1},{1,0},{2,3},{3,2},{4,5},{5,4},{6,7},{7,6},{8,9},{9,8},{10,11... | collective-permute-start | bytes 2359304 | tf_op jit(solution)/shard_map/ppermute | solution.py:308
  30.3 6.0 %collective-permute-start.8 = (f16[512,128]{1,0:T(8,128)(2,1)S(1)}, f16[512,128]{1,0:T(8,128)(2,1)S(1)}, u32[]{:S(2)}, u32[]{:S(2)}) collective-permute-start(f16[512,128]{1,0:T(8,128)(2,1)S(1)} %get-tuple-element.105), channel_id=1, source_target_pairs={{0,4},{2,6},{4,0},{6,2},{8,12},{10,14},{12,8},{14,10},{1,5},{3,7},... | collective-permute-start | bytes 393224 | tf_op jit(solution)/shard_map/ppermute | solution.py:305
  36.2 1.7 %collective-permute-start.10 = (bf16[256,512]{1,0:T(8,128)(2,1)S(1)}, bf16[256,512]{1,0:T(8,128)(2,1)S(1)}, u32[]{:S(2)}, u32[]{:S(2)}) collective-permute-start(bf16[256,512]{1,0:T(8,128)(2,1)S(1)} %collective-permute-done.7.refs_3_), channel_id=1, source_target_pairs={{0,1},{1,0},{2,3},{3,2},{4,5},{5,4},{6,7},{7,6},{8,9},{9,8},{10,11... | collective-permute-start | bytes 786440 | tf_op jit(solution)/shard_map/ppermute | solution.py:308
  36.4 6.0 %collective-permute-start.11 = (f16[512,128]{1,0:T(8,128)(2,1)S(1)}, f16[512,128]{1,0:T(8,128)(2,1)S(1)}, u32[]{:S(2)}, u32[]{:S(2)}) collective-permute-start(f16[512,128]{1,0:T(8,128)(2,1)S(1)} %get-tuple-element.104), channel_id=1, source_target_pairs={{0,4},{2,6},{4,0},{6,2},{8,12},{10,14},{12,8},{14,10},{1,5},{3,7},... | collective-permute-start | bytes 393224 | tf_op jit(solution)/shard_map/ppermute | solution.py:305
  39.2 9.2 %collective-permute-start.13 = (bf16[1024,128]{1,0:T(8,128)(2,1)S(1)}, bf16[1024,128]{1,0:T(8,128)(2,1)S(1)}, u32[]{:S(2)}, u32[]{:S(2)}) collective-permute-start(bf16[1024,128]{1,0:T(8,128)(2,1)S(1)} %get-tuple-element.61), channel_id=1, source_target_pairs={{0,2},{2,0},{4,6},{6,4},{8,10},{10,8},{12,14},{14,12},{1,3},{3,1},... | collective-permute-start | bytes 786440 | tf_op jit(solution)/shard_map/ppermute | solution.py:305
  43.7 9.7 %collective-permute-start.12 = (bf16[1024,128]{1,0:T(8,128)(2,1)S(1)}, bf16[1024,128]{1,0:T(8,128)(2,1)S(1)}, u32[]{:S(2)}, u32[]{:S(2)}) collective-permute-start(bf16[1024,128]{1,0:T(8,128)(2,1)S(1)} %get-tuple-element.58), channel_id=1, source_target_pairs={{0,2},{2,0},{4,6},{6,4},{8,10},{10,8},{12,14},{14,12},{1,3},{3,1},... | collective-permute-start | bytes 786440 | tf_op jit(solution)/shard_map/ppermute | solution.py:305
  49.2 5.6 %collective-permute-start.14 = (bf16[128,512]{1,0:T(8,128)(2,1)S(1)}, bf16[128,512]{1,0:T(8,128)(2,1)S(1)}, u32[]{:S(2)}, u32[]{:S(2)}) collective-permute-start(bf16[128,512]{1,0:T(8,128)(2,1)S(1)} %get-tuple-element.62), channel_id=1, source_target_pairs={{0,4},{2,6},{4,0},{6,2},{8,12},{10,14},{12,8},{14,10},{1,5},{3,7},... | collective-permute-start | bytes 393224 | tf_op jit(solution)/shard_map/ppermute | solution.py:305
  50.5 5.7 %collective-permute-start.16 = (bf16[128,512]{1,0:T(8,128)(2,1)S(1)}, bf16[128,512]{1,0:T(8,128)(2,1)S(1)}, u32[]{:S(2)}, u32[]{:S(2)}) collective-permute-start(bf16[128,512]{1,0:T(8,128)(2,1)S(1)} %get-tuple-element.69), channel_id=1, source_target_pairs={{0,4},{2,6},{4,0},{6,2},{8,12},{10,14},{12,8},{14,10},{1,5},{3,7},... | collective-permute-start | bytes 393224 | tf_op jit(solution)/shard_map/ppermute | solution.py:305
  54.8 12.7 %copy-start.2 = (f32[512,256]{1,0:T(8,128)S(1)}, f32[512,256]{1,0:T(8,128)}, u32[]{:S(2)}) copy-start(f32[512,256]{1,0:T(8,128)} %m_ref.3) | copy-start | bytes 1572868
  54.8 12.7 %copy-start.3 = (f32[512,256]{1,0:T(8,128)S(1)}, f32[512,256]{1,0:T(8,128)}, u32[]{:S(2)}) copy-start(f32[512,256]{1,0:T(8,128)} %v_ref.3) | copy-start | bytes 1572868
  56.2 5.3 %collective-permute-start.17 = (bf16[136,512]{1,0:T(8,128)(2,1)S(1)}, bf16[136,512]{1,0:T(8,128)(2,1)S(1)}, u32[]{:S(2)}, u32[]{:S(2)}) collective-permute-start(bf16[136,512]{1,0:T(8,128)(2,1)S(1)} %get-tuple-element.71), channel_id=1, source_target_pairs={{0,4},{2,6},{4,0},{6,2},{8,12},{10,14},{12,8},{14,10},{1,5},{3,7},... | collective-permute-start | bytes 417800 | tf_op jit(solution)/shard_map/ppermute | solution.py:305
  57.8 9.7 %collective-permute-start.19 = (bf16[136,512]{1,0:T(8,128)(2,1)S(1)}, bf16[136,512]{1,0:T(8,128)(2,1)S(1)}, u32[]{:S(2)}, u32[]{:S(2)}) collective-permute-start(bf16[136,512]{1,0:T(8,128)(2,1)S(1)} %get-tuple-element.78), channel_id=1, source_target_pairs={{0,8},{2,10},{4,12},{6,14},{8,0},{10,2},{12,4},{14,6},{1,9},{3,11}... | collective-permute-start | bytes 417800 | tf_op jit(solution)/shard_map/ppermute | solution.py:305
  61.6 9.0 %collective-permute-start.18 = (bf16[136,512]{1,0:T(8,128)(2,1)S(1)}, bf16[136,512]{1,0:T(8,128)(2,1)S(1)}, u32[]{:S(2)}, u32[]{:S(2)}) collective-permute-start(bf16[136,512]{1,0:T(8,128)(2,1)S(1)} %get-tuple-element.73), channel_id=1, source_target_pairs={{0,8},{2,10},{4,12},{6,14},{8,0},{10,2},{12,4},{14,6},{1,9},{3,11}... | collective-permute-start | bytes 417800 | tf_op jit(solution)/shard_map/ppermute | solution.py:305
  65.1 5.7 %collective-permute-start.15 = (bf16[128,512]{1,0:T(8,128)(2,1)S(1)}, bf16[128,512]{1,0:T(8,128)(2,1)S(1)}, u32[]{:S(2)}, u32[]{:S(2)}) collective-permute-start(bf16[128,512]{1,0:T(8,128)(2,1)S(1)} %get-tuple-element.66), channel_id=1, source_target_pairs={{0,4},{2,6},{4,0},{6,2},{8,12},{10,14},{12,8},{14,10},{1,5},{3,7},... | collective-permute-start | bytes 393224 | tf_op jit(solution)/shard_map/ppermute | solution.py:305
  70.6 1.4 %collective-permute-start.20 = (f32[1,128]{1,0:T(1,128)S(1)}, f32[1,128]{1,0:T(1,128)S(1)}, u32[]{:S(2)}, u32[]{:S(2)}) collective-permute-start(f32[1,128]{1,0:T(1,128)S(1)} %total_loss.1), channel_id=1, source_target_pairs={{0,1},{1,0},{2,3},{3,2},{4,5},{5,4},{6,7},{7,6},{8,9},{9,8},{10,11... | collective-permute-start | bytes 1544 | tf_op jit(solution)/shard_map/ppermute | solution.py:308
